TPU v7x, 128 devices: a whole 4x4x4 slice. The times are simulated.
128 devices in a mesh: row: 16 (over x, y_lo, core), col: 8 (over y_hi, z).
Axes of the slice: x: 4, y: 4 (y_hi: 2, y_lo: 2; y = y_hi * 2 + y_lo), z: 4, core: 2. Of those that a mesh axis runs over, the one named last changes fastest.
Arguments:
- radar_tiles: bfloat16 [1024, 512, 256], P('row', 'col'), may hold values from -6 to 6
- conv_scale: float32 [256], replicated, may hold values from 0.5 to 1.5
- conv_shift: float32 [256], replicated, may hold values from -3 to 3
- expand_weight: bfloat16 [256, 1024], replicated, may hold values from -0.375 to 0.375
- expand_bias: float32 [1024], replicated, may hold values from -3 to 3
- depth_kernel: float32 [3, 3, 1024], replicated, may hold values from -2 to 2
- depth_bias: float32 [1024], replicated, may hold values from -3 to 3
- project_weight: bfloat16 [1024, 256], replicated, may hold values from -0.1875 to 0.1875
- block_gains: float32 [2, 256], replicated, may hold values from 0.5 to 1.5
- block_entry: bfloat16 [256, 768], replicated, may hold values from -0.375 to 0.375
- block_leave: bfloat16 [256, 256], replicated, may hold values from -0.375 to 0.375
- block_offsets: float32 [8, 64, 64], replicated, may hold values from -6 to 6
- block_widen: bfloat16 [256, 1024], replicated, may hold values from -0.375 to 0.375
- block_shrink: bfloat16 [1024, 256], replicated, may hold values from -0.1875 to 0.1875
- grid_gains: float32 [2, 256], replicated, may hold values from 0.5 to 1.5
- grid_entry: bfloat16 [256, 768], replicated, may hold values from -0.375 to 0.375
- grid_leave: bfloat16 [256, 256], replicated, may hold values from -0.375 to 0.375
- grid_offsets: float32 [8, 64, 64], replicated, may hold values from -6 to 6
- grid_widen: bfloat16 [256, 1024], replicated, may hold values from -0.375 to 0.375
- grid_shrink: bfloat16 [1024, 256], replicated, may hold values from -0.1875 to 0.1875
Outputs:
- refined: bfloat16 [1024, 512, 256], P('row', 'col')
All inputs are finite; a program needn't handle non-finite values.
Results may differ from a plain program's by a relative error of at most 0.015.
Values may be sent and summed in bfloat16 or wider, within the bound.
No kernel may reach another device: no remote copies, remote signals or barrier semaphores. Data moves between devices by JAX's collectives and lax.ppermute only.
A program may use at most 128 MiB of HBM per device.

v0:
```python
import math

import jax
import jax.numpy as jnp
from jax import lax
from jax.sharding import PartitionSpec as P

WIN = 8


epsilon = 1e-05


def with_halo(block, sides, width):
    for axis, dim in sides:
        count = lax.axis_size(axis)
        forward = [(i, i + 1) for i in range(count - 1)]
        backward = [(target, source) for source, target in forward]
        low = lax.ppermute(
            lax.slice_in_dim(block, block.shape[dim] - width, None, axis=dim), axis, forward
        )
        high = lax.ppermute(lax.slice_in_dim(block, 0, width, axis=dim), axis, backward)
        block = jnp.concatenate([low, block, high], axis=dim)
    return block


def layer_norm(values, gain_row):
    center = values - jnp.mean(values, axis=-1, keepdims=True)
    spread = jnp.mean(center * center, axis=-1, keepdims=True)
    return center * lax.rsqrt(spread + epsilon) * gain_row


def attend(
    windows, norm_gains, entry_weight, leave_weight, offset_table, widen_weight, shrink_weight
):
    win_count, positions, channels = windows.shape
    head_count = offset_table.shape[0]
    head_size = channels // head_count
    flattened = windows.reshape(-1, channels)
    lifted = layer_norm(flattened.astype(jnp.float32), norm_gains[0]).astype(jnp.bfloat16)
    projected = jnp.dot(lifted, entry_weight, preferred_element_type=jnp.float32).astype(
        jnp.bfloat16
    )
    projected = projected.reshape(win_count, positions, 3, head_count, head_size)
    query_rows = projected[:, :, 0]
    key_rows = projected[:, :, 1]
    value_rows = projected[:, :, 2]
    score_scale = 1.0 / math.sqrt(head_size)
    scores = (
        jnp.einsum("nqhd,nkhd->nhqk", query_rows, key_rows, preferred_element_type=jnp.float32)
        * score_scale
        + offset_table
    )
    weights = jnp.exp(scores)
    weights = (weights / jnp.sum(weights, axis=-1, keepdims=True)).astype(jnp.bfloat16)
    mixture = jnp.einsum("nhqk,nkhd->nqhd", weights, value_rows, preferred_element_type=jnp.float32)
    mixture = mixture.astype(jnp.bfloat16).reshape(-1, channels)
    attended = (
        flattened.astype(jnp.float32)
        + jnp.dot(mixture, leave_weight, preferred_element_type=jnp.float32)
    ).astype(jnp.bfloat16)
    second = layer_norm(attended.astype(jnp.float32), norm_gains[1]).astype(jnp.bfloat16)
    hidden = jax.nn.gelu(jnp.dot(second, widen_weight, preferred_element_type=jnp.float32)).astype(
        jnp.bfloat16
    )
    result = attended.astype(jnp.float32) + jnp.dot(
        hidden, shrink_weight, preferred_element_type=jnp.float32
    )
    return result.astype(jnp.bfloat16).reshape(win_count, positions, channels)


def expand_cells(cells, expand_weight, expand_bias):
    first_dim, second_dim, channels = cells.shape
    product = jnp.dot(
        cells.reshape(-1, channels), expand_weight, preferred_element_type=jnp.float32
    )
    return (
        jax.nn.gelu(product + expand_bias).astype(jnp.bfloat16).reshape(first_dim, second_dim, -1)
    )


def shards(
    radar_tiles,
    conv_scale,
    conv_shift,
    expand_weight,
    expand_bias,
    depth_kernel,
    depth_bias,
    project_weight,
    block_gains,
    block_entry,
    block_leave,
    block_offsets,
    block_widen,
    block_shrink,
    grid_gains,
    grid_entry,
    grid_leave,
    grid_offsets,
    grid_widen,
    grid_shrink,
):
    rows_here, cols_here, channels = radar_tiles.shape
    inner_width = expand_weight.shape[1]
    source = radar_tiles.astype(jnp.float32)
    normed = (source * conv_scale + conv_shift).astype(jnp.bfloat16)
    inner_cells = expand_cells(normed, expand_weight, expand_bias)
    padded = with_halo(inner_cells, (("row", 0), ("col", 1)), 1)
    summed = jnp.zeros((rows_here, cols_here, inner_width), jnp.float32)
    for shift_row in range(3):
        for shift_col in range(3):
            summed = (
                summed
                + padded[
                    shift_row : shift_row + rows_here, shift_col : shift_col + cols_here
                ].astype(jnp.float32)
                * depth_kernel[shift_row, shift_col]
            )
    activated = jax.nn.gelu(summed + depth_bias).astype(jnp.bfloat16)
    product = jnp.dot(
        activated.reshape(-1, inner_width), project_weight, preferred_element_type=jnp.float32
    )
    section_one = (source + product.reshape(rows_here, cols_here, channels)).astype(jnp.bfloat16)
    blocks = section_one.reshape(rows_here // WIN, WIN, cols_here // WIN, WIN, channels).transpose(
        0, 2, 1, 3, 4
    )
    blocks = blocks.reshape(-1, WIN * WIN, channels)
    attended_tiles = attend(
        blocks, block_gains, block_entry, block_leave, block_offsets, block_widen, block_shrink
    )
    section_two = attended_tiles.reshape(
        rows_here // WIN, cols_here // WIN, WIN, WIN, channels
    ).transpose(0, 2, 1, 3, 4)
    section_two = section_two.reshape(rows_here, cols_here, channels)
    row_count = lax.axis_size("row")
    col_count = lax.axis_size("col")
    held_rows = max(1, WIN // row_count)
    held_cols = max(1, WIN // col_count)
    row_phases = max(1, row_count // WIN)
    col_phases = max(1, col_count // WIN)
    row_cells = rows_here // held_rows
    col_cells = cols_here // held_cols
    devices = row_count * col_count
    per_piece = row_cells * col_cells // devices
    outgoing = section_two.reshape(held_rows, row_cells, held_cols, col_cells, channels).transpose(
        1, 3, 0, 2, 4
    )
    outgoing = outgoing.reshape(devices, per_piece, held_rows, held_cols, channels)
    arrived = lax.all_to_all(outgoing, ("row", "col"), split_axis=0, concat_axis=0, tiled=True)
    slot_count = arrived.shape[1]
    regroup_slot_count = arrived.shape[1]
    grouped = arrived.reshape(
        row_count // row_phases,
        row_phases,
        col_count // col_phases,
        col_phases,
        regroup_slot_count,
        held_rows,
        held_cols,
        channels,
    )
    grouped = grouped.transpose(1, 3, 4, 0, 5, 2, 6, 7).reshape(-1, WIN * WIN, channels)
    finished = attend(
        grouped, grid_gains, grid_entry, grid_leave, grid_offsets, grid_widen, grid_shrink
    )
    finished = finished.reshape(
        row_phases,
        col_phases,
        regroup_slot_count,
        row_count // row_phases,
        held_rows,
        col_count // col_phases,
        held_cols,
        channels,
    )
    returning = finished.transpose(3, 0, 5, 1, 2, 4, 6, 7).reshape(
        devices, slot_count, held_rows, held_cols, channels
    )
    returned = lax.all_to_all(returning, ("row", "col"), split_axis=0, concat_axis=0, tiled=True)
    finished_tiles = returned.reshape(
        row_cells, col_cells, held_rows, held_cols, channels
    ).transpose(2, 0, 3, 1, 4)
    return finished_tiles.reshape(rows_here, cols_here, channels)


def solution(mesh):
    return jax.shard_map(
        shards,
        mesh=mesh,
        in_specs=(
            P("row", "col", None),
            P(),
            P(),
            P(),
            P(),
            P(),
            P(),
            P(),
            P(),
            P(),
            P(),
            P(),
            P(),
            P(),
            P(),
            P(),
            P(),
            P(),
            P(),
            P(),
        ),
        out_specs=P("row", "col", None),
        check_vma=False,
    )
```

profile of v0, /device:TPU:0, one launch (start us, length us, event | category | flops | bytes accessed | tf_op | source)
XLA Modules:
  0.0 410.8 jit_solution(6498971673184961252)
XLA Ops:
  2.3 7.1 %fusion.7 = bf16[4096,1024]{1,0:T(8,128)(2,1)S(1)} fusion(bf16[4096,256]{1,0:T(8,128)(2,1)S(1)} %bitcast.153, bf16[256,1024]{1,0:T(8,128)(2,1)S(1)} %copy-done, f32[1024]{0:T(1024)} %param.24), kind=kOutput, calls=%fused_computation.11 | convolution fusion | flops 2189426688 | bytes 11014144 | tf_op jit(solution)/shard_map/dot_general | solution.py:74
  15.5 3.6 collective-permute-done.1
  21.1 3.8 collective-permute-start.2
  29.1 4.5 %collective-permute-done.3 = bf16[66,1,1024]{2,1,0:T(2,128)(2,1)S(1)} collective-permute-done((bf16[66,1,1024]{2,1,0:T(2,128)(2,1)S(1)}, bf16[66,1,1024]{2,1,0:T(2,128)(2,1)S(1)}, u32[]{:S(2)}, u32[]{:S(2)}) %collective-permute-start.3) | collective-permute-done | bytes 135200 | tf_op jit(solution)/shard_map/ppermute | solution.py:22
  33.7 13.8 %maximum_maximum_fusion = (bf16[66,65,1024]{2,1,0:T(8,128)(2,1)}, bf16[66,65,1024]{2,1,0:T(8,128)(2,1)}) fusion(bf16[1,64,1024]{2,1,0:T(8,128)(2,1)S(1)} %collective-permute-done.1, bf16[64,64,1024]{2,1,0:T(8,128)(2,1)S(1)} %bitcast.140, bf16[1,64,1024]{2,1,0:T(8,128)(2,1)S(1)} %collective-permute-done, bf16[66,1,1024]{2,1,0:T(2,128)(2,1)S(1)} %collective-permute-done.2, ...), kind=kLoop, calls=%fused_computation.42 | loop fusion | flops 70287360 | bytes 26492928 | tf_op jit(solution)/shard_map/concatenate | solution.py:23
  47.4 32.6 %fusion.70 = bf16[64,64,256]{2,1,0:T(8,128)(2,1)} fusion(bf16[64,64,256]{2,1,0:T(8,128)(2,1)} %param.20, bf16[64,64,1024]{2,1,0:T(8,128)(2,1)S(1)} %bitcast.141, bf16[66,65,1024]{2,1,0:T(8,128)(2,1)} %get-tuple-element.12, bf16[1,64,1024]{2,1,0:T(8,128)(2,1)S(1)} %collective-permute-done.1, bf16[66,65,1024]{2,1,0:T(8,128)(2,1)} %get-tuple-element.11, ...), kind=kOutput, calls=%fused_computation.81 | convolution fusion | flops 2310012928 | bytes 63741952 | tf_op jit(solution)/shard_map/dot_general | solution.py:121
  82.5 4.1 %convert_bitcast_fusion.1 = f32[8,8,8,8,256]{4,3,1,2,0:T(8,128)} fusion(bf16[8,8,8,8,256]{4,3,2,1,0:T(8,128)(2,1)} %bitcast.146), kind=kLoop, calls=%fused_computation.95 | loop fusion | flops 1048576 | bytes 6291456 | tf_op jit(solution)/shard_map/convert_element_type | solution.py:59
  88.3 4.8 %copy.52 = f32[8,8,8,8,256]{4,3,2,1,0:T(8,128)} copy(f32[8,8,8,8,256]{4,3,1,2,0:T(8,128)} %convert_bitcast_fusion.1) | data formatting | bytes 8388608 | tf_op jit(solution)/shard_map/convert_element_type | solution.py:59
  96.1 4.5 %convolution_convert_fusion.1 = bf16[4096,768]{1,0:T(8,128)(2,1)} fusion(bf16[4096,256]{1,0:T(8,128)(2,1)S(1)} %fusion.78, bf16[256,768]{1,0:T(8,128)(2,1)S(1)} %copy-done.7), kind=kOutput, calls=%fused_computation.52 | convolution fusion | flops 1613758464 | bytes 8781824 | tf_op jit(solution)/shard_map/dot_general | solution.py:41
  100.5 8.7 %copy.55 = bf16[4096,768]{0,1:T(8,128)(2,1)} copy(bf16[4096,768]{1,0:T(8,128)(2,1)} %convolution_convert_fusion.1) | data formatting | bytes 12582912 | tf_op jit(solution)/shard_map/convert_element_type | solution.py:41
  109.3 17.9 %reshape.145 = bf16[64,64,3,8,32]{1,0,4,3,2:T(8,128)(2,1)} reshape(bf16[4096,768]{0,1:T(8,128)(2,1)} %copy.55) | data formatting | bytes 12582912 | tf_op jit(solution)/shard_map/reshape | solution.py:44
  127.1 8.5 %fusion.116 = (bf16[64,64,1,8,32]{1,0,4,3,2:T(8,128)(2,1)}, bf16[64,64,1,8,32]{1,0,4,3,2:T(8,128)(2,1)S(1)}, bf16[64,64,1,8,32]{1,0,4,3,2:T(8,128)(2,1)}) fusion(bf16[64,64,3,8,32]{1,0,4,3,2:T(8,128)(2,1)} %reshape.145), kind=kLoop, calls=%fused_computation.142 | loop fusion | bytes 12582912 | tf_op jit(solution)/shard_map/slice | solution.py:47
  135.6 20.3 %fusion.32 = (f32[64,8,64]{2,1,0:T(8,128)S(1)}, f32[64,8,64,64]{2,3,1,0:T(8,128)}) fusion(f32[8,64,64]{1,2,0:T(8,128)S(1)} %copy.59, bf16[64,64,1,8,32]{1,0,4,3,2:T(8,128)(2,1)} %get-tuple-element.10, bf16[64,64,1,8,32]{1,0,4,3,2:T(8,128)(2,1)S(1)} %get-tuple-element.9), kind=kOutput, calls=%fused_computation.40 | convolution fusion | flops 140476416 | bytes 12845056 | tf_op jit(solution)/shard_map/nqhd,nkhd->nhqk/dot_general | solution.py:50
  155.9 19.5 %convert_bitcast_fusion.3 = bf16[64,64,8,32]{1,3,2,0:T(8,128)(2,1)} fusion(f32[64,8,64,64]{2,3,1,0:T(8,128)} %get-tuple-element.31, f32[64,8,64]{2,1,0:T(8,128)S(1)} %get-tuple-element.30, f32[8,64,64]{1,2,0:T(8,128)S(1)} %copy.59, bf16[64,64,1,8,32]{1,0,4,3,2:T(8,128)(2,1)} %get-tuple-element.8), kind=kOutput, calls=%fused_computation.102 | convolution fusion | flops 143654912 | bytes 12845056 | tf_op jit(solution)/shard_map/nhqk,nkhd->nqhd/dot_general | solution.py:56
  175.4 7.1 %copy.61 = bf16[64,64,8,32]{1,0,3,2:T(8,128)(2,1)} copy(bf16[64,64,8,32]{1,3,2,0:T(8,128)(2,1)} %convert_bitcast_fusion.3) | data formatting | bytes 4194304 | tf_op jit(solution)/shard_map/convert_element_type | solution.py:57
  182.5 5.7 %reshape.146 = bf16[4096,256]{0,1:T(8,128)(2,1)S(1)} reshape(bf16[64,64,8,32]{1,0,3,2:T(8,128)(2,1)} %copy.61) | data formatting | bytes 4194304 | tf_op jit(solution)/shard_map/reshape | solution.py:57
  188.2 3.5 convert_reduce_fusion.1
  194.4 9.1 %fusion.48 = bf16[4096,256]{1,0:T(8,128)(2,1)S(1)} fusion(bf16[1024,256]{1,0:T(8,128)(2,1)S(1)} %copy-done.17, bf16[4096,256]{1,0:T(8,128)(2,1)} %copy-done.5, bf16[256,1024]{1,0:T(8,128)(2,1)} %param.32, f32[256]{0:T(256)S(1)} %bitcast.165, f32[4096]{0:T(1024)S(1)} %add_rsqrt_fusion.3, f32[4096]{0:T(1024)S(1)} %broadcast_multiply_fusion.3), kind=kOutput, calls=%fused_computation.65 | convolution fusion | flops 4341104640 | bytes 5276672 | tf_op jit(solution)/shard_map/dot_general | solution.py:66
  205.1 16.7 %all-to-all-start = ((bf16[128,32,1,1,256]{4,1,3,2,0:T(8,128)(2,1)}), bf16[128,32,1,1,256]{4,1,3,2,0:T(8,128)(2,1)S(1)}, u32[]{:S(2)}, u32[]{:S(2)}) async-start(bf16[128,32,1,1,256]{4,1,3,2,0:T(8,128)(2,1)} %bitcast.148), calls=%async_computation | async-start | bytes 4194304 | tf_op jit(solution)/shard_map/all_to_all | solution.py:150
  222.0 30.2 %all-to-all-done = bf16[128,32,1,1,256]{4,1,3,2,0:T(8,128)(2,1)S(1)} async-done(((bf16[128,32,1,1,256]{4,1,3,2,0:T(8,128)(2,1)}), bf16[128,32,1,1,256]{4,1,3,2,0:T(8,128)(2,1)S(1)}, u32[]{:S(2)}, u32[]{:S(2)}) %all-to-all-start) | async-done | bytes 2097184 | tf_op jit(solution)/shard_map/all_to_all | solution.py:150
  257.2 6.6 %copy.65 = f32[2,1,32,8,1,8,1,256]{7,5,3,2,0,6,4,1:T(8,128)} copy(f32[2,1,32,8,1,8,1,256]{7,2,5,0,3,6,4,1:T(8,128)} %convert_bitcast_fusion) | data formatting | bytes 8388608 | tf_op jit(solution)/shard_map/convert_element_type | solution.py:59
  266.7 4.5 %convolution_convert_fusion = bf16[4096,768]{1,0:T(8,128)(2,1)} fusion(bf16[4096,256]{1,0:T(8,128)(2,1)S(1)} %fusion.75, bf16[256,768]{1,0:T(8,128)(2,1)S(1)} %copy-done.8), kind=kOutput, calls=%fused_computation.51 | convolution fusion | flops 1613758464 | bytes 8781824 | tf_op jit(solution)/shard_map/dot_general | solution.py:41
  271.2 8.7 %copy.68 = bf16[4096,768]{0,1:T(8,128)(2,1)} copy(bf16[4096,768]{1,0:T(8,128)(2,1)} %convolution_convert_fusion) | data formatting | bytes 12582912 | tf_op jit(solution)/shard_map/convert_element_type | solution.py:41
  279.9 17.9 %reshape.147 = bf16[64,64,3,8,32]{1,0,4,3,2:T(8,128)(2,1)} reshape(bf16[4096,768]{0,1:T(8,128)(2,1)} %copy.68) | data formatting | bytes 12582912 | tf_op jit(solution)/shard_map/reshape | solution.py:44
  297.8 8.3 %fusion.115 = (bf16[64,64,1,8,32]{1,0,4,3,2:T(8,128)(2,1)}, bf16[64,64,1,8,32]{1,0,4,3,2:T(8,128)(2,1)S(1)}, bf16[64,64,1,8,32]{1,0,4,3,2:T(8,128)(2,1)}) fusion(bf16[64,64,3,8,32]{1,0,4,3,2:T(8,128)(2,1)} %reshape.147), kind=kLoop, calls=%fused_computation.141 | loop fusion | bytes 12582912 | tf_op jit(solution)/shard_map/slice | solution.py:47
  306.1 20.2 %fusion.33 = (f32[64,8,64]{2,1,0:T(8,128)S(1)}, f32[64,8,64,64]{2,3,1,0:T(8,128)}) fusion(f32[8,64,64]{1,2,0:T(8,128)S(1)} %copy.72, bf16[64,64,1,8,32]{1,0,4,3,2:T(8,128)(2,1)} %get-tuple-element.7, bf16[64,64,1,8,32]{1,0,4,3,2:T(8,128)(2,1)S(1)} %get-tuple-element.6), kind=kOutput, calls=%fused_computation.41 | convolution fusion | flops 140476416 | bytes 12845056 | tf_op jit(solution)/shard_map/nqhd,nkhd->nhqk/dot_general | solution.py:50
  326.3 18.8 %convert_bitcast_fusion.2 = bf16[64,64,8,32]{1,3,2,0:T(8,128)(2,1)} fusion(f32[64,8,64,64]{2,3,1,0:T(8,128)} %get-tuple-element.35, f32[64,8,64]{2,1,0:T(8,128)S(1)} %get-tuple-element.34, f32[8,64,64]{1,2,0:T(8,128)S(1)} %copy.72, bf16[64,64,1,8,32]{1,0,4,3,2:T(8,128)(2,1)} %get-tuple-element.5), kind=kOutput, calls=%fused_computation.100 | convolution fusion | flops 143654912 | bytes 12845056 | tf_op jit(solution)/shard_map/nhqk,nkhd->nqhd/dot_general | solution.py:56
  345.2 7.1 %copy.74 = bf16[64,64,8,32]{1,0,3,2:T(8,128)(2,1)} copy(bf16[64,64,8,32]{1,3,2,0:T(8,128)(2,1)} %convert_bitcast_fusion.2) | data formatting | bytes 4194304 | tf_op jit(solution)/shard_map/convert_element_type | solution.py:57
  352.3 5.7 %reshape.148 = bf16[4096,256]{0,1:T(8,128)(2,1)S(1)} reshape(bf16[64,64,8,32]{1,0,3,2:T(8,128)(2,1)} %copy.74) | data formatting | bytes 4194304 | tf_op jit(solution)/shard_map/reshape | solution.py:57
  358.0 3.5 convert_reduce_fusion
  364.2 9.1 %fusion.51 = bf16[4096,256]{1,0:T(8,128)(2,1)S(1)} fusion(bf16[1024,256]{1,0:T(8,128)(2,1)S(1)} %copy-done.18, bf16[4096,256]{1,0:T(8,128)(2,1)} %copy-done.6, bf16[256,1024]{1,0:T(8,128)(2,1)} %param.38, f32[256]{0:T(256)S(1)} %bitcast.166, f32[4096]{0:T(1024)S(1)} %add_rsqrt_fusion.2, f32[4096]{0:T(1024)S(1)} %broadcast_multiply_fusion.2), kind=kOutput, calls=%fused_computation.66 | convolution fusion | flops 4341104640 | bytes 5276672 | tf_op jit(solution)/shard_map/dot_general | solution.py:66
  374.5 34.8 %all_to_all.10 = bf16[128,32,1,1,256]{4,1,3,2,0:T(8,128)(2,1)S(1)} all-to-all(bf16[128,32,1,1,256]{4,1,3,2,0:T(8,128)(2,1)S(1)} %bitcast.149), channel_id=1, replica_groups=mesh['row'=16,'col'=8] {'row','col'}, dimensions={0} | all-to-all | bytes 4194304 | tf_op jit(solution)/shard_map/all_to_all | solution.py:180
  (81 shorter events, 38.8 us)
Async XLA Ops:
  0.0 2.2 copy-start
  2.2 13.0 %copy-start.9 = (f32[8,64,64]{2,1,0:T(8,128)S(1)}, f32[8,64,64]{2,1,0:T(8,128)}, u32[]{:S(2)}) copy-start(f32[8,64,64]{2,1,0:T(8,128)} %param.31) | copy-start | bytes 393220
  2.2 13.1 %copy-start.13 = (f32[3,3,1024]{2,1,0:T(4,128)S(1)}, f32[3,3,1024]{2,1,0:T(4,128)}, u32[]{:S(2)}) copy-start(f32[3,3,1024]{2,1,0:T(4,128)} %param.25) | copy-start | bytes 110596
  9.4 3.2 copy-start.2
  12.6 13.8 %copy-start.14 = (f32[2,256]{1,0:T(2,128)S(1)}, f32[2,256]{1,0:T(2,128)}, u32[]{:S(2)}) copy-start(f32[2,256]{1,0:T(2,128)} %param.28) | copy-start | bytes 6148
  12.6 2.8 collective-permute-start
  13.9 5.1 %collective-permute-start.1 = (bf16[1,64,1024]{2,1,0:T(8,128)(2,1)S(1)}, bf16[1,64,1024]{2,1,0:T(8,128)(2,1)S(1)}, u32[]{:S(2)}, u32[]{:S(2)}) collective-permute-start(bf16[1,64,1024]{2,1,0:T(8,128)(2,1)S(1)} %get-tuple-element.16), channel_id=1, source_target_pairs={{8,0},{16,8},{24,16},{32,24},{40,32},{48,40},{56,48},{64,56},{72,6... | collective-permute-start | bytes 393224 | tf_op jit(solution)/shard_map/ppermute | solution.py:22
  15.4 18.3 %copy-start.3 = (bf16[4096,1024]{1,0:T(8,128)(2,1)S(1)}, bf16[4096,1024]{1,0:T(8,128)(2,1)}, u32[]{:S(2)}) copy-start(bf16[4096,1024]{1,0:T(8,128)(2,1)} %copy-done.2) | copy-start | bytes 25165828
  21.1 8.0 %collective-permute-start.2 = (bf16[66,1,1024]{2,1,0:T(2,128)(2,1)S(1)}, bf16[66,1,1024]{2,1,0:T(2,128)(2,1)S(1)}, u32[]{:S(2)}, u32[]{:S(2)}) collective-permute-start(bf16[66,1,1024]{2,1,0:T(2,128)(2,1)S(1)} %get-tuple-element.13), channel_id=1, source_target_pairs={{0,1},{1,2},{2,3},{3,4},{4,5},{5,6},{6,7},{8,9},{9,10},{10,11},{11... | collective-permute-start | bytes 405512 | tf_op jit(solution)/shard_map/ppermute | solution.py:19
  24.9 8.7 %collective-permute-start.3 = (bf16[66,1,1024]{2,1,0:T(2,128)(2,1)S(1)}, bf16[66,1,1024]{2,1,0:T(2,128)(2,1)S(1)}, u32[]{:S(2)}, u32[]{:S(2)}) collective-permute-start(bf16[66,1,1024]{2,1,0:T(2,128)(2,1)S(1)} %get-tuple-element.14), channel_id=1, source_target_pairs={{1,0},{2,1},{3,2},{4,3},{5,4},{6,5},{7,6},{9,8},{10,9},{11,10},{12... | collective-permute-start | bytes 405512 | tf_op jit(solution)/shard_map/ppermute | solution.py:22
  26.4 21.0 %copy-start.16 = (bf16[1024,256]{1,0:T(8,128)(2,1)S(1)}, bf16[1024,256]{1,0:T(8,128)(2,1)}, u32[]{:S(2)}) copy-start(bf16[1024,256]{1,0:T(8,128)(2,1)} %param.27) | copy-start | bytes 1572868
  26.4 21.0 %copy-start.19 = (f32[1024]{0:T(1024)S(1)}, f32[1024]{0:T(1024)}, u32[]{:S(2)}) copy-start(f32[1024]{0:T(1024)} %param.26) | copy-start | bytes 12292
  80.1 6.5 %copy-start.4 = (bf16[64,64,256]{2,1,0:T(8,128)(2,1)S(1)}, bf16[64,64,256]{2,1,0:T(8,128)(2,1)}, u32[]{:S(2)}) copy-start(bf16[64,64,256]{2,1,0:T(8,128)(2,1)} %fusion.70) | copy-start | bytes 6291460
  88.0 8.1 %copy-start.7 = (bf16[256,768]{1,0:T(8,128)(2,1)S(1)}, bf16[256,768]{1,0:T(8,128)(2,1)}, u32[]{:S(2)}) copy-start(bf16[256,768]{1,0:T(8,128)(2,1)} %param.29) | copy-start | bytes 1179652
  175.4 12.8 %copy-start.11 = (bf16[256,256]{1,0:T(8,128)(2,1)S(1)}, bf16[256,256]{1,0:T(8,128)(2,1)}, u32[]{:S(2)}) copy-start(bf16[256,256]{1,0:T(8,128)(2,1)} %param.30) | copy-start | bytes 393220
  182.5 11.9 %copy-start.17 = (bf16[1024,256]{1,0:T(8,128)(2,1)S(1)}, bf16[1024,256]{1,0:T(8,128)(2,1)}, u32[]{:S(2)}) copy-start(bf16[1024,256]{1,0:T(8,128)(2,1)} %param.33) | copy-start | bytes 1572868
  191.7 1.3 copy-start.5
  203.5 18.3 %copy-start.10 = (f32[8,64,64]{2,1,0:T(8,128)S(1)}, f32[8,64,64]{2,1,0:T(8,128)}, u32[]{:S(2)}) copy-start(f32[8,64,64]{2,1,0:T(8,128)} %param.37) | copy-start | bytes 393220
  203.5 18.5 %copy-start.15 = (f32[2,256]{1,0:T(2,128)S(1)}, f32[2,256]{1,0:T(2,128)}, u32[]{:S(2)}) copy-start(f32[2,256]{1,0:T(2,128)} %param.34) | copy-start | bytes 6148
  205.1 47.1 %all-to-all-start = ((bf16[128,32,1,1,256]{4,1,3,2,0:T(8,128)(2,1)}), bf16[128,32,1,1,256]{4,1,3,2,0:T(8,128)(2,1)S(1)}, u32[]{:S(2)}, u32[]{:S(2)}) async-start(bf16[128,32,1,1,256]{4,1,3,2,0:T(8,128)(2,1)} %bitcast.148), calls=%async_computation | async-start | bytes 4194304 | tf_op jit(solution)/shard_map/all_to_all | solution.py:150
  256.7 10.1 %copy-start.8 = (bf16[256,768]{1,0:T(8,128)(2,1)S(1)}, bf16[256,768]{1,0:T(8,128)(2,1)}, u32[]{:S(2)}) copy-start(bf16[256,768]{1,0:T(8,128)(2,1)} %param.35) | copy-start | bytes 1179652
  345.2 12.8 %copy-start.12 = (bf16[256,256]{1,0:T(8,128)(2,1)S(1)}, bf16[256,256]{1,0:T(8,128)(2,1)}, u32[]{:S(2)}) copy-start(bf16[256,256]{1,0:T(8,128)(2,1)} %param.36) | copy-start | bytes 393220
  352.3 11.9 %copy-start.18 = (bf16[1024,256]{1,0:T(8,128)(2,1)S(1)}, bf16[1024,256]{1,0:T(8,128)(2,1)}, u32[]{:S(2)}) copy-start(bf16[1024,256]{1,0:T(8,128)(2,1)} %param.39) | copy-start | bytes 1572868
  361.6 1.3 copy-start.6
  364.2 46.4 %copy-start.1 = (bf16[256,1024]{1,0:T(8,128)(2,1)S(1)}, bf16[256,1024]{1,0:T(8,128)(2,1)}, u32[]{:S(2)}) copy-start(bf16[256,1024]{1,0:T(8,128)(2,1)} %param.23) | copy-start | bytes 1572868
where the time goes:
time: 416 us; the launch traced here: 411 us
  matrix products  153 us (37%)
  local copies, waits for them, and re-layouts  118 us (28%)
  waiting for transfers between devices  41.1 us (10%)
  other arithmetic  38.7 us (9%)
  blocking collectives  34.8 us (8%)
  starting transfers between devices  24.6 us (6%)
    dot_general x2, matrix products, attend(): jnp.einsum('nqhd,nkhd->nhqk', query_rows, key_rows, preferred_element_typ...  40.5 us
    dot_general x2, matrix products, attend(): jnp.einsum('nhqk,nkhd->nqhd', weights, value_rows, preferred_element_type...  38.3 us
    reshape x2, local copies, waits for them, and re-layouts, attend(): projected.reshape(win_count, positions, 3, head_count, head_size)  35.7 us
    all_to_all x1, blocking collectives, shards(): lax.all_to_all(returning, ('row', 'col'), split_axis=0, concat_axis=0, ti...  34.8 us
    dot_general x1, matrix products, shards(): jnp.dot(activated.reshape(-1, inner_width), project_weight, preferred_ele...  32.6 us
    all_to_all x1, waiting for transfers between devices, shards(): lax.all_to_all(outgoing, ('row', 'col'), split_axis=0, concat_axis=0, til...  30.2 us
    dot_general x2, matrix products, attend(): jnp.dot(hidden, shrink_weight, preferred_element_type=jnp.float32)  18.2 us
    convert_element_type x2, local copies, waits for them, and re-layouts, attend(): jnp.dot(lifted, entry_weight, preferred_element_type=jnp.float32)  17.4 us
  transfers between devices with their start and end apart: 5, of which 4 were waited for; matrix products, arithmetic and copies ran while one was open for 0% of the time, Pallas kernels for 0%

commit v1 on v0

v1 whole, which is shorter than its diff:
```python
import functools
import math

import jax
import jax.numpy as jnp
from jax import lax
from jax.experimental import pallas as pl
from jax.experimental.pallas import tpu as pltpu
from jax.sharding import Mesh, PartitionSpec as P

WIN = 8
STRIP = 8
epsilon = 1e-05
F32 = jnp.float32
BF16 = jnp.bfloat16
GELU_A = math.sqrt(2.0 / math.pi)
GELU_B = GELU_A * 0.044715
LOG2E = math.log2(math.e)


def twice_gelu(v):
    return v + v * jnp.tanh(v * (GELU_A + GELU_B * (v * v)))


def dot(a, b):
    return jnp.dot(a, b, preferred_element_type=F32)


def load_halves(ref, where):
    return jnp.concatenate([ref[0, where, :], ref[1, where, :]], axis=-1)


def store_halves(ref, where, values):
    ref[0, where, :] = values[:, :128]
    ref[1, where, :] = values[:, 128:]


def layer_norm(values, values_bf16, averager, gain):
    mean = dot(values_bf16, averager)
    center = values - jnp.concatenate([mean, mean], axis=-1)
    spread = dot((center * center).astype(BF16), averager)
    scale = lax.rsqrt(spread + epsilon)
    return (center * jnp.concatenate([scale, scale], axis=-1) * gain).astype(BF16)


def prepare_offsets(table_ref, offs_scr):
    heads = table_ref.shape[0]
    for pair in range(heads // 2):
        two = jnp.concatenate([table_ref[2 * pair], table_ref[2 * pair + 1]], axis=-1)
        offs_scr[:, pair * 128 : (pair + 1) * 128] = two * LOG2E


def attend_rows(rows, gains_ref, entry_ref, leave_ref, widen_ref, shrink_ref, offs_scr, scr):
    qkv_scr, prob_scr, mix_scr, hid_scr = scr
    count, channels = rows.shape
    windows = count // 64
    averager = jnp.full((channels, 128), 1.0 / channels, BF16)
    normed = layer_norm(rows, rows.astype(BF16), averager, gains_ref[0:1, :])
    for part in range(3):
        cut = slice(part * channels, (part + 1) * channels)
        qkv_scr[:, cut] = dot(normed, entry_ref[:, cut]).astype(BF16)
    scale = LOG2E / math.sqrt(32.0)
    lane = lax.broadcasted_iota(jnp.int32, (64, 128), 1) // 32
    masks = [(lane == h).astype(F32).astype(BF16) for h in range(4)]
    key_head = lax.broadcasted_iota(jnp.int32, (256, 256), 0) // 64
    out_head = lax.broadcasted_iota(jnp.int32, (256, 256), 1) // 64
    adder = (key_head == out_head).astype(F32).astype(BF16)
    for w in range(windows):
        here = slice(w * 64, (w + 1) * 64)
        for g in range(2):
            part = slice(g * 128, (g + 1) * 128)
            keys = qkv_scr[here, channels + g * 128 : channels + (g + 1) * 128]
            wide = jnp.concatenate([keys * m for m in masks], axis=0)
            score = lax.dot_general(
                qkv_scr[here, part], wide, (((1,), (1,)), ((), ())), preferred_element_type=F32
            )
            wide_part = slice(g * 256, (g + 1) * 256)
            prob = jnp.exp2(score * scale + offs_scr[:, wide_part])
            prob_scr[here, wide_part] = prob
    for g in range(2):
        wide_part = slice(g * 256, (g + 1) * 256)
        prob = prob_scr[:, wide_part]
        total = dot(prob.astype(BF16), adder)
        weight = (prob / total).astype(BF16)
        for w in range(windows):
            here = slice(w * 64, (w + 1) * 64)
            start = 2 * channels + g * 128
            vals = qkv_scr[here, start : start + 128]
            wide = jnp.concatenate([vals * m for m in masks], axis=0)
            mix_scr[here, g * 128 : (g + 1) * 128] = dot(weight[here], wide).astype(BF16)
    attended_bf16 = (rows + dot(mix_scr[...], leave_ref[...])).astype(BF16)
    attended = attended_bf16.astype(F32)
    second = layer_norm(attended, attended_bf16, averager, gains_ref[1:2, :])
    inner = widen_ref.shape[1]
    for cut in range(0, inner, 256):
        hid_scr[:, cut : cut + 256] = twice_gelu(dot(second, widen_ref[:, cut : cut + 256])).astype(
            BF16
        )
    return attended + 0.5 * dot(hid_scr[...], shrink_ref[...])


def conv_block_kernel(
    flags_ref,
    x_ref,
    above_ref,
    below_ref,
    sides_ref,
    first_sides_ref,
    scale_ref,
    shift_ref,
    expand_ref,
    expand_bias_ref,
    depth_ref,
    depth_bias_ref,
    project_ref,
    gains_ref,
    entry_ref,
    leave_ref,
    offsets_ref,
    widen_ref,
    shrink_ref,
    out_ref,
    x_scr,
    wide_scr,
    norm_scr,
    exp_scr,
    act_scr,
    prod_scr,
    offs_scr,
    *attend_scr,
):
    step = pl.program_id(0)
    steps = pl.num_programs(0)
    strip_tokens = STRIP * 64
    inner = expand_ref.shape[1]
    blocks = inner // 256

    def expand(ext_rows, row_count, first_slot_row, left, right):
        tokens = row_count * 64
        cells = x_scr[pl.ds(pl.multiple_of(ext_rows * 64, 64), tokens), :].astype(F32)
        store_halves(wide_scr, slice(0, tokens), cells)
        per = row_count * 8
        for low in range(8):
            part = load_halves(wide_scr, pl.ds(low, per, stride=8))
            norm_scr[low * per : (low + 1) * per, :] = (
                part * scale_ref[...] + shift_ref[...]
            ).astype(BF16)
        side = jnp.concatenate([left, right], axis=0)
        norm_scr[8 * per : 8 * per + 16, :] = (side * scale_ref[...] + shift_ref[...]).astype(BF16)

        sub = lax.broadcasted_iota(jnp.int32, (8, 256), 0)

        def one(block, carry):
            cut = pl.ds(pl.multiple_of(block * 256, 256), 256)
            bias = expand_bias_ref[:, cut]
            cells = twice_gelu(
                dot(norm_scr[0 : 8 * per + 16, :], expand_ref[:, cut]) + bias
            )
            for low in range(8):
                exp_scr[low + 1, pl.ds(first_slot_row, row_count), :, cut] = cells[
                    low * per : (low + 1) * per
                ].reshape(row_count, 8, 256)
            for y in range(row_count):
                last = cells[7 * per + y * 8 : 7 * per + y * 8 + 8]
                first = cells[y * 8 : y * 8 + 8]
                at_left = cells[8 * per + y : 8 * per + y + 1] * flags_ref[2]
                at_right = cells[8 * per + 8 + y : 8 * per + 9 + y] * flags_ref[3]
                exp_scr[0, first_slot_row + y, :, cut] = jnp.where(
                    sub == 0, at_left, pltpu.roll(last, 1, 0)
                )
                exp_scr[9, first_slot_row + y, :, cut] = jnp.where(
                    sub == 7, at_right, pltpu.roll(first, 7, 0)
                )
            return carry

        lax.fori_loop(0, blocks, one, 0)

    @pl.when(step == 0)
    def _():
        body = x_ref.shape[0]
        x_scr[0:64, :] = above_ref[...]
        x_scr[64 : 64 + body, :] = x_ref[...]
        x_scr[64 + body : 128 + body, :] = below_ref[...]
        prepare_offsets(offsets_ref, offs_scr)
        expand(0, 2, 0, first_sides_ref[0], first_sides_ref[1])
        for slot in range(10):
            exp_scr[slot, 0] = exp_scr[slot, 0] * flags_ref[0]

    @pl.when(step > 0)
    def _():
        for slot in range(10):
            exp_scr[slot, 0:2] = exp_scr[slot, 8:10]

    expand(step * STRIP + 2, STRIP, 2, sides_ref[0], sides_ref[1])

    @pl.when(step == steps - 1)
    def _():
        for slot in range(10):
            exp_scr[slot, 9] = exp_scr[slot, 9] * flags_ref[1]

    def convolve(block, carry):
        cut = pl.ds(pl.multiple_of(block * 256, 256), 256)
        taps = [
            [jnp.broadcast_to(0.5 * depth_ref[3 * s + t : 3 * s + t + 1, cut], (8, 256)) for t in range(3)]
            for s in range(3)
        ]
        bias = jnp.broadcast_to(depth_bias_ref[:, cut], (8, 256))
        for low in range(8):
            total = jnp.broadcast_to(bias[None], (8, 8, 256))
            for s in range(3):
                for t in range(3):
                    total = total + exp_scr[low + t, s : s + 8, :, cut] * taps[s][t][None]
            act_scr[low * 64 : (low + 1) * 64, cut] = (
                twice_gelu(total).reshape(64, 256).astype(BF16)
            )
        return carry

    lax.fori_loop(0, blocks, convolve, 0)
    store_halves(prod_scr, slice(0, strip_tokens), dot(act_scr[...], project_ref[...]))
    pieces = []
    for w in range(8):
        for y in range(8):
            pieces.append(load_halves(prod_scr, pl.ds(y * 8 + w, 8, stride=64)))
    product = jnp.concatenate(pieces, axis=0)
    source = x_scr[pl.ds(pl.multiple_of((step * STRIP + 1) * 64, 64), strip_tokens), :].astype(F32)
    source = source.reshape(8, 8, 8, 256).swapaxes(0, 1).reshape(strip_tokens, 256)
    rows = (source + 0.5 * product).astype(BF16).astype(F32)
    done = attend_rows(
        rows, gains_ref, entry_ref, leave_ref, widen_ref, shrink_ref, offs_scr, attend_scr
    )
    done = done.reshape(8, 8, 8, 256).swapaxes(0, 1).reshape(strip_tokens, 256)
    out_ref[...] = done.astype(BF16)


def grid_kernel(
    x_ref,
    gains_ref,
    entry_ref,
    leave_ref,
    offsets_ref,
    widen_ref,
    shrink_ref,
    out_ref,
    in_scr,
    back_scr,
    offs_scr,
    *attend_scr,
):
    @pl.when(pl.program_id(0) == 0)
    def _():
        prepare_offsets(offsets_ref, offs_scr)

    store_halves(in_scr, slice(0, 512), x_ref[...].astype(F32).reshape(512, 256))
    rows = jnp.concatenate([load_halves(in_scr, pl.ds(w, 64, stride=8)) for w in range(8)], axis=0)
    done = attend_rows(
        rows, gains_ref, entry_ref, leave_ref, widen_ref, shrink_ref, offs_scr, attend_scr
    )
    for w in range(8):
        store_halves(back_scr, pl.ds(w, 64, stride=8), done[w * 64 : (w + 1) * 64])
    out_ref[...] = load_halves(back_scr, slice(0, 512)).reshape(64, 8, 256).astype(BF16)


def attend_scratch():
    return [
        pltpu.VMEM((64, 512), F32),
        pltpu.VMEM((512, 768), BF16),
        pltpu.VMEM((512, 512), F32),
        pltpu.VMEM((512, 256), BF16),
        pltpu.VMEM((512, 1024), BF16),
    ]


def whole(shape):
    return pl.BlockSpec(shape, lambda i: (0,) * len(shape))


def conv_block(flags, x, part, parts, above, below, sides, first_sides, weights):
    tokens, channels = x.shape
    body = tokens // parts
    steps = body // (STRIP * 64)
    return pl.pallas_call(
        conv_block_kernel,
        grid=(steps,),
        in_specs=[
            pl.BlockSpec(memory_space=pltpu.SMEM),
            pl.BlockSpec((body, channels), lambda i: (part, 0)),
            whole((64, channels)) if above.shape[0] == 64 else pl.BlockSpec((64, channels), lambda i: (part * (body // 64) - 1, 0)),
            whole((64, channels)) if below.shape[0] == 64 else pl.BlockSpec((64, channels), lambda i: ((part + 1) * (body // 64), 0)),
            pl.BlockSpec((2, 8, channels), lambda i: (0, i, 0)),
            whole((2, 8, channels)),
        ]
        + [whole(w.shape) for w in weights],
        out_specs=pl.BlockSpec((STRIP * 64, channels), lambda i: (i, 0)),
        out_shape=jax.ShapeDtypeStruct((body, channels), BF16),
        scratch_shapes=[
            pltpu.VMEM((body + 128, channels), BF16),
            pltpu.VMEM((2, 512, 128), F32),
            pltpu.VMEM((528, channels), BF16),
            pltpu.VMEM((10, 10, 8, 1024), F32),
            pltpu.VMEM((512, 1024), BF16),
            pltpu.VMEM((2, 512, 128), F32),
        ]
        + attend_scratch(),
        compiler_params=pltpu.CompilerParams(vmem_limit_bytes=56 << 20),
        cost_estimate=pl.CostEstimate(
            flops=body * 2600000, bytes_accessed=body * 1024 + 4000000, transcendentals=0
        ),
        name="conv_block",
    )(flags, x, above, below, sides, first_sides, *weights)


def grid_attend(x, weights):
    sources, count, channels = x.shape
    return pl.pallas_call(
        grid_kernel,
        grid=(count // 8,),
        in_specs=[pl.BlockSpec((sources, 8, channels), lambda i: (0, i, 0))]
        + [whole(w.shape) for w in weights],
        out_specs=pl.BlockSpec((sources, 8, channels), lambda i: (0, i, 0)),
        out_shape=jax.ShapeDtypeStruct(x.shape, BF16),
        scratch_shapes=[pltpu.VMEM((2, 512, 128), F32), pltpu.VMEM((2, 512, 128), F32)]
        + attend_scratch(),
        compiler_params=pltpu.CompilerParams(vmem_limit_bytes=56 << 20),
        cost_estimate=pl.CostEstimate(
            flops=sources * count * 1600000, bytes_accessed=sources * count * 1024 + 4000000, transcendentals=0
        ),
        name="grid_attend",
    )(x, *weights)


ROW = ("row_hi", "core")
GROUP = ("row_hi", "col")


def shards(
    radar_tiles,
    conv_scale,
    conv_shift,
    expand_weight,
    expand_bias,
    depth_kernel,
    depth_bias,
    project_weight,
    block_gains,
    block_entry,
    block_leave,
    block_offsets,
    block_widen,
    block_shrink,
    grid_gains,
    grid_entry,
    grid_leave,
    grid_offsets,
    grid_widen,
    grid_shrink,
    parts=2,
):
    rows_here, cols_here, channels = radar_tiles.shape
    row_count, col_count = lax.axis_size(ROW), lax.axis_size("col")
    row, col = lax.axis_index(ROW), lax.axis_index("col")

    def shifted(values, axis, count, step):
        pairs = [(i, i + step) for i in range(count) if 0 <= i + step < count]
        return lax.ppermute(values, axis, pairs)

    above = shifted(radar_tiles[-1:], ROW, row_count, 1)
    below = shifted(radar_tiles[:1], ROW, row_count, -1)
    edges = [
        jnp.concatenate([above[:, e], radar_tiles[:, e], below[:, e]], axis=0) for e in (-1, 0)
    ]
    left = shifted(edges[0], "col", col_count, 1)
    right = shifted(edges[1], "col", col_count, -1)
    sides = jnp.stack([left, right]).astype(F32)
    x = radar_tiles.reshape(rows_here * cols_here, channels)
    above = above.reshape(cols_here, channels)
    below = below.reshape(cols_here, channels)
    weights = (
        conv_scale.reshape(1, -1),
        conv_shift.reshape(1, -1),
        expand_weight,
        expand_bias.reshape(1, -1),
        depth_kernel.reshape(9, -1),
        depth_bias.reshape(1, -1),
        project_weight,
        block_gains,
        block_entry,
        block_leave,
        block_offsets,
        block_widen,
        block_shrink,
    )
    grid_weights = (grid_gains, grid_entry, grid_leave, grid_offsets, grid_widen, grid_shrink)
    group = row_count // 2 * col_count
    span = rows_here // parts
    outs = []
    for part in range(parts):
        start = part * span
        flags = jnp.stack(
            [
                jnp.where(row > 0, 1.0, 0.0) if part == 0 else jnp.float32(1.0),
                jnp.where(row < row_count - 1, 1.0, 0.0) if part == parts - 1 else jnp.float32(1.0),
                jnp.where(col > 0, 1.0, 0.0),
                jnp.where(col < col_count - 1, 1.0, 0.0),
            ]
        ).astype(F32)
        first = jnp.pad(sides[:, start : start + 2], ((0, 0), (0, 6), (0, 0)))
        mine = conv_block(
            flags,
            x,
            part,
            parts,
            above if part == 0 else x,
            below if part == parts - 1 else x,
            sides[:, start + 2 : start + 2 + span],
            first,
            weights,
        )
        outgoing = mine.reshape(group, -1, channels)
        outs.append(lax.all_to_all(outgoing, GROUP, split_axis=0, concat_axis=0, tiled=True))
    finished = []
    for arrived in outs:
        spread = grid_attend(arrived, grid_weights)
        finished.append(lax.all_to_all(spread, GROUP, split_axis=0, concat_axis=0, tiled=True))
    return jnp.concatenate(
        [f.reshape(span, cols_here, channels) for f in finished], axis=0
    )


def solution(mesh):
    inner = Mesh(mesh.devices.reshape(8, 2, 8), ("row_hi", "core", "col"))
    tiles = P(ROW, "col", None)
    return jax.shard_map(
        shards,
        mesh=inner,
        in_specs=(tiles,) + (P(),) * 19,
        out_specs=tiles,
        check_vma=False,
    )
```

time: 416 us -> 178 us (0.43); the launches traced: 411 us -> 177 us
  matrix products: 153 us -> 0 us
  local copies, waits for them, and re-layouts: 118 us -> 4.68 us
  Pallas kernels: 0 us -> 92.1 us
  other arithmetic: 38.7 us -> 4.09 us
  waiting for transfers between devices: 41.1 us -> 10.7 us
  starting transfers between devices: 24.6 us -> 41.8 us
  blocking collectives: 34.8 us -> 23.8 us
    dot_general x12 -> x0, matrix products: 153 us -> none  [the longest x2 40.5 us: attend(): jnp.einsum('nqhd,nkhd->nhqk', query_rows, key_rows, preferred_element_typ...]
    pallas_call x0 -> x4, Pallas kernels: none -> 92.1 us  [the longest x2 64.1 us: conv_block(): pl.pallas_call(conv_block_kernel, grid=(steps,), in_specs=[pl.BlockSpec(m...]
    reshape x4 -> x1, local copies, waits for them, and re-layouts: 47.2 us -> 1.45 us  [shards(): depth_kernel.reshape(9, -1)]
    convert_element_type x6 -> x0, local copies, waits for them, and re-layouts: 42.9 us -> none  [the longest x2 17.4 us: attend(): jnp.dot(lifted, entry_weight, preferred_element_type=jnp.float32)]
    all_to_all x1 -> x3, waiting for transfers between devices: 30.2 us -> 8.26 us  [the longest x2 4.35 us: shards(): lax.all_to_all(outgoing, GROUP, split_axis=0, concat_axis=0, tiled=True)]
    all_to_all x1 -> x3, starting transfers between devices: 16.7 us -> 33.4 us  [the longest x2 27.6 us: shards(): lax.all_to_all(outgoing, GROUP, split_axis=0, concat_axis=0, tiled=True)]
    convert_element_type x5 -> x1, other arithmetic: 14.6 us -> 0.01 us  [shards(): sides = jnp.stack([left, right]).astype(F32)]
    slice x6 -> x3, local copies, waits for them, and re-layouts: 16.8 us -> 2.58 us  [the longest x1 1.14 us: shards(): radar_tiles[:, e]]
  transfers between devices with their start and end apart: 5 -> 7, of which waited for: 4 -> 3; matrix products, arithmetic and copies ran while one was open for 0% -> 3% of each run, Pallas kernels for 0% -> 34%
where the time goes in v1:
time: 178 us; the launch traced here: 177 us
  Pallas kernels  92.1 us (52%)
  starting transfers between devices  41.8 us (23%)
  blocking collectives  23.8 us (13%)
  waiting for transfers between devices  10.7 us (6%)
  local copies, waits for them, and re-layouts  4.68 us (3%)
  other arithmetic  4.09 us (2%)
    pallas_call x2, Pallas kernels, conv_block(): pl.pallas_call(conv_block_kernel, grid=(steps,), in_specs=[pl.BlockSpec(m...  64.1 us
    pallas_call x2, Pallas kernels, grid_attend(): pl.pallas_call(grid_kernel, grid=(count // 8,), in_specs=[pl.BlockSpec((s...  28 us
    all_to_all x2, starting transfers between devices, shards(): lax.all_to_all(outgoing, GROUP, split_axis=0, concat_axis=0, tiled=True)  27.6 us
    all_to_all x1, blocking collectives, shards(): lax.all_to_all(spread, GROUP, split_axis=0, concat_axis=0, tiled=True)  23.8 us
    ppermute x4, starting transfers between devices, shifted(): return lax.ppermute(values, axis, pairs)  8.41 us
    all_to_all x1, starting transfers between devices, shards(): lax.all_to_all(spread, GROUP, split_axis=0, concat_axis=0, tiled=True)  5.81 us
    all_to_all x2, waiting for transfers between devices, shards(): lax.all_to_all(outgoing, GROUP, split_axis=0, concat_axis=0, tiled=True)  4.35 us
    all_to_all x1, waiting for transfers between devices, shards(): lax.all_to_all(spread, GROUP, split_axis=0, concat_axis=0, tiled=True)  3.91 us
  transfers between devices with their start and end apart: 7, of which 3 were waited for; matrix products, arithmetic and copies ran while one was open for 3% of the time, Pallas kernels for 34%

profile of v1, /device:TPU:0, one launch (start us, length us, event | category | flops | bytes accessed | tf_op | source)
XLA Modules:
  0.0 177.4 jit_solution(2212576820069104465)
XLA Ops:
  0.0 0.8 fusion.1
  0.8 1.3 collective-permute-start
  2.1 1.3 collective-permute-start.1
  3.4 1.1 fusion
  4.6 0.0 collective-permute-done
  4.6 0.0 copy-start.3
  4.6 2.5 %collective-permute-done.1 = bf16[1,64,256]{2,1,0:T(8,128)(2,1)S(1)} collective-permute-done((bf16[1,64,256]{2,1,0:T(8,128)(2,1)S(1)}, bf16[1,64,256]{2,1,0:T(8,128)(2,1)S(1)}, u32[]{:S(2)}, u32[]{:S(2)}) %collective-permute-start.1) | collective-permute-done | bytes 32800 | tf_op jit(solution)/shard_map/ppermute | solution.py:364
  7.1 1.3 collective-permute-start.3
  8.4 4.5 %collective-permute-start.2 = (bf16[66,256]{1,0:T(8,128)(2,1)S(1)}, bf16[66,256]{1,0:T(8,128)(2,1)S(1)}, u32[]{:S(2)}, u32[]{:S(2)}) collective-permute-start(bf16[66,256]{1,0:T(8,128)(2,1)S(1)} %pad_maximum_fusion.1), channel_id=1, source_target_pairs={{0,1},{1,2},{2,3},{3,4},{4,5},{5,6},{6,7},{8,9},{9,10},{10,11},{11... | collective-permute-start | bytes 101384 | tf_op jit(solution)/shard_map/ppermute | solution.py:364
  13.0 0.6 maximum_maximum_fusion.flags_ref
  13.6 1.4 reshape.41.depth_ref
  15.0 0.0 collective-permute-done.3
  15.0 0.0 collective-permute-done.2
  15.1 1.3 convert_select_fusion.first_sides_ref
  16.4 0.7 fusion.2
  17.0 0.0 copy-done.3
  17.1 32.1 %conv_block.2 = bf16[2048,256]{1,0:T(8,128)(2,1)} custom-call(f32[4]{0:T(128)} %maximum_maximum_fusion.flags_ref, bf16[4096,256]{1,0:T(8,128)(2,1)} %bitcast.43, bf16[64,256]{1,0:T(8,128)(2,1)} %bitcast.48, bf16[4096,256]{1,0:T(8,128)(2,1)} %bitcast.44, f32[2,32,256]{2,1,0:T(8,128)} %get-tuple-element.9.sides_ref, ...), custom_call_target="tpu_custom_call" | custom-call | flops 5324800000 | bytes 6097152 | tf_op jit(solution)/shard_map/conv_block/pallas_call | solution.py:281
  49.1 17.1 %all-to-all-start = ((bf16[64,32,256]{2,1,0:T(8,128)(2,1)}), bf16[64,32,256]{2,1,0:T(8,128)(2,1)S(1)}, u32[]{:S(2)}, u32[]{:S(2)}) async-start(bf16[64,32,256]{2,1,0:T(8,128)(2,1)} %bitcast.33), calls=%async_computation | async-start | bytes 2097152 | tf_op jit(solution)/shard_map/all_to_all | solution.py:419
  66.2 0.6 maximum_maximum_fusion.1.flags_ref
  66.8 0.6 pad.8.first_sides_ref
  67.4 32.0 %conv_block.3 = bf16[2048,256]{1,0:T(8,128)(2,1)} custom-call(f32[4]{0:T(128)} %maximum_maximum_fusion.1.flags_ref, bf16[4096,256]{1,0:T(8,128)(2,1)} %bitcast.45, bf16[4096,256]{1,0:T(8,128)(2,1)} %bitcast.46, bf16[64,256]{1,0:T(8,128)(2,1)} %bitcast.47, f32[2,32,256]{2,1,0:T(8,128)} %get-tuple-element.10.sides_ref, f32[2,8,256]{2,1,0:T(8,128)} %pad.8.first_sides_ref, ...), custom_call_target="tpu_custom_call" | custom-call | flops 5324800000 | bytes 6097152 | tf_op jit(solution)/shard_map/conv_block/pallas_call | solution.py:281
  99.4 0.0 all-to-all-done.x_ref
  99.4 0.0 copy-start
  99.4 10.5 %all-to-all-start.2 = ((bf16[64,32,256]{2,1,0:T(8,128)(2,1)}), bf16[64,32,256]{2,1,0:T(8,128)(2,1)S(1)}, u32[]{:S(2)}, u32[]{:S(2)}) async-start(bf16[64,32,256]{2,1,0:T(8,128)(2,1)} %bitcast.34), calls=%async_computation.2 | async-start | bytes 2097152 | tf_op jit(solution)/shard_map/all_to_all | solution.py:419
  110.0 14.0 %grid_attend.2 = bf16[64,32,256]{2,1,0:T(8,128)(2,1)} custom-call(bf16[64,32,256]{2,1,0:T(8,128)(2,1)} %copy-done, f32[2,256]{1,0:T(2,128)} %gains_ref.7, bf16[256,768]{1,0:T(8,128)(2,1)} %entry_ref.7, bf16[256,256]{1,0:T(8,128)(2,1)} %leave_ref.7, f32[8,64,64]{2,1,0:T(8,128)} %offsets_ref.7, bf16[256,1024]{1,0:T(8,128)(2,1)} %widen_ref.7, ...), custom_call_target="tpu_custom_call" | custom-call | flops 3276800000 | bytes 6097152 | tf_op jit(solution)/shard_map/grid_attend/pallas_call | solution.py:314
  124.0 4.3 %all-to-all-done.2.x_ref = bf16[64,32,256]{2,1,0:T(8,128)(2,1)S(1)} async-done(((bf16[64,32,256]{2,1,0:T(8,128)(2,1)}), bf16[64,32,256]{2,1,0:T(8,128)(2,1)S(1)}, u32[]{:S(2)}, u32[]{:S(2)}) %all-to-all-start.2) | async-done | bytes 1048608 | tf_op jit(solution)/shard_map/all_to_all | solution.py:419
  128.3 5.8 %all-to-all-start.1 = ((bf16[64,32,256]{2,1,0:T(8,128)(2,1)}), bf16[64,32,256]{2,1,0:T(8,128)(2,1)S(1)}, u32[]{:S(2)}, u32[]{:S(2)}) async-start(bf16[64,32,256]{2,1,0:T(8,128)(2,1)} %grid_attend.2), calls=%async_computation.1 | async-start | bytes 2097152 | tf_op jit(solution)/shard_map/all_to_all | solution.py:423
  134.1 0.0 copy-done.1
  134.2 14.0 %grid_attend.3 = bf16[64,32,256]{2,1,0:T(8,128)(2,1)} custom-call(bf16[64,32,256]{2,1,0:T(8,128)(2,1)} %copy-done.1, f32[2,256]{1,0:T(2,128)} %gains_ref.7, bf16[256,768]{1,0:T(8,128)(2,1)} %entry_ref.7, bf16[256,256]{1,0:T(8,128)(2,1)} %leave_ref.7, f32[8,64,64]{2,1,0:T(8,128)} %offsets_ref.7, bf16[256,1024]{1,0:T(8,128)(2,1)} %widen_ref.7, ...), custom_call_target="tpu_custom_call" | custom-call | flops 3276800000 | bytes 6097152 | tf_op jit(solution)/shard_map/grid_attend/pallas_call | solution.py:314
  148.2 3.9 %all-to-all-done.1 = bf16[64,32,256]{2,1,0:T(8,128)(2,1)S(1)} async-done(((bf16[64,32,256]{2,1,0:T(8,128)(2,1)}), bf16[64,32,256]{2,1,0:T(8,128)(2,1)S(1)}, u32[]{:S(2)}, u32[]{:S(2)}) %all-to-all-start.1) | async-done | bytes 1048608 | tf_op jit(solution)/shard_map/all_to_all | solution.py:423
  152.1 23.8 %all_to_all.20 = bf16[64,32,256]{2,1,0:T(8,128)(2,1)S(1)} all-to-all(bf16[64,32,256]{2,1,0:T(8,128)(2,1)} %grid_attend.3), channel_id=1, replica_groups=mesh['row_hi'=8,'core'=2,'col'=8] {'row_hi','col'}, dimensions={0} | all-to-all | bytes 2097152 | tf_op jit(solution)/shard_map/all_to_all | solution.py:423
  175.9 1.5 pad_maximum_fusion
  (12 shorter events, 0.1 us)
Async XLA Ops:
  0.8 3.8 %collective-permute-start = (bf16[1,64,256]{2,1,0:T(8,128)(2,1)S(1)}, bf16[1,64,256]{2,1,0:T(8,128)(2,1)S(1)}, u32[]{:S(2)}, u32[]{:S(2)}) collective-permute-start(bf16[1,64,256]{2,1,0:T(8,128)(2,1)S(1)} %get-tuple-element.7), channel_id=1, source_target_pairs={{0,8},{8,16},{16,24},{24,32},{32,40},{40,48},{48,56},{56,64},{64,7... | collective-permute-start | bytes 98312 | tf_op jit(solution)/shard_map/ppermute | solution.py:364
  2.1 5.0 %collective-permute-start.1 = (bf16[1,64,256]{2,1,0:T(8,128)(2,1)S(1)}, bf16[1,64,256]{2,1,0:T(8,128)(2,1)S(1)}, u32[]{:S(2)}, u32[]{:S(2)}) collective-permute-start(bf16[1,64,256]{2,1,0:T(8,128)(2,1)S(1)} %get-tuple-element.8), channel_id=1, source_target_pairs={{8,0},{16,8},{24,16},{32,24},{40,32},{48,40},{56,48},{64,56},{72,6... | collective-permute-start | bytes 98312 | tf_op jit(solution)/shard_map/ppermute | solution.py:364
  4.6 12.5 %copy-start.3 = (bf16[1,64,256]{2,1,0:T(8,128)(2,1)}, bf16[1,64,256]{2,1,0:T(8,128)(2,1)S(1)}, u32[]{:S(2)}) copy-start(bf16[1,64,256]{2,1,0:T(8,128)(2,1)S(1)} %collective-permute-done) | copy-start | bytes 98308
  7.1 42.1 %copy-start.2 = (bf16[1,64,256]{2,1,0:T(8,128)(2,1)}, bf16[1,64,256]{2,1,0:T(8,128)(2,1)S(1)}, u32[]{:S(2)}) copy-start(bf16[1,64,256]{2,1,0:T(8,128)(2,1)S(1)} %collective-permute-done.1) | copy-start | bytes 98308
  7.1 7.9 %collective-permute-start.3 = (bf16[66,256]{1,0:T(8,128)(2,1)S(1)}, bf16[66,256]{1,0:T(8,128)(2,1)S(1)}, u32[]{:S(2)}, u32[]{:S(2)}) collective-permute-start(bf16[66,256]{1,0:T(8,128)(2,1)S(1)} %pad_maximum_fusion.2), channel_id=1, source_target_pairs={{1,0},{2,1},{3,2},{4,3},{5,4},{6,5},{7,6},{9,8},{10,9},{11,10},{12... | collective-permute-start | bytes 101384 | tf_op jit(solution)/shard_map/ppermute | solution.py:364
  8.4 6.6 %collective-permute-start.2 = (bf16[66,256]{1,0:T(8,128)(2,1)S(1)}, bf16[66,256]{1,0:T(8,128)(2,1)S(1)}, u32[]{:S(2)}, u32[]{:S(2)}) collective-permute-start(bf16[66,256]{1,0:T(8,128)(2,1)S(1)} %pad_maximum_fusion.1), channel_id=1, source_target_pairs={{0,1},{1,2},{2,3},{3,4},{4,5},{5,6},{6,7},{8,9},{9,10},{10,11},{11... | collective-permute-start | bytes 101384 | tf_op jit(solution)/shard_map/ppermute | solution.py:364
  49.1 50.3 %all-to-all-start = ((bf16[64,32,256]{2,1,0:T(8,128)(2,1)}), bf16[64,32,256]{2,1,0:T(8,128)(2,1)S(1)}, u32[]{:S(2)}, u32[]{:S(2)}) async-start(bf16[64,32,256]{2,1,0:T(8,128)(2,1)} %bitcast.33), calls=%async_computation | async-start | bytes 2097152 | tf_op jit(solution)/shard_map/all_to_all | solution.py:419
  99.4 10.5 %copy-start = (bf16[64,32,256]{2,1,0:T(8,128)(2,1)}, bf16[64,32,256]{2,1,0:T(8,128)(2,1)S(1)}, u32[]{:S(2)}) copy-start(bf16[64,32,256]{2,1,0:T(8,128)(2,1)S(1)} %all-to-all-done.x_ref) | copy-start | bytes 3145732
  99.4 28.9 %all-to-all-start.2 = ((bf16[64,32,256]{2,1,0:T(8,128)(2,1)}), bf16[64,32,256]{2,1,0:T(8,128)(2,1)S(1)}, u32[]{:S(2)}, u32[]{:S(2)}) async-start(bf16[64,32,256]{2,1,0:T(8,128)(2,1)} %bitcast.34), calls=%async_computation.2 | async-start | bytes 2097152 | tf_op jit(solution)/shard_map/all_to_all | solution.py:419
  128.3 5.8 %copy-start.1 = (bf16[64,32,256]{2,1,0:T(8,128)(2,1)}, bf16[64,32,256]{2,1,0:T(8,128)(2,1)S(1)}, u32[]{:S(2)}) copy-start(bf16[64,32,256]{2,1,0:T(8,128)(2,1)S(1)} %all-to-all-done.2.x_ref) | copy-start | bytes 3145732
  128.3 23.8 %all-to-all-start.1 = ((bf16[64,32,256]{2,1,0:T(8,128)(2,1)}), bf16[64,32,256]{2,1,0:T(8,128)(2,1)S(1)}, u32[]{:S(2)}, u32[]{:S(2)}) async-start(bf16[64,32,256]{2,1,0:T(8,128)(2,1)} %grid_attend.2), calls=%async_computation.1 | async-start | bytes 2097152 | tf_op jit(solution)/shard_map/all_to_all | solution.py:423

commit v2 on v1

v2 whole, which is shorter than its diff:
```python
import functools
import math

import jax
import jax.numpy as jnp
from jax import lax
from jax.experimental import pallas as pl
from jax.experimental.pallas import tpu as pltpu
from jax.sharding import Mesh, PartitionSpec as P

WIN = 8
STRIP = 16
GRID_WINDOWS = 16
epsilon = 1e-05
F32 = jnp.float32
BF16 = jnp.bfloat16
GELU_A = math.sqrt(2.0 / math.pi)
GELU_B = GELU_A * 0.044715
LOG2E = math.log2(math.e)


def twice_gelu(v):
    return v + v * jnp.tanh(v * (GELU_A + GELU_B * (v * v)))


def dot(a, b):
    return jnp.dot(a, b, preferred_element_type=F32)


def load_halves(ref, where):
    return jnp.concatenate([ref[0, where, :], ref[1, where, :]], axis=-1)


def store_halves(ref, where, values):
    ref[0, where, :] = values[:, :128]
    ref[1, where, :] = values[:, 128:]


def layer_norm(values, gain):
    mean = jnp.mean(values, axis=-1, keepdims=True)
    center = values - mean
    spread = jnp.mean(center * center, axis=-1, keepdims=True)
    return (center * lax.rsqrt(spread + epsilon) * gain).astype(BF16)


def halves_dot(a, b):
    half = a.shape[0] // 2
    return jnp.concatenate([dot(a[:half], b), dot(a[half:], b)], axis=0)


def prepare_offsets(table_ref, offs_scr):
    heads = table_ref.shape[0]
    for pair in range(heads // 2):
        two = jnp.concatenate([table_ref[2 * pair], table_ref[2 * pair + 1]], axis=-1)
        offs_scr[:, pair * 128 : (pair + 1) * 128] = two * LOG2E


def attend_rows(rows, gains_ref, entry_ref, leave_ref, widen_ref, shrink_ref, offs_scr):
    count, channels = rows.shape
    windows = count // 64
    normed = layer_norm(rows, gains_ref[0:1, :])
    scale = LOG2E / math.sqrt(32.0)
    qkv = [
        halves_dot(normed, entry_ref[:, part * channels : (part + 1) * channels])
        for part in range(3)
    ]
    queries = (qkv[0] * scale).astype(BF16)
    keys = qkv[1].astype(BF16)
    values = qkv[2].astype(BF16)
    lane = lax.broadcasted_iota(jnp.int32, (64, 128), 1) // 32
    masks = [(lane == h).astype(F32).astype(BF16) for h in range(4)]
    key_head = lax.broadcasted_iota(jnp.int32, (256, 256), 0) // 64
    out_head = lax.broadcasted_iota(jnp.int32, (256, 256), 1) // 64
    adder = (key_head == out_head).astype(F32).astype(BF16)
    sides = []
    for g in range(2):
        part = slice(g * 128, (g + 1) * 128)
        wide_part = slice(g * 256, (g + 1) * 256)
        probs = []
        for w in range(windows):
            here = slice(w * 64, (w + 1) * 64)
            wide = jnp.concatenate([keys[here, part] * m for m in masks], axis=0)
            score = lax.dot_general(
                queries[here, part], wide, (((1,), (1,)), ((), ())), preferred_element_type=F32
            )
            probs.append(jnp.exp2(score + offs_scr[:, wide_part]))
        prob = jnp.concatenate(probs, axis=0)
        total = halves_dot(prob.astype(BF16), adder)
        weight = (prob / total).astype(BF16)
        mixed = []
        for w in range(windows):
            here = slice(w * 64, (w + 1) * 64)
            wide = jnp.concatenate([values[here, part] * m for m in masks], axis=0)
            mixed.append(dot(weight[here], wide).astype(BF16))
        sides.append(jnp.concatenate(mixed, axis=0))
    mixture = jnp.concatenate(sides, axis=-1)
    attended = (rows + halves_dot(mixture, leave_ref[...])).astype(BF16).astype(F32)
    second = layer_norm(attended, gains_ref[1:2, :])
    inner = widen_ref.shape[1]
    hidden = jnp.concatenate(
        [
            twice_gelu(halves_dot(second, widen_ref[:, cut : cut + 256]).astype(BF16))
            for cut in range(0, inner, 256)
        ],
        axis=-1,
    )
    return attended + 0.5 * halves_dot(hidden, shrink_ref[...])


def conv_block_kernel(
    flags_ref,
    x_ref,
    above_ref,
    below_ref,
    sides_ref,
    scale_ref,
    shift_ref,
    expand_ref,
    expand_bias_ref,
    depth_ref,
    depth_bias_ref,
    project_ref,
    gains_ref,
    entry_ref,
    leave_ref,
    offsets_ref,
    widen_ref,
    shrink_ref,
    out_ref,
    x_scr,
    wide_scr,
    prod_scr,
    offs_scr,
):
    step = pl.program_id(0)
    steps = pl.num_programs(0)
    tokens = STRIP * 64
    inner = expand_ref.shape[1]

    @pl.when(step == 0)
    def _():
        body = x_ref.shape[0]
        x_scr[0:64, :] = above_ref[...]
        x_scr[64 : 64 + body, :] = x_ref[...]
        x_scr[64 + body : 128 + body, :] = below_ref[...]
        prepare_offsets(offsets_ref, offs_scr)

    ext = STRIP + 2
    start = pl.multiple_of(step * tokens, tokens)
    store_halves(
        wide_scr, slice(0, ext * 64), x_scr[pl.ds(start, ext * 64), :].astype(F32)
    )
    where_in = lax.broadcasted_iota(jnp.int32, (ext, 8, 256), 1)
    scale = scale_ref[...][None]
    shift = shift_ref[...][None]

    def paired(cells):
        both = jnp.stack([cells[:10], cells[8:18]], axis=1)
        return (both * scale[None] + shift[None]).reshape(160, 256).astype(BF16)

    def side(which):
        rows = sides_ref[which, pl.ds(pl.multiple_of(step * STRIP, 8), 24), :]
        return jnp.broadcast_to(rows[:ext, None, :], (ext, 8, 256))

    slots = [None] * 10
    for low in range(8):
        cells = load_halves(wide_scr, pl.ds(low, ext * 8, stride=8))
        slots[low + 1] = paired(cells.reshape(ext, 8, 256))
        if low == 7:
            rolled = pltpu.roll(cells, 1, 0).reshape(ext, 8, 256)
            slots[0] = paired(jnp.where(where_in == 0, side(0), rolled))
        if low == 0:
            rolled = pltpu.roll(cells, ext * 8 - 1, 0).reshape(ext, 8, 256)
            slots[9] = paired(jnp.where(where_in == 7, side(1), rolled))

    sub = lax.broadcasted_iota(jnp.int32, (16, 256), 0)

    def keep(condition, flag):
        return jnp.where(condition, flag, 1.0).astype(BF16)

    top = keep(sub < 8, jnp.where(step == 0, flags_ref[0], 1.0))
    bottom = keep(sub >= 8, jnp.where(step == steps - 1, flags_ref[1], 1.0))
    at_left = keep(sub % 8 == 0, flags_ref[2])
    at_right = keep(sub % 8 == 7, flags_ref[3])

    product = [None] * 8
    for cut in range(0, inner, 256):
        here = slice(cut, cut + 256)
        bias = expand_bias_ref[:, here]
        cells = []
        for slot in range(10):
            one = twice_gelu((dot(slots[slot], expand_ref[:, here]) + bias).astype(BF16))
            one = one.reshape(10, 16, 256)
            one = jnp.concatenate([one[:1] * top[None], one[1:9], one[9:] * bottom[None]], axis=0)
            if slot == 0:
                one = one * at_left[None]
            if slot == 9:
                one = one * at_right[None]
            cells.append(one)
        taps = (0.5 * depth_ref[:, here]).astype(BF16)
        depth_bias = depth_bias_ref[:, here].astype(BF16)
        for low in range(8):
            total = depth_bias[None]
            for s in range(3):
                for t in range(3):
                    tap = taps[3 * s + t : 3 * s + t + 1][None]
                    total = total + cells[low + t][s : s + 8] * tap
            part = dot(twice_gelu(total).reshape(128, 256), project_ref[here, :])
            product[low] = part if product[low] is None else product[low] + part
    for low in range(8):
        store_halves(prod_scr, slice(low * 128, (low + 1) * 128), product[low])
    pieces = []
    for w in range(16):
        for y in range(8):
            pieces.append(load_halves(prod_scr, pl.ds(y * 16 + w, 8, stride=128)))
    source = x_scr[pl.ds(pl.multiple_of(start + 64, 64), tokens), :].astype(F32)
    source = source.reshape(2, 8, 8, 8, 256).swapaxes(1, 2).reshape(tokens, 256)
    rows = (source + 0.5 * jnp.concatenate(pieces, axis=0)).astype(BF16).astype(F32)
    done = attend_rows(
        rows, gains_ref, entry_ref, leave_ref, widen_ref, shrink_ref, offs_scr
    )
    done = done.reshape(2, 8, 8, 8, 256).swapaxes(1, 2).reshape(tokens, 256)
    out_ref[...] = done.astype(BF16)


def grid_kernel(
    x_ref,
    gains_ref,
    entry_ref,
    leave_ref,
    offsets_ref,
    widen_ref,
    shrink_ref,
    out_ref,
    in_scr,
    back_scr,
    offs_scr,
):
    @pl.when(pl.program_id(0) == 0)
    def _():
        prepare_offsets(offsets_ref, offs_scr)

    count = x_ref.shape[1]
    tokens = count * 64
    store_halves(in_scr, slice(0, tokens), x_ref[...].astype(F32).reshape(tokens, 256))
    rows = jnp.concatenate(
        [load_halves(in_scr, pl.ds(w, 64, stride=count)) for w in range(count)], axis=0
    )
    done = attend_rows(
        rows, gains_ref, entry_ref, leave_ref, widen_ref, shrink_ref, offs_scr
    )
    for w in range(count):
        store_halves(back_scr, pl.ds(w, 64, stride=count), done[w * 64 : (w + 1) * 64])
    out_ref[...] = load_halves(back_scr, slice(0, tokens)).reshape(64, count, 256).astype(BF16)


def attend_scratch():
    return [pltpu.VMEM((64, 512), F32)]


def whole(shape):
    return pl.BlockSpec(shape, lambda i: (0,) * len(shape))


def conv_block(flags, x, part, parts, above, below, sides, weights):
    tokens, channels = x.shape
    body = tokens // parts
    steps = body // (STRIP * 64)

    def border(rows, index):
        if rows.shape[0] == 64:
            return whole((64, channels))
        return pl.BlockSpec((64, channels), lambda i: (index, 0))

    return pl.pallas_call(
        conv_block_kernel,
        grid=(steps,),
        in_specs=[
            pl.BlockSpec(memory_space=pltpu.SMEM),
            pl.BlockSpec((body, channels), lambda i: (part, 0)),
            border(above, part * (body // 64) - 1),
            border(below, (part + 1) * (body // 64)),
            whole(sides.shape),
        ]
        + [whole(w.shape) for w in weights],
        out_specs=pl.BlockSpec((STRIP * 64, channels), lambda i: (i, 0)),
        out_shape=jax.ShapeDtypeStruct((body, channels), BF16),
        scratch_shapes=[
            pltpu.VMEM((body + 128, channels), BF16),
            pltpu.VMEM((2, (STRIP + 2) * 64, 128), F32),
            pltpu.VMEM((2, STRIP * 64, 128), F32),
            pltpu.VMEM((64, 512), F32),
        ],
        compiler_params=pltpu.CompilerParams(vmem_limit_bytes=56 << 20),
        cost_estimate=pl.CostEstimate(
            flops=body * 2600000, bytes_accessed=body * 1024 + 4000000, transcendentals=0
        ),
        name="conv_block",
    )(flags, x, above, below, sides, *weights)


def grid_attend(x, weights):
    sources, count, channels = x.shape
    block = pl.BlockSpec((sources, GRID_WINDOWS, channels), lambda i: (0, i, 0))
    tokens = sources * GRID_WINDOWS
    return pl.pallas_call(
        grid_kernel,
        grid=(count // GRID_WINDOWS,),
        in_specs=[block] + [whole(w.shape) for w in weights],
        out_specs=block,
        out_shape=jax.ShapeDtypeStruct(x.shape, BF16),
        scratch_shapes=[
            pltpu.VMEM((2, tokens, 128), F32),
            pltpu.VMEM((2, tokens, 128), F32),
            pltpu.VMEM((64, 512), F32),
        ],
        compiler_params=pltpu.CompilerParams(vmem_limit_bytes=56 << 20),
        cost_estimate=pl.CostEstimate(
            flops=sources * count * 1600000,
            bytes_accessed=sources * count * 1024 + 4000000,
            transcendentals=0,
        ),
        name="grid_attend",
    )(x, *weights)


ROW = ("row_hi", "core")
GROUP = ("row_hi", "col")


def shards(
    radar_tiles,
    conv_scale,
    conv_shift,
    expand_weight,
    expand_bias,
    depth_kernel,
    depth_bias,
    project_weight,
    block_gains,
    block_entry,
    block_leave,
    block_offsets,
    block_widen,
    block_shrink,
    grid_gains,
    grid_entry,
    grid_leave,
    grid_offsets,
    grid_widen,
    grid_shrink,
    parts=2,
):
    rows_here, cols_here, channels = radar_tiles.shape
    row_count, col_count = lax.axis_size(ROW), lax.axis_size("col")
    row, col = lax.axis_index(ROW), lax.axis_index("col")

    def shifted(values, axis, count, step):
        pairs = [(i, i + step) for i in range(count) if 0 <= i + step < count]
        return lax.ppermute(values, axis, pairs)

    above = shifted(radar_tiles[-1:], ROW, row_count, 1)
    below = shifted(radar_tiles[:1], ROW, row_count, -1)
    edges = [
        jnp.concatenate([above[:, e], radar_tiles[:, e], below[:, e]], axis=0) for e in (-1, 0)
    ]
    left = shifted(edges[0], "col", col_count, 1)
    right = shifted(edges[1], "col", col_count, -1)
    sides = jnp.stack([left, right]).astype(F32)
    x = radar_tiles.reshape(rows_here * cols_here, channels)
    above = above.reshape(cols_here, channels)
    below = below.reshape(cols_here, channels)
    weights = (
        conv_scale.reshape(1, -1),
        conv_shift.reshape(1, -1),
        expand_weight,
        expand_bias.reshape(1, -1),
        depth_kernel.reshape(9, -1),
        depth_bias.reshape(1, -1),
        project_weight,
        block_gains,
        block_entry,
        block_leave,
        block_offsets,
        block_widen,
        block_shrink,
    )
    grid_weights = (grid_gains, grid_entry, grid_leave, grid_offsets, grid_widen, grid_shrink)
    group = row_count // 2 * col_count
    span = rows_here // parts
    outs = []
    for part in range(parts):
        start = part * span
        flags = jnp.stack(
            [
                jnp.where(row > 0, 1.0, 0.0) if part == 0 else jnp.float32(1.0),
                jnp.where(row < row_count - 1, 1.0, 0.0) if part == parts - 1 else jnp.float32(1.0),
                jnp.where(col > 0, 1.0, 0.0),
                jnp.where(col < col_count - 1, 1.0, 0.0),
            ]
        ).astype(F32)
        mine = conv_block(
            flags,
            x,
            part,
            parts,
            above if part == 0 else x,
            below if part == parts - 1 else x,
            jnp.pad(sides[:, start : start + span + 2], ((0, 0), (0, 6), (0, 0))),
            weights,
        )
        outgoing = mine.reshape(group, -1, channels)
        outs.append(lax.all_to_all(outgoing, GROUP, split_axis=0, concat_axis=0, tiled=True))
    finished = []
    for arrived in outs:
        spread = grid_attend(arrived, grid_weights)
        finished.append(lax.all_to_all(spread, GROUP, split_axis=0, concat_axis=0, tiled=True))
    return jnp.concatenate(
        [f.reshape(span, cols_here, channels) for f in finished], axis=0
    )


def solution(mesh):
    inner = Mesh(mesh.devices.reshape(8, 2, 8), ("row_hi", "core", "col"))
    tiles = P(ROW, "col", None)
    return jax.shard_map(
        shards,
        mesh=inner,
        in_specs=(tiles,) + (P(),) * 19,
        out_specs=tiles,
        check_vma=False,
    )
```

time: 178 us -> 148 us (0.83)
  Pallas kernels: 92.1 us -> 60.5 us
  waiting for transfers between devices: 10.7 us -> 15.8 us
    pallas_call x2, Pallas kernels: 64.1 us -> 38.1 us  [conv_block(): pl.pallas_call(conv_block_kernel, grid=(steps,), in_specs=[pl.BlockSpec(m...]
    pallas_call x2, Pallas kernels: 28 us -> 22.4 us  [grid_attend(): pl.pallas_call(grid_kernel, grid=(count // GRID_WINDOWS,), in_specs=[bloc...]
    all_to_all x2, waiting for transfers between devices: 4.35 us -> 7.12 us  [shards(): lax.all_to_all(outgoing, GROUP, split_axis=0, concat_axis=0, tiled=True)]
    all_to_all x1, waiting for transfers between devices: 3.91 us -> 6.25 us  [shards(): lax.all_to_all(spread, GROUP, split_axis=0, concat_axis=0, tiled=True)]
  transfers between devices with their start and end apart: 7 -> 7, of which waited for: 3 -> 3; matrix products, arithmetic and copies ran while one was open for 3% -> 3% of each run, Pallas kernels for 34% -> 28%
where the time goes in v2:
time: 148 us; the launch traced here: 147 us
  Pallas kernels  60.5 us (41%)
  starting transfers between devices  41 us (28%)
  blocking collectives  22.3 us (15%)
  waiting for transfers between devices  15.8 us (11%)
  local copies, waits for them, and re-layouts  4.07 us (3%)
  other arithmetic  3.5 us (2%)
    pallas_call x2, Pallas kernels, conv_block(): pl.pallas_call(conv_block_kernel, grid=(steps,), in_specs=[pl.BlockSpec(m...  38.1 us
    all_to_all x2, starting transfers between devices, shards(): lax.all_to_all(outgoing, GROUP, split_axis=0, concat_axis=0, tiled=True)  27.6 us
    pallas_call x2, Pallas kernels, grid_attend(): pl.pallas_call(grid_kernel, grid=(count // GRID_WINDOWS,), in_specs=[bloc...  22.4 us
    all_to_all x1, blocking collectives, shards(): lax.all_to_all(spread, GROUP, split_axis=0, concat_axis=0, tiled=True)  22.3 us
    ppermute x4, starting transfers between devices, shifted(): return lax.ppermute(values, axis, pairs)  8.41 us
    all_to_all x2, waiting for transfers between devices, shards(): lax.all_to_all(outgoing, GROUP, split_axis=0, concat_axis=0, tiled=True)  7.12 us
    all_to_all x1, waiting for transfers between devices, shards(): lax.all_to_all(spread, GROUP, split_axis=0, concat_axis=0, tiled=True)  6.25 us
    all_to_all x1, starting transfers between devices, shards(): lax.all_to_all(spread, GROUP, split_axis=0, concat_axis=0, tiled=True)  4.99 us
  transfers between devices with their start and end apart: 7, of which 3 were waited for; matrix products, arithmetic and copies ran while one was open for 3% of the time, Pallas kernels for 28%

profile of v2, /device:TPU:0, one launch (start us, length us, event | category | flops | bytes accessed | tf_op | source)
XLA Modules:
  0.0 147.4 jit_solution(15493539800992047816)
XLA Ops:
  0.0 0.8 fusion.1
  0.8 1.3 collective-permute-start
  2.1 1.3 collective-permute-start.1
  3.4 1.1 fusion
  4.6 0.0 collective-permute-done
  4.6 0.0 copy-start.3
  4.6 2.5 %collective-permute-done.1 = bf16[1,64,256]{2,1,0:T(8,128)(2,1)S(1)} collective-permute-done((bf16[1,64,256]{2,1,0:T(8,128)(2,1)S(1)}, bf16[1,64,256]{2,1,0:T(8,128)(2,1)S(1)}, u32[]{:S(2)}, u32[]{:S(2)}) %collective-permute-start.1) | collective-permute-done | bytes 32800 | tf_op jit(solution)/shard_map/ppermute | solution.py:360
  7.1 1.3 collective-permute-start.3
  8.4 4.5 %collective-permute-start.2 = (bf16[66,256]{1,0:T(8,128)(2,1)S(1)}, bf16[66,256]{1,0:T(8,128)(2,1)S(1)}, u32[]{:S(2)}, u32[]{:S(2)}) collective-permute-start(bf16[66,256]{1,0:T(8,128)(2,1)S(1)} %pad_maximum_fusion.1), channel_id=1, source_target_pairs={{0,1},{1,2},{2,3},{3,4},{4,5},{5,6},{6,7},{8,9},{9,10},{10,11},{11... | collective-permute-start | bytes 101384 | tf_op jit(solution)/shard_map/ppermute | solution.py:360
  13.0 0.7 maximum_maximum_fusion.1.flags_ref
  13.6 1.4 reshape.41.depth_ref
  15.1 0.0 collective-permute-done.3
  15.1 0.0 collective-permute-done.2
  15.1 0.7 pad.8.sides_ref
  15.8 19.1 %conv_block.3 = bf16[2048,256]{1,0:T(8,128)(2,1)} custom-call(f32[4]{0:T(128)} %maximum_maximum_fusion.1.flags_ref, bf16[4096,256]{1,0:T(8,128)(2,1)} %bitcast.39, bf16[4096,256]{1,0:T(8,128)(2,1)} %bitcast.40, bf16[64,256]{1,0:T(8,128)(2,1)} %bitcast.44, f32[2,40,256]{2,1,0:T(8,128)} %pad.8.sides_ref, f32[1,256]{1,0:T(1,128)} %bitcast.49, ...), custom_call_target="tpu_custom_call" | custom-call | flops 5324800000 | bytes 6097152 | tf_op jit(solution)/shard_map/conv_block/pallas_call | solution.py:275
  34.8 0.0 copy-start.2
  34.8 17.2 %all-to-all-start.2 = ((bf16[64,32,256]{2,1,0:T(8,128)(2,1)}), bf16[64,32,256]{2,1,0:T(8,128)(2,1)S(1)}, u32[]{:S(2)}, u32[]{:S(2)}) async-start(bf16[64,32,256]{2,1,0:T(8,128)(2,1)} %bitcast.33), calls=%async_computation.2 | async-start | bytes 2097152 | tf_op jit(solution)/shard_map/all_to_all | solution.py:413
  52.1 0.6 maximum_maximum_fusion.flags_ref
  52.7 0.0 copy-done.2
  52.7 0.7 slice_select_fusion.sides_ref
  53.4 19.0 %conv_block.2 = bf16[2048,256]{1,0:T(8,128)(2,1)} custom-call(f32[4]{0:T(128)} %maximum_maximum_fusion.flags_ref, bf16[4096,256]{1,0:T(8,128)(2,1)} %bitcast.41, bf16[64,256]{1,0:T(8,128)(2,1)} %bitcast.43, bf16[4096,256]{1,0:T(8,128)(2,1)} %bitcast.42, f32[2,40,256]{2,1,0:T(8,128)} %slice_select_fusion.sides_ref, f32[1,256]{1,0:T(1,128)} %bitcast.50, ...), custom_call_target="tpu_custom_call" | custom-call | flops 5324800000 | bytes 6097152 | tf_op jit(solution)/shard_map/conv_block/pallas_call | solution.py:275
  72.4 0.0 all-to-all-done.2.x_ref
  72.4 0.0 copy-start
  72.4 10.4 %all-to-all-start = ((bf16[64,32,256]{2,1,0:T(8,128)(2,1)}), bf16[64,32,256]{2,1,0:T(8,128)(2,1)S(1)}, u32[]{:S(2)}, u32[]{:S(2)}) async-start(bf16[64,32,256]{2,1,0:T(8,128)(2,1)} %bitcast.34), calls=%async_computation | async-start | bytes 2097152 | tf_op jit(solution)/shard_map/all_to_all | solution.py:413
  82.8 11.2 %grid_attend.3 = bf16[64,32,256]{2,1,0:T(8,128)(2,1)} custom-call(bf16[64,32,256]{2,1,0:T(8,128)(2,1)} %copy-done, f32[2,256]{1,0:T(2,128)} %gains_ref.7, bf16[256,768]{1,0:T(8,128)(2,1)} %entry_ref.7, bf16[256,256]{1,0:T(8,128)(2,1)} %leave_ref.7, f32[8,64,64]{2,1,0:T(8,128)} %offsets_ref.7, bf16[256,1024]{1,0:T(8,128)(2,1)} %widen_ref.7, ...), custom_call_target="tpu_custom_call" | custom-call | flops 3276800000 | bytes 6097152 | tf_op jit(solution)/shard_map/grid_attend/pallas_call | solution.py:306
  94.0 7.1 %all-to-all-done.x_ref = bf16[64,32,256]{2,1,0:T(8,128)(2,1)S(1)} async-done(((bf16[64,32,256]{2,1,0:T(8,128)(2,1)}), bf16[64,32,256]{2,1,0:T(8,128)(2,1)S(1)}, u32[]{:S(2)}, u32[]{:S(2)}) %all-to-all-start) | async-done | bytes 1048608 | tf_op jit(solution)/shard_map/all_to_all | solution.py:413
  101.1 5.0 %all-to-all-start.3 = ((bf16[64,32,256]{2,1,0:T(8,128)(2,1)}), bf16[64,32,256]{2,1,0:T(8,128)(2,1)S(1)}, u32[]{:S(2)}, u32[]{:S(2)}) async-start(bf16[64,32,256]{2,1,0:T(8,128)(2,1)} %grid_attend.3), calls=%async_computation.3 | async-start | bytes 2097152 | tf_op jit(solution)/shard_map/all_to_all | solution.py:417
  106.1 0.0 copy-done.1
  106.1 11.2 %grid_attend.2 = bf16[64,32,256]{2,1,0:T(8,128)(2,1)} custom-call(bf16[64,32,256]{2,1,0:T(8,128)(2,1)} %copy-done.1, f32[2,256]{1,0:T(2,128)} %gains_ref.7, bf16[256,768]{1,0:T(8,128)(2,1)} %entry_ref.7, bf16[256,256]{1,0:T(8,128)(2,1)} %leave_ref.7, f32[8,64,64]{2,1,0:T(8,128)} %offsets_ref.7, bf16[256,1024]{1,0:T(8,128)(2,1)} %widen_ref.7, ...), custom_call_target="tpu_custom_call" | custom-call | flops 3276800000 | bytes 6097152 | tf_op jit(solution)/shard_map/grid_attend/pallas_call | solution.py:306
  117.3 6.3 %all-to-all-done.3 = bf16[64,32,256]{2,1,0:T(8,128)(2,1)S(1)} async-done(((bf16[64,32,256]{2,1,0:T(8,128)(2,1)}), bf16[64,32,256]{2,1,0:T(8,128)(2,1)S(1)}, u32[]{:S(2)}, u32[]{:S(2)}) %all-to-all-start.3) | async-done | bytes 1048608 | tf_op jit(solution)/shard_map/all_to_all | solution.py:417
  123.6 22.3 %all_to_all.20 = bf16[64,32,256]{2,1,0:T(8,128)(2,1)S(1)} all-to-all(bf16[64,32,256]{2,1,0:T(8,128)(2,1)} %grid_attend.2), channel_id=1, replica_groups=mesh['row_hi'=8,'core'=2,'col'=8] {'row_hi','col'}, dimensions={0} | all-to-all | bytes 2097152 | tf_op jit(solution)/shard_map/all_to_all | solution.py:417
  145.9 1.5 %pad_maximum_fusion = bf16[64,64,256]{2,1,0:T(8,128)(2,1)} fusion(bf16[32,64,256]{2,1,0:T(8,128)(2,1)S(1)} %bitcast.31, bf16[32,64,256]{2,1,0:T(8,128)(2,1)S(1)} %bitcast.32), kind=kLoop, calls=%fused_computation | loop fusion | flops 1048576 | bytes 4194304 | tf_op jit(solution)/shard_map/concatenate | solution.py:418
  (13 shorter events, 0.1 us)
Async XLA Ops:
  0.8 3.8 %collective-permute-start = (bf16[1,64,256]{2,1,0:T(8,128)(2,1)S(1)}, bf16[1,64,256]{2,1,0:T(8,128)(2,1)S(1)}, u32[]{:S(2)}, u32[]{:S(2)}) collective-permute-start(bf16[1,64,256]{2,1,0:T(8,128)(2,1)S(1)} %get-tuple-element.7), channel_id=1, source_target_pairs={{0,8},{8,16},{16,24},{24,32},{32,40},{40,48},{48,56},{56,64},{64,7... | collective-permute-start | bytes 98312 | tf_op jit(solution)/shard_map/ppermute | solution.py:360
  2.1 5.0 %collective-permute-start.1 = (bf16[1,64,256]{2,1,0:T(8,128)(2,1)S(1)}, bf16[1,64,256]{2,1,0:T(8,128)(2,1)S(1)}, u32[]{:S(2)}, u32[]{:S(2)}) collective-permute-start(bf16[1,64,256]{2,1,0:T(8,128)(2,1)S(1)} %get-tuple-element.8), channel_id=1, source_target_pairs={{8,0},{16,8},{24,16},{32,24},{40,32},{48,40},{56,48},{64,56},{72,6... | collective-permute-start | bytes 98312 | tf_op jit(solution)/shard_map/ppermute | solution.py:360
  4.6 30.3 %copy-start.3 = (bf16[1,64,256]{2,1,0:T(8,128)(2,1)}, bf16[1,64,256]{2,1,0:T(8,128)(2,1)S(1)}, u32[]{:S(2)}) copy-start(bf16[1,64,256]{2,1,0:T(8,128)(2,1)S(1)} %collective-permute-done) | copy-start | bytes 98308
  7.1 8.7 %copy-start.4 = (bf16[1,64,256]{2,1,0:T(8,128)(2,1)}, bf16[1,64,256]{2,1,0:T(8,128)(2,1)S(1)}, u32[]{:S(2)}) copy-start(bf16[1,64,256]{2,1,0:T(8,128)(2,1)S(1)} %collective-permute-done.1) | copy-start | bytes 98308
  7.1 8.0 %collective-permute-start.3 = (bf16[66,256]{1,0:T(8,128)(2,1)S(1)}, bf16[66,256]{1,0:T(8,128)(2,1)S(1)}, u32[]{:S(2)}, u32[]{:S(2)}) collective-permute-start(bf16[66,256]{1,0:T(8,128)(2,1)S(1)} %pad_maximum_fusion.2), channel_id=1, source_target_pairs={{1,0},{2,1},{3,2},{4,3},{5,4},{6,5},{7,6},{9,8},{10,9},{11,10},{12... | collective-permute-start | bytes 101384 | tf_op jit(solution)/shard_map/ppermute | solution.py:360
  8.4 6.7 %collective-permute-start.2 = (bf16[66,256]{1,0:T(8,128)(2,1)S(1)}, bf16[66,256]{1,0:T(8,128)(2,1)S(1)}, u32[]{:S(2)}, u32[]{:S(2)}) collective-permute-start(bf16[66,256]{1,0:T(8,128)(2,1)S(1)} %pad_maximum_fusion.1), channel_id=1, source_target_pairs={{0,1},{1,2},{2,3},{3,4},{4,5},{5,6},{6,7},{8,9},{9,10},{10,11},{11... | collective-permute-start | bytes 101384 | tf_op jit(solution)/shard_map/ppermute | solution.py:360
  34.8 17.8 %copy-start.2 = (pred[40]{0:T(512)(128)(4,1)S(1)}, pred[40]{0:T(512)(128)(4,1)}, u32[]{:S(2)}) copy-start(pred[40]{0:T(512)(128)(4,1)} %constant.28.clone.1) | copy-start | bytes 124
  34.8 37.5 %all-to-all-start.2 = ((bf16[64,32,256]{2,1,0:T(8,128)(2,1)}), bf16[64,32,256]{2,1,0:T(8,128)(2,1)S(1)}, u32[]{:S(2)}, u32[]{:S(2)}) async-start(bf16[64,32,256]{2,1,0:T(8,128)(2,1)} %bitcast.33), calls=%async_computation.2 | async-start | bytes 2097152 | tf_op jit(solution)/shard_map/all_to_all | solution.py:413
  72.4 10.4 %copy-start = (bf16[64,32,256]{2,1,0:T(8,128)(2,1)}, bf16[64,32,256]{2,1,0:T(8,128)(2,1)S(1)}, u32[]{:S(2)}) copy-start(bf16[64,32,256]{2,1,0:T(8,128)(2,1)S(1)} %all-to-all-done.2.x_ref) | copy-start | bytes 3145732
  72.4 28.7 %all-to-all-start = ((bf16[64,32,256]{2,1,0:T(8,128)(2,1)}), bf16[64,32,256]{2,1,0:T(8,128)(2,1)S(1)}, u32[]{:S(2)}, u32[]{:S(2)}) async-start(bf16[64,32,256]{2,1,0:T(8,128)(2,1)} %bitcast.34), calls=%async_computation | async-start | bytes 2097152 | tf_op jit(solution)/shard_map/all_to_all | solution.py:413
  101.1 5.0 %copy-start.1 = (bf16[64,32,256]{2,1,0:T(8,128)(2,1)}, bf16[64,32,256]{2,1,0:T(8,128)(2,1)S(1)}, u32[]{:S(2)}) copy-start(bf16[64,32,256]{2,1,0:T(8,128)(2,1)S(1)} %all-to-all-done.x_ref) | copy-start | bytes 3145732
  101.1 22.5 %all-to-all-start.3 = ((bf16[64,32,256]{2,1,0:T(8,128)(2,1)}), bf16[64,32,256]{2,1,0:T(8,128)(2,1)S(1)}, u32[]{:S(2)}, u32[]{:S(2)}) async-start(bf16[64,32,256]{2,1,0:T(8,128)(2,1)} %grid_attend.3), calls=%async_computation.3 | async-start | bytes 2097152 | tf_op jit(solution)/shard_map/all_to_all | solution.py:417

commit v3 on v2

--- a/solution.py
+++ b/solution.py
@@ -19,8 +19,13 @@
 LOG2E = math.log2(math.e)
 
 
-def twice_gelu(v):
-    return v + v * jnp.tanh(v * (GELU_A + GELU_B * (v * v)))
+GELU_S = GELU_B ** (1.0 / 3.0)
+GELU_C = GELU_A / GELU_S
+GELU_BACK = 0.5 / GELU_S
+
+
+def scaled_gelu(z):
+    return z + z * jnp.tanh(z * (z * z + GELU_C))
 
 
 def dot(a, b):
@@ -95,43 +100,44 @@
         sides.append(jnp.concatenate(mixed, axis=0))
     mixture = jnp.concatenate(sides, axis=-1)
     attended = (rows + halves_dot(mixture, leave_ref[...])).astype(BF16).astype(F32)
-    second = layer_norm(attended, gains_ref[1:2, :])
+    second = layer_norm(attended, GELU_S * gains_ref[1:2, :])
     inner = widen_ref.shape[1]
     hidden = jnp.concatenate(
         [
-            twice_gelu(halves_dot(second, widen_ref[:, cut : cut + 256]).astype(BF16))
+            scaled_gelu(halves_dot(second, widen_ref[:, cut : cut + 256]).astype(BF16))
             for cut in range(0, inner, 256)
         ],
         axis=-1,
     )
-    return attended + 0.5 * halves_dot(hidden, shrink_ref[...])
-
-
-def conv_block_kernel(
-    flags_ref,
-    x_ref,
-    above_ref,
-    below_ref,
-    sides_ref,
-    scale_ref,
-    shift_ref,
-    expand_ref,
-    expand_bias_ref,
-    depth_ref,
-    depth_bias_ref,
-    project_ref,
-    gains_ref,
-    entry_ref,
-    leave_ref,
-    offsets_ref,
-    widen_ref,
-    shrink_ref,
-    out_ref,
-    x_scr,
-    wide_scr,
-    prod_scr,
-    offs_scr,
-):
+    return attended + GELU_BACK * halves_dot(hidden, shrink_ref[...])
+
+
+def conv_block_kernel(edge, x_ref, above_ref, below_ref, *refs):
+    if edge:
+        halo_above_ref, halo_below_ref = refs[:2]
+        refs = refs[2:]
+    (
+        left_ref,
+        right_ref,
+        scale_ref,
+        shift_ref,
+        expand_ref,
+        expand_bias_ref,
+        depth_ref,
+        depth_bias_ref,
+        project_ref,
+        gains_ref,
+        entry_ref,
+        leave_ref,
+        offsets_ref,
+        widen_ref,
+        shrink_ref,
+        out_ref,
+        wide_scr,
+        side_scr,
+        prod_scr,
+        offs_scr,
+    ) = refs
     step = pl.program_id(0)
     steps = pl.num_programs(0)
     tokens = STRIP * 64
@@ -139,27 +145,34 @@
 
     @pl.when(step == 0)
     def _():
-        body = x_ref.shape[0]
-        x_scr[0:64, :] = above_ref[...]
-        x_scr[64 : 64 + body, :] = x_ref[...]
-        x_scr[64 + body : 128 + body, :] = below_ref[...]
         prepare_offsets(offsets_ref, offs_scr)
+        for which, ref in enumerate((left_ref, right_ref)):
+            side = ref[...].astype(F32)
+            first = 0 if edge else STRIP
+            second = side.shape[0] - STRIP - 2 - first
+            side_scr[which, 0:18, :] = side[first : first + 18]
+            side_scr[which, 24:42, :] = side[second : second + 18]
+
+    above = above_ref[...].astype(F32)
+    below = below_ref[...].astype(F32)
+    if edge:
+        above = jnp.where(step == 0, halo_above_ref[...].astype(F32), above)
+        below = jnp.where(step == steps - 1, halo_below_ref[...].astype(F32), below)
 
     ext = STRIP + 2
-    start = pl.multiple_of(step * tokens, tokens)
-    store_halves(
-        wide_scr, slice(0, ext * 64), x_scr[pl.ds(start, ext * 64), :].astype(F32)
-    )
+    store_halves(wide_scr, slice(0, 64), above)
+    store_halves(wide_scr, slice(64, 64 + tokens), x_ref[...].astype(F32))
+    store_halves(wide_scr, slice(64 + tokens, 128 + tokens), below)
     where_in = lax.broadcasted_iota(jnp.int32, (ext, 8, 256), 1)
-    scale = scale_ref[...][None]
-    shift = shift_ref[...][None]
+    scale = (GELU_S * scale_ref[...])[None]
+    shift = (GELU_S * shift_ref[...])[None]
 
     def paired(cells):
         both = jnp.stack([cells[:10], cells[8:18]], axis=1)
         return (both * scale[None] + shift[None]).reshape(160, 256).astype(BF16)
 
     def side(which):
-        rows = sides_ref[which, pl.ds(pl.multiple_of(step * STRIP, 8), 24), :]
+        rows = side_scr[which, pl.ds(pl.multiple_of(step * 24, 8), 24), :]
         return jnp.broadcast_to(rows[:ext, None, :], (ext, 8, 256))
 
     slots = [None] * 10
@@ -175,37 +188,44 @@
 
     sub = lax.broadcasted_iota(jnp.int32, (16, 256), 0)
 
-    def keep(condition, flag):
-        return jnp.where(condition, flag, 1.0).astype(BF16)
-
-    top = keep(sub < 8, jnp.where(step == 0, flags_ref[0], 1.0))
-    bottom = keep(sub >= 8, jnp.where(step == steps - 1, flags_ref[1], 1.0))
-    at_left = keep(sub % 8 == 0, flags_ref[2])
-    at_right = keep(sub % 8 == 7, flags_ref[3])
+    def keep(condition, outside):
+        value = jnp.where(outside, 0.0, 1.0)
+        return jnp.where(condition, value, 1.0).astype(BF16)
+
+    row, rows_of = lax.axis_index(ROW), lax.axis_size(ROW)
+    col, cols_of = lax.axis_index("col"), lax.axis_size("col")
+    if edge:
+        top = keep(sub < 8, jnp.logical_and(step == 0, row == 0))
+        bottom = keep(sub >= 8, jnp.logical_and(step == steps - 1, row == rows_of - 1))
+    at_left = keep(sub % 8 == 0, col == 0)
+    at_right = keep(sub % 8 == 7, col == cols_of - 1)
 
     product = [None] * 8
     for cut in range(0, inner, 256):
         here = slice(cut, cut + 256)
-        bias = expand_bias_ref[:, here]
+        bias = (GELU_S * expand_bias_ref[:, here]).astype(BF16)
         cells = []
         for slot in range(10):
-            one = twice_gelu((dot(slots[slot], expand_ref[:, here]) + bias).astype(BF16))
+            one = scaled_gelu(dot(slots[slot], expand_ref[:, here]).astype(BF16) + bias)
             one = one.reshape(10, 16, 256)
-            one = jnp.concatenate([one[:1] * top[None], one[1:9], one[9:] * bottom[None]], axis=0)
+            if edge:
+                one = jnp.concatenate(
+                    [one[:1] * top[None], one[1:9], one[9:] * bottom[None]], axis=0
+                )
             if slot == 0:
                 one = one * at_left[None]
             if slot == 9:
                 one = one * at_right[None]
             cells.append(one)
-        taps = (0.5 * depth_ref[:, here]).astype(BF16)
-        depth_bias = depth_bias_ref[:, here].astype(BF16)
+        taps = [(GELU_S * GELU_BACK * depth_ref[k][:, here]).astype(BF16) for k in range(3)]
+        depth_bias = (GELU_S * depth_bias_ref[:, here]).astype(BF16)
         for low in range(8):
             total = depth_bias[None]
             for s in range(3):
                 for t in range(3):
-                    tap = taps[3 * s + t : 3 * s + t + 1][None]
+                    tap = taps[s][t : t + 1][None]
                     total = total + cells[low + t][s : s + 8] * tap
-            part = dot(twice_gelu(total).reshape(128, 256), project_ref[here, :])
+            part = dot(scaled_gelu(total).reshape(128, 256), project_ref[here, :])
             product[low] = part if product[low] is None else product[low] + part
     for low in range(8):
         store_halves(prod_scr, slice(low * 128, (low + 1) * 128), product[low])
@@ -213,9 +233,9 @@
     for w in range(16):
         for y in range(8):
             pieces.append(load_halves(prod_scr, pl.ds(y * 16 + w, 8, stride=128)))
-    source = x_scr[pl.ds(pl.multiple_of(start + 64, 64), tokens), :].astype(F32)
+    source = x_ref[...].astype(F32)
     source = source.reshape(2, 8, 8, 8, 256).swapaxes(1, 2).reshape(tokens, 256)
-    rows = (source + 0.5 * jnp.concatenate(pieces, axis=0)).astype(BF16).astype(F32)
+    rows = (source + GELU_BACK * jnp.concatenate(pieces, axis=0)).astype(BF16).astype(F32)
     done = attend_rows(
         rows, gains_ref, entry_ref, leave_ref, widen_ref, shrink_ref, offs_scr
     )
@@ -262,41 +282,38 @@
     return pl.BlockSpec(shape, lambda i: (0,) * len(shape))
 
 
-def conv_block(flags, x, part, parts, above, below, sides, weights):
-    tokens, channels = x.shape
-    body = tokens // parts
-    steps = body // (STRIP * 64)
-
-    def border(rows, index):
-        if rows.shape[0] == 64:
-            return whole((64, channels))
-        return pl.BlockSpec((64, channels), lambda i: (index, 0))
-
+def conv_block(x, body, above, below, halos, left, right, weights):
+    channels = x.shape[1]
+    steps = 2
+    tokens = STRIP * 64
+    row = (64, channels)
     return pl.pallas_call(
-        conv_block_kernel,
+        functools.partial(conv_block_kernel, bool(halos)),
         grid=(steps,),
         in_specs=[
-            pl.BlockSpec(memory_space=pltpu.SMEM),
-            pl.BlockSpec((body, channels), lambda i: (part, 0)),
-            border(above, part * (body // 64) - 1),
-            border(below, (part + 1) * (body // 64)),
-            whole(sides.shape),
+            pl.BlockSpec((tokens, channels), lambda i: (body(i), 0)),
+            pl.BlockSpec(row, lambda i: (above(i), 0)),
+            pl.BlockSpec(row, lambda i: (below(i), 0)),
         ]
+        + [whole(h.shape) for h in halos]
+        + [whole(left.shape), whole(right.shape)]
         + [whole(w.shape) for w in weights],
-        out_specs=pl.BlockSpec((STRIP * 64, channels), lambda i: (i, 0)),
-        out_shape=jax.ShapeDtypeStruct((body, channels), BF16),
+        out_specs=pl.BlockSpec((tokens, channels), lambda i: (i, 0)),
+        out_shape=jax.ShapeDtypeStruct((steps * tokens, channels), BF16),
         scratch_shapes=[
-            pltpu.VMEM((body + 128, channels), BF16),
             pltpu.VMEM((2, (STRIP + 2) * 64, 128), F32),
-            pltpu.VMEM((2, STRIP * 64, 128), F32),
+            pltpu.VMEM((2, 48, channels), F32),
+            pltpu.VMEM((2, tokens, 128), F32),
             pltpu.VMEM((64, 512), F32),
         ],
         compiler_params=pltpu.CompilerParams(vmem_limit_bytes=56 << 20),
         cost_estimate=pl.CostEstimate(
-            flops=body * 2600000, bytes_accessed=body * 1024 + 4000000, transcendentals=0
+            flops=steps * tokens * 7000000,
+            bytes_accessed=steps * tokens * 1024 + 4000000,
+            transcendentals=0,
         ),
         name="conv_block",
-    )(flags, x, above, below, sides, *weights)
+    )(x, x, x, *halos, left, right, *weights)
 
 
 def grid_attend(x, weights):
@@ -316,7 +333,7 @@
         ],
         compiler_params=pltpu.CompilerParams(vmem_limit_bytes=56 << 20),
         cost_estimate=pl.CostEstimate(
-            flops=sources * count * 1600000,
+            flops=sources * count * 5000000,
             bytes_accessed=sources * count * 1024 + 4000000,
             transcendentals=0,
         ),
@@ -349,33 +366,29 @@
     grid_offsets,
     grid_widen,
     grid_shrink,
-    parts=2,
 ):
     rows_here, cols_here, channels = radar_tiles.shape
     row_count, col_count = lax.axis_size(ROW), lax.axis_size("col")
-    row, col = lax.axis_index(ROW), lax.axis_index("col")
 
     def shifted(values, axis, count, step):
         pairs = [(i, i + step) for i in range(count) if 0 <= i + step < count]
         return lax.ppermute(values, axis, pairs)
 
-    above = shifted(radar_tiles[-1:], ROW, row_count, 1)
-    below = shifted(radar_tiles[:1], ROW, row_count, -1)
+    x = radar_tiles.reshape(rows_here * cols_here, channels)
+    above = shifted(x[-cols_here:], ROW, row_count, 1)
+    below = shifted(x[:cols_here], ROW, row_count, -1)
     edges = [
-        jnp.concatenate([above[:, e], radar_tiles[:, e], below[:, e]], axis=0) for e in (-1, 0)
+        jnp.concatenate([above[e][None], radar_tiles[:, e], below[e][None]], axis=0)
+        for e in (-1, 0)
     ]
     left = shifted(edges[0], "col", col_count, 1)
     right = shifted(edges[1], "col", col_count, -1)
-    sides = jnp.stack([left, right]).astype(F32)
-    x = radar_tiles.reshape(rows_here * cols_here, channels)
-    above = above.reshape(cols_here, channels)
-    below = below.reshape(cols_here, channels)
     weights = (
         conv_scale.reshape(1, -1),
         conv_shift.reshape(1, -1),
         expand_weight,
         expand_bias.reshape(1, -1),
-        depth_kernel.reshape(9, -1),
+        depth_kernel,
         depth_bias.reshape(1, -1),
         project_weight,
         block_gains,
@@ -387,37 +400,37 @@
     )
     grid_weights = (grid_gains, grid_entry, grid_leave, grid_offsets, grid_widen, grid_shrink)
     group = row_count // 2 * col_count
-    span = rows_here // parts
-    outs = []
-    for part in range(parts):
-        start = part * span
-        flags = jnp.stack(
-            [
-                jnp.where(row > 0, 1.0, 0.0) if part == 0 else jnp.float32(1.0),
-                jnp.where(row < row_count - 1, 1.0, 0.0) if part == parts - 1 else jnp.float32(1.0),
-                jnp.where(col > 0, 1.0, 0.0),
-                jnp.where(col < col_count - 1, 1.0, 0.0),
-            ]
-        ).astype(F32)
-        mine = conv_block(
-            flags,
-            x,
-            part,
-            parts,
-            above if part == 0 else x,
-            below if part == parts - 1 else x,
-            jnp.pad(sides[:, start : start + span + 2], ((0, 0), (0, 6), (0, 0))),
-            weights,
-        )
-        outgoing = mine.reshape(group, -1, channels)
-        outs.append(lax.all_to_all(outgoing, GROUP, split_axis=0, concat_axis=0, tiled=True))
-    finished = []
-    for arrived in outs:
-        spread = grid_attend(arrived, grid_weights)
-        finished.append(lax.all_to_all(spread, GROUP, split_axis=0, concat_axis=0, tiled=True))
-    return jnp.concatenate(
-        [f.reshape(span, cols_here, channels) for f in finished], axis=0
-    )
+    blocks = rows_here // STRIP
+    inner = conv_block(
+        x,
+        lambda i: i + 1,
+        lambda i: STRIP * (i + 1) - 1,
+        lambda i: STRIP * (i + 2),
+        (),
+        left,
+        right,
+        weights,
+    )
+
+    def spread(values):
+        values = values.reshape(group, -1, channels)
+        return lax.all_to_all(values, GROUP, split_axis=0, concat_axis=0, tiled=True)
+
+    inner_there = spread(inner)
+    outer = conv_block(
+        x,
+        lambda i: (blocks - 1) * i,
+        lambda i: (rows_here - STRIP - 1) * i,
+        lambda i: STRIP + (rows_here - STRIP - 1) * i,
+        (above, below),
+        left,
+        right,
+        weights,
+    )
+    outer_there = spread(outer)
+    inner_back = spread(grid_attend(inner_there, grid_weights)).reshape(-1, cols_here, channels)
+    outer_back = spread(grid_attend(outer_there, grid_weights)).reshape(-1, cols_here, channels)
+    return jnp.concatenate([outer_back[:STRIP], inner_back, outer_back[STRIP:]], axis=0)
 
 
 def solution(mesh):

time: 148 us -> 142 us (0.959)
  blocking collectives: 22.3 us -> 0 us
  waiting for transfers between devices: 15.8 us -> 31.7 us
  starting transfers between devices: 41 us -> 46.4 us
  other arithmetic: 3.5 us -> 1.59 us
    all_to_all x1 -> x0, blocking collectives: 22.3 us -> none  [shards(): lax.all_to_all(spread, GROUP, split_axis=0, concat_axis=0, tiled=True)]
    all_to_all x3 -> x4, waiting for transfers between devices: 13.4 us -> 26.9 us  [spread(): lax.all_to_all(values, GROUP, split_axis=0, concat_axis=0, tiled=True)]
    all_to_all x3 -> x4, starting transfers between devices: 32.6 us -> 36.9 us  [spread(): lax.all_to_all(values, GROUP, split_axis=0, concat_axis=0, tiled=True)]
    ppermute x4, waiting for transfers between devices: 2.47 us -> 4.81 us  [shifted(): return lax.ppermute(values, axis, pairs)]
  transfers between devices with their start and end apart: 7 -> 8, of which waited for: 3 -> 5; matrix products, arithmetic and copies ran while one was open for 3% -> 1% of each run, Pallas kernels for 28% -> 29%
where the time goes in v3:
time: 142 us
  Pallas kernels  59.2 us (42%)
  starting transfers between devices  46.4 us (33%)
  waiting for transfers between devices  31.7 us (22%)
  local copies, waits for them, and re-layouts  2.64 us (2%)
  other arithmetic  1.59 us (1%)
    all_to_all x4, starting transfers between devices, spread(): lax.all_to_all(values, GROUP, split_axis=0, concat_axis=0, tiled=True)  36.9 us
    pallas_call x2, Pallas kernels, conv_block(): pl.pallas_call(functools.partial(conv_block_kernel, bool(halos)), grid=(s...  36.8 us
    all_to_all x4, waiting for transfers between devices, spread(): lax.all_to_all(values, GROUP, split_axis=0, concat_axis=0, tiled=True)  26.9 us
    pallas_call x2, Pallas kernels, grid_attend(): pl.pallas_call(grid_kernel, grid=(count // GRID_WINDOWS,), in_specs=[bloc...  22.5 us
    ppermute x4, starting transfers between devices, shifted(): return lax.ppermute(values, axis, pairs)  9.51 us
    ppermute x4, waiting for transfers between devices, shifted(): return lax.ppermute(values, axis, pairs)  4.81 us
  transfers between devices with their start and end apart: 8, of which 5 were waited for; matrix products, arithmetic and copies ran while one was open for 1% of the time, Pallas kernels for 29%

profile of v3, /device:TPU:0, one launch (start us, length us, event | category | flops | bytes accessed | tf_op | source)
XLA Modules:
  0.0 141.7 jit_solution(11134122308554829388)
XLA Ops:
  0.0 0.8 slice_bitcast_fusion
  0.8 1.3 collective-permute-start.1
  2.1 3.0 %collective-permute-start = (bf16[64,256]{1,0:T(8,128)(2,1)S(1)}, bf16[64,256]{1,0:T(8,128)(2,1)S(1)}, u32[]{:S(2)}, u32[]{:S(2)}) collective-permute-start(bf16[64,256]{1,0:T(8,128)(2,1)S(1)} %get-tuple-element.8), channel_id=1, source_target_pairs={{0,8},{8,16},{16,24},{24,32},{32,40},{40,48},{48,56},{56,64},{64,7... | collective-permute-start | bytes 98312 | tf_op jit(solution)/shard_map/ppermute | solution.py:375
  5.1 1.1 fusion
  6.3 0.0 collective-permute-done.1.refs_1_
  6.3 0.0 copy-start.2
  6.3 0.0 collective-permute-done.refs_0_
  6.3 0.0 copy-start.3
  6.4 3.9 %collective-permute-start.2 = (bf16[66,256]{1,0:T(8,128)(2,1)S(1)}, bf16[66,256]{1,0:T(8,128)(2,1)S(1)}, u32[]{:S(2)}, u32[]{:S(2)}) collective-permute-start(bf16[66,256]{1,0:T(8,128)(2,1)S(1)} %pad_maximum_fusion.1), channel_id=1, source_target_pairs={{0,1},{1,2},{2,3},{3,4},{4,5},{5,6},{6,7},{8,9},{9,10},{10,11},{11... | collective-permute-start | bytes 101384 | tf_op jit(solution)/shard_map/ppermute | solution.py:375
  10.3 1.3 collective-permute-start.3
  11.6 0.3 collective-permute-done.2.refs_2_.refs_0_
  11.9 4.5 %collective-permute-done.3.refs_3_.refs_1_ = bf16[66,256]{1,0:T(8,128)(2,1)S(1)} collective-permute-done((bf16[66,256]{1,0:T(8,128)(2,1)S(1)}, bf16[66,256]{1,0:T(8,128)(2,1)S(1)}, u32[]{:S(2)}, u32[]{:S(2)}) %collective-permute-start.3) | collective-permute-done | bytes 33824 | tf_op jit(solution)/shard_map/ppermute | solution.py:375
  16.4 0.0 copy-done.2
  16.4 0.0 copy-done.3
  16.4 0.6 copy-done.5
  17.0 18.4 %conv_block.2 = bf16[2048,256]{1,0:T(8,128)(2,1)} custom-call(bf16[4096,256]{1,0:T(8,128)(2,1)} %bitcast.27, bf16[4096,256]{1,0:T(8,128)(2,1)} %bitcast.28, bf16[4096,256]{1,0:T(8,128)(2,1)} %bitcast.29, bf16[64,256]{1,0:T(8,128)(2,1)} %copy-done.3, bf16[64,256]{1,0:T(8,128)(2,1)} %copy-done.2, bf16[66,256]{1,0:T(8,128)(2,1)} %copy-done.4, ...), custom_call_target="tpu_custom_call" | custom-call | flops 14336000000 | bytes 6097152 | tf_op jit(solution)/shard_map/conv_block/pallas_call | solution.py:290
  35.5 15.4 %all-to-all-start = ((bf16[64,32,256]{2,1,0:T(8,128)(2,1)}), bf16[64,32,256]{2,1,0:T(8,128)(2,1)S(1)}, u32[]{:S(2)}, u32[]{:S(2)}) async-start(bf16[64,32,256]{2,1,0:T(8,128)(2,1)} %bitcast.24), calls=%async_computation | async-start | bytes 2097152 | tf_op jit(solution)/shard_map/all_to_all | solution.py:417
  50.9 18.3 %conv_block.3 = bf16[2048,256]{1,0:T(8,128)(2,1)} custom-call(bf16[4096,256]{1,0:T(8,128)(2,1)} %bitcast.30, bf16[4096,256]{1,0:T(8,128)(2,1)} %bitcast.31, bf16[4096,256]{1,0:T(8,128)(2,1)} %bitcast.32, bf16[66,256]{1,0:T(8,128)(2,1)} %copy-done.4, bf16[66,256]{1,0:T(8,128)(2,1)} %copy-done.5, f32[1,256]{1,0:T(1,128)} %bitcast.38, f32[1,256]{1,0:T(1,128)} %bitcast.40, ...), custom_call_target="tpu_custom_call" | custom-call | flops 14336000000 | bytes 6097152 | tf_op jit(solution)/shard_map/conv_block/pallas_call | solution.py:290
  69.3 0.0 all-to-all-done.x_ref
  69.3 0.0 copy-start
  69.3 10.4 %all-to-all-start.2 = ((bf16[64,32,256]{2,1,0:T(8,128)(2,1)}), bf16[64,32,256]{2,1,0:T(8,128)(2,1)S(1)}, u32[]{:S(2)}, u32[]{:S(2)}) async-start(bf16[64,32,256]{2,1,0:T(8,128)(2,1)} %bitcast.23), calls=%async_computation.2 | async-start | bytes 2097152 | tf_op jit(solution)/shard_map/all_to_all | solution.py:417
  79.7 0.0 copy-done
  79.7 11.2 %grid_attend.2 = bf16[64,32,256]{2,1,0:T(8,128)(2,1)} custom-call(bf16[64,32,256]{2,1,0:T(8,128)(2,1)} %copy-done, f32[2,256]{1,0:T(2,128)} %gains_ref.3, bf16[256,768]{1,0:T(8,128)(2,1)} %entry_ref.3, bf16[256,256]{1,0:T(8,128)(2,1)} %leave_ref.3, f32[8,64,64]{2,1,0:T(8,128)} %offsets_ref.3, bf16[256,1024]{1,0:T(8,128)(2,1)} %widen_ref.3, ...), custom_call_target="tpu_custom_call" | custom-call | flops 10240000000 | bytes 6097152 | tf_op jit(solution)/shard_map/grid_attend/pallas_call | solution.py:323
  90.9 4.0 %all-to-all-done.2.x_ref = bf16[64,32,256]{2,1,0:T(8,128)(2,1)S(1)} async-done(((bf16[64,32,256]{2,1,0:T(8,128)(2,1)}), bf16[64,32,256]{2,1,0:T(8,128)(2,1)S(1)}, u32[]{:S(2)}, u32[]{:S(2)}) %all-to-all-start.2) | async-done | bytes 1048608 | tf_op jit(solution)/shard_map/all_to_all | solution.py:417
  95.0 6.1 %all-to-all-start.1 = ((bf16[64,32,256]{2,1,0:T(8,128)(2,1)}), bf16[64,32,256]{2,1,0:T(8,128)(2,1)S(1)}, u32[]{:S(2)}, u32[]{:S(2)}) async-start(bf16[64,32,256]{2,1,0:T(8,128)(2,1)} %grid_attend.2), calls=%async_computation.1 | async-start | bytes 2097152 | tf_op jit(solution)/shard_map/all_to_all | solution.py:417
  101.0 0.0 copy-done.1
  101.0 11.2 %grid_attend.3 = bf16[64,32,256]{2,1,0:T(8,128)(2,1)} custom-call(bf16[64,32,256]{2,1,0:T(8,128)(2,1)} %copy-done.1, f32[2,256]{1,0:T(2,128)} %gains_ref.3, bf16[256,768]{1,0:T(8,128)(2,1)} %entry_ref.3, bf16[256,256]{1,0:T(8,128)(2,1)} %leave_ref.3, f32[8,64,64]{2,1,0:T(8,128)} %offsets_ref.3, bf16[256,1024]{1,0:T(8,128)(2,1)} %widen_ref.3, ...), custom_call_target="tpu_custom_call" | custom-call | flops 10240000000 | bytes 6097152 | tf_op jit(solution)/shard_map/grid_attend/pallas_call | solution.py:323
  112.3 5.4 %all-to-all-done.1 = bf16[64,32,256]{2,1,0:T(8,128)(2,1)S(1)} async-done(((bf16[64,32,256]{2,1,0:T(8,128)(2,1)}), bf16[64,32,256]{2,1,0:T(8,128)(2,1)S(1)}, u32[]{:S(2)}, u32[]{:S(2)}) %all-to-all-start.1) | async-done | bytes 1048608 | tf_op jit(solution)/shard_map/all_to_all | solution.py:417
  117.6 5.0 %all-to-all-start.3 = ((bf16[64,32,256]{2,1,0:T(8,128)(2,1)}), bf16[64,32,256]{2,1,0:T(8,128)(2,1)S(1)}, u32[]{:S(2)}, u32[]{:S(2)}) async-start(bf16[64,32,256]{2,1,0:T(8,128)(2,1)} %grid_attend.3), calls=%async_computation.3 | async-start | bytes 2097152 | tf_op jit(solution)/shard_map/all_to_all | solution.py:417
  122.6 0.1 fusion.1
  122.7 17.5 %all-to-all-done.3 = bf16[64,32,256]{2,1,0:T(8,128)(2,1)S(1)} async-done(((bf16[64,32,256]{2,1,0:T(8,128)(2,1)}), bf16[64,32,256]{2,1,0:T(8,128)(2,1)S(1)}, u32[]{:S(2)}, u32[]{:S(2)}) %all-to-all-start.3) | async-done | bytes 1048608 | tf_op jit(solution)/shard_map/all_to_all | solution.py:417
  140.2 1.6 %pad_maximum_fusion = bf16[64,64,256]{2,1,0:T(8,128)(2,1)} fusion(bf16[16,64,256]{2,1,0:T(8,128)(2,1)S(1)} %bitcast.22, bf16[32,64,256]{2,1,0:T(8,128)(2,1)S(1)} %bitcast.20, bf16[16,64,256]{2,1,0:T(8,128)(2,1)S(1)} %bitcast.21), kind=kLoop, calls=%fused_computation | loop fusion | flops 2097152 | bytes 4194304 | tf_op jit(solution)/shard_map/concatenate | solution.py:433
  (10 shorter events, 0.1 us)
Async XLA Ops:
  0.8 5.5 %collective-permute-start.1 = (bf16[64,256]{1,0:T(8,128)(2,1)S(1)}, bf16[64,256]{1,0:T(8,128)(2,1)S(1)}, u32[]{:S(2)}, u32[]{:S(2)}) collective-permute-start(bf16[64,256]{1,0:T(8,128)(2,1)S(1)} %get-tuple-element.7), channel_id=1, source_target_pairs={{8,0},{16,8},{24,16},{32,24},{40,32},{48,40},{56,48},{64,56},{72,6... | collective-permute-start | bytes 98312 | tf_op jit(solution)/shard_map/ppermute | solution.py:375
  2.1 4.3 %collective-permute-start = (bf16[64,256]{1,0:T(8,128)(2,1)S(1)}, bf16[64,256]{1,0:T(8,128)(2,1)S(1)}, u32[]{:S(2)}, u32[]{:S(2)}) collective-permute-start(bf16[64,256]{1,0:T(8,128)(2,1)S(1)} %get-tuple-element.8), channel_id=1, source_target_pairs={{0,8},{8,16},{16,24},{24,32},{32,40},{40,48},{48,56},{56,64},{64,7... | collective-permute-start | bytes 98312 | tf_op jit(solution)/shard_map/ppermute | solution.py:375
  6.3 10.1 %copy-start.2 = (bf16[64,256]{1,0:T(8,128)(2,1)}, bf16[64,256]{1,0:T(8,128)(2,1)S(1)}, u32[]{:S(2)}) copy-start(bf16[64,256]{1,0:T(8,128)(2,1)S(1)} %collective-permute-done.1.refs_1_) | copy-start | bytes 98308
  6.3 10.1 %copy-start.3 = (bf16[64,256]{1,0:T(8,128)(2,1)}, bf16[64,256]{1,0:T(8,128)(2,1)S(1)}, u32[]{:S(2)}) copy-start(bf16[64,256]{1,0:T(8,128)(2,1)S(1)} %collective-permute-done.refs_0_) | copy-start | bytes 98308
  6.4 5.5 %collective-permute-start.2 = (bf16[66,256]{1,0:T(8,128)(2,1)S(1)}, bf16[66,256]{1,0:T(8,128)(2,1)S(1)}, u32[]{:S(2)}, u32[]{:S(2)}) collective-permute-start(bf16[66,256]{1,0:T(8,128)(2,1)S(1)} %pad_maximum_fusion.1), channel_id=1, source_target_pairs={{0,1},{1,2},{2,3},{3,4},{4,5},{5,6},{6,7},{8,9},{9,10},{10,11},{11... | collective-permute-start | bytes 101384 | tf_op jit(solution)/shard_map/ppermute | solution.py:375
  10.3 6.1 %collective-permute-start.3 = (bf16[66,256]{1,0:T(8,128)(2,1)S(1)}, bf16[66,256]{1,0:T(8,128)(2,1)S(1)}, u32[]{:S(2)}, u32[]{:S(2)}) collective-permute-start(bf16[66,256]{1,0:T(8,128)(2,1)S(1)} %pad_maximum_fusion.2), channel_id=1, source_target_pairs={{1,0},{2,1},{3,2},{4,3},{5,4},{6,5},{7,6},{9,8},{10,9},{11,10},{12... | collective-permute-start | bytes 101384 | tf_op jit(solution)/shard_map/ppermute | solution.py:375
  11.9 4.5 %copy-start.4 = (bf16[66,256]{1,0:T(8,128)(2,1)}, bf16[66,256]{1,0:T(8,128)(2,1)S(1)}, u32[]{:S(2)}) copy-start(bf16[66,256]{1,0:T(8,128)(2,1)S(1)} %collective-permute-done.2.refs_2_.refs_0_) | copy-start | bytes 101380
  16.4 0.6 copy-start.5
  35.5 33.8 %all-to-all-start = ((bf16[64,32,256]{2,1,0:T(8,128)(2,1)}), bf16[64,32,256]{2,1,0:T(8,128)(2,1)S(1)}, u32[]{:S(2)}, u32[]{:S(2)}) async-start(bf16[64,32,256]{2,1,0:T(8,128)(2,1)} %bitcast.24), calls=%async_computation | async-start | bytes 2097152 | tf_op jit(solution)/shard_map/all_to_all | solution.py:417
  69.3 10.4 %copy-start = (bf16[64,32,256]{2,1,0:T(8,128)(2,1)}, bf16[64,32,256]{2,1,0:T(8,128)(2,1)S(1)}, u32[]{:S(2)}) copy-start(bf16[64,32,256]{2,1,0:T(8,128)(2,1)S(1)} %all-to-all-done.x_ref) | copy-start | bytes 3145732
  69.3 25.7 %all-to-all-start.2 = ((bf16[64,32,256]{2,1,0:T(8,128)(2,1)}), bf16[64,32,256]{2,1,0:T(8,128)(2,1)S(1)}, u32[]{:S(2)}, u32[]{:S(2)}) async-start(bf16[64,32,256]{2,1,0:T(8,128)(2,1)} %bitcast.23), calls=%async_computation.2 | async-start | bytes 2097152 | tf_op jit(solution)/shard_map/all_to_all | solution.py:417
  95.0 6.1 %copy-start.1 = (bf16[64,32,256]{2,1,0:T(8,128)(2,1)}, bf16[64,32,256]{2,1,0:T(8,128)(2,1)S(1)}, u32[]{:S(2)}) copy-start(bf16[64,32,256]{2,1,0:T(8,128)(2,1)S(1)} %all-to-all-done.2.x_ref) | copy-start | bytes 3145732
  95.0 22.7 %all-to-all-start.1 = ((bf16[64,32,256]{2,1,0:T(8,128)(2,1)}), bf16[64,32,256]{2,1,0:T(8,128)(2,1)S(1)}, u32[]{:S(2)}, u32[]{:S(2)}) async-start(bf16[64,32,256]{2,1,0:T(8,128)(2,1)} %grid_attend.2), calls=%async_computation.1 | async-start | bytes 2097152 | tf_op jit(solution)/shard_map/all_to_all | solution.py:417
  117.6 22.6 %all-to-all-start.3 = ((bf16[64,32,256]{2,1,0:T(8,128)(2,1)}), bf16[64,32,256]{2,1,0:T(8,128)(2,1)S(1)}, u32[]{:S(2)}, u32[]{:S(2)}) async-start(bf16[64,32,256]{2,1,0:T(8,128)(2,1)} %grid_attend.3), calls=%async_computation.3 | async-start | bytes 2097152 | tf_op jit(solution)/shard_map/all_to_all | solution.py:417

commit v4 on v3

--- a/solution.py
+++ b/solution.py
@@ -60,7 +60,7 @@
         offs_scr[:, pair * 128 : (pair + 1) * 128] = two * LOG2E
 
 
-def attend_rows(rows, gains_ref, entry_ref, leave_ref, widen_ref, shrink_ref, offs_scr):
+def attend_rows(rows, gains_ref, entry_ref, leave_ref, offs_scr):
     count, channels = rows.shape
     windows = count // 64
     normed = layer_norm(rows, gains_ref[0:1, :])
@@ -99,7 +99,10 @@
             mixed.append(dot(weight[here], wide).astype(BF16))
         sides.append(jnp.concatenate(mixed, axis=0))
     mixture = jnp.concatenate(sides, axis=-1)
-    attended = (rows + halves_dot(mixture, leave_ref[...])).astype(BF16).astype(F32)
+    return (rows + halves_dot(mixture, leave_ref[...])).astype(BF16).astype(F32)
+
+
+def feed_forward(attended, gains_ref, widen_ref, shrink_ref):
     second = layer_norm(attended, GELU_S * gains_ref[1:2, :])
     inner = widen_ref.shape[1]
     hidden = jnp.concatenate(
@@ -109,7 +112,7 @@
         ],
         axis=-1,
     )
-    return attended + GELU_BACK * halves_dot(hidden, shrink_ref[...])
+    return (attended + GELU_BACK * halves_dot(hidden, shrink_ref[...])).astype(BF16)
 
 
 def conv_block_kernel(edge, x_ref, above_ref, below_ref, *refs):
@@ -130,8 +133,6 @@
         entry_ref,
         leave_ref,
         offsets_ref,
-        widen_ref,
-        shrink_ref,
         out_ref,
         wide_scr,
         side_scr,
@@ -236,15 +237,16 @@
     source = x_ref[...].astype(F32)
     source = source.reshape(2, 8, 8, 8, 256).swapaxes(1, 2).reshape(tokens, 256)
     rows = (source + GELU_BACK * jnp.concatenate(pieces, axis=0)).astype(BF16).astype(F32)
-    done = attend_rows(
-        rows, gains_ref, entry_ref, leave_ref, widen_ref, shrink_ref, offs_scr
-    )
+    done = attend_rows(rows, gains_ref, entry_ref, leave_ref, offs_scr)
     done = done.reshape(2, 8, 8, 8, 256).swapaxes(1, 2).reshape(tokens, 256)
     out_ref[...] = done.astype(BF16)
 
 
 def grid_kernel(
     x_ref,
+    before_gains_ref,
+    before_widen_ref,
+    before_shrink_ref,
     gains_ref,
     entry_ref,
     leave_ref,
@@ -262,20 +264,17 @@
 
     count = x_ref.shape[1]
     tokens = count * 64
-    store_halves(in_scr, slice(0, tokens), x_ref[...].astype(F32).reshape(tokens, 256))
+    came = x_ref[...].astype(F32).reshape(tokens, 256)
+    came = feed_forward(came, before_gains_ref, before_widen_ref, before_shrink_ref)
+    store_halves(in_scr, slice(0, tokens), came.astype(F32))
     rows = jnp.concatenate(
         [load_halves(in_scr, pl.ds(w, 64, stride=count)) for w in range(count)], axis=0
     )
-    done = attend_rows(
-        rows, gains_ref, entry_ref, leave_ref, widen_ref, shrink_ref, offs_scr
-    )
+    attended = attend_rows(rows, gains_ref, entry_ref, leave_ref, offs_scr)
+    done = feed_forward(attended, gains_ref, widen_ref, shrink_ref).astype(F32)
     for w in range(count):
         store_halves(back_scr, pl.ds(w, 64, stride=count), done[w * 64 : (w + 1) * 64])
     out_ref[...] = load_halves(back_scr, slice(0, tokens)).reshape(64, count, 256).astype(BF16)
-
-
-def attend_scratch():
-    return [pltpu.VMEM((64, 512), F32)]
 
 
 def whole(shape):
@@ -395,10 +394,18 @@
         block_entry,
         block_leave,
         block_offsets,
+    )
+    grid_weights = (
+        block_gains,
         block_widen,
         block_shrink,
-    )
-    grid_weights = (grid_gains, grid_entry, grid_leave, grid_offsets, grid_widen, grid_shrink)
+        grid_gains,
+        grid_entry,
+        grid_leave,
+        grid_offsets,
+        grid_widen,
+        grid_shrink,
+    )
     group = row_count // 2 * col_count
     blocks = rows_here // STRIP
     inner = conv_block(

time: 142 us -> 139 us (0.979)
  waiting for transfers between devices: 31.7 us -> 21.1 us
  starting transfers between devices: 46.4 us -> 53.8 us
    all_to_all x4, waiting for transfers between devices: 26.9 us -> 16.3 us  [spread(): lax.all_to_all(values, GROUP, split_axis=0, concat_axis=0, tiled=True)]
    all_to_all x4, starting transfers between devices: 36.9 us -> 44.3 us  [spread(): lax.all_to_all(values, GROUP, split_axis=0, concat_axis=0, tiled=True)]
    pallas_call x2, Pallas kernels: 22.5 us -> 28.7 us  [grid_attend(): pl.pallas_call(grid_kernel, grid=(count // GRID_WINDOWS,), in_specs=[bloc...]
    pallas_call x2, Pallas kernels: 36.8 us -> 30.6 us  [conv_block(): pl.pallas_call(functools.partial(conv_block_kernel, bool(halos)), grid=(s...]
  transfers between devices with their start and end apart: 8 -> 8, of which waited for: 5 -> 6; matrix products, arithmetic and copies ran while one was open for 1% -> 1% of each run, Pallas kernels for 29% -> 32%
where the time goes in v4:
time: 139 us
  Pallas kernels  59.3 us (43%)
  starting transfers between devices  53.8 us (39%)
  waiting for transfers between devices  21.1 us (15%)
  local copies, waits for them, and re-layouts  2.64 us (2%)
  other arithmetic  1.59 us (1%)
    all_to_all x4, starting transfers between devices, spread(): lax.all_to_all(values, GROUP, split_axis=0, concat_axis=0, tiled=True)  44.3 us
    pallas_call x2, Pallas kernels, conv_block(): pl.pallas_call(functools.partial(conv_block_kernel, bool(halos)), grid=(s...  30.6 us
    pallas_call x2, Pallas kernels, grid_attend(): pl.pallas_call(grid_kernel, grid=(count // GRID_WINDOWS,), in_specs=[bloc...  28.7 us
    all_to_all x4, waiting for transfers between devices, spread(): lax.all_to_all(values, GROUP, split_axis=0, concat_axis=0, tiled=True)  16.3 us
    ppermute x4, starting transfers between devices, shifted(): return lax.ppermute(values, axis, pairs)  9.51 us
    ppermute x4, waiting for transfers between devices, shifted(): return lax.ppermute(values, axis, pairs)  4.81 us
  transfers between devices with their start and end apart: 8, of which 6 were waited for; matrix products, arithmetic and copies ran while one was open for 1% of the time, Pallas kernels for 32%

profile of v4, /device:TPU:0, one launch (start us, length us, event | category | flops | bytes accessed | tf_op | source)
XLA Modules:
  0.0 138.6 jit_solution(2765417194234383471)
XLA Ops:
  0.0 0.8 slice_bitcast_fusion
  0.8 1.3 collective-permute-start.1
  2.1 3.0 %collective-permute-start = (bf16[64,256]{1,0:T(8,128)(2,1)S(1)}, bf16[64,256]{1,0:T(8,128)(2,1)S(1)}, u32[]{:S(2)}, u32[]{:S(2)}) collective-permute-start(bf16[64,256]{1,0:T(8,128)(2,1)S(1)} %get-tuple-element.8), channel_id=1, source_target_pairs={{0,8},{8,16},{16,24},{24,32},{32,40},{40,48},{48,56},{56,64},{64,7... | collective-permute-start | bytes 98312 | tf_op jit(solution)/shard_map/ppermute | solution.py:374
  5.1 1.1 fusion
  6.3 0.0 collective-permute-done.1.refs_1_
  6.3 0.0 copy-start.2
  6.3 0.0 collective-permute-done.refs_0_
  6.3 0.0 copy-start.3
  6.4 3.9 %collective-permute-start.2 = (bf16[66,256]{1,0:T(8,128)(2,1)S(1)}, bf16[66,256]{1,0:T(8,128)(2,1)S(1)}, u32[]{:S(2)}, u32[]{:S(2)}) collective-permute-start(bf16[66,256]{1,0:T(8,128)(2,1)S(1)} %pad_maximum_fusion.1), channel_id=1, source_target_pairs={{0,1},{1,2},{2,3},{3,4},{4,5},{5,6},{6,7},{8,9},{9,10},{10,11},{11... | collective-permute-start | bytes 101384 | tf_op jit(solution)/shard_map/ppermute | solution.py:374
  10.3 1.3 collective-permute-start.3
  11.6 0.3 collective-permute-done.2.refs_2_.refs_0_
  11.9 4.5 %collective-permute-done.3.refs_3_.refs_1_ = bf16[66,256]{1,0:T(8,128)(2,1)S(1)} collective-permute-done((bf16[66,256]{1,0:T(8,128)(2,1)S(1)}, bf16[66,256]{1,0:T(8,128)(2,1)S(1)}, u32[]{:S(2)}, u32[]{:S(2)}) %collective-permute-start.3) | collective-permute-done | bytes 33824 | tf_op jit(solution)/shard_map/ppermute | solution.py:374
  16.4 0.0 copy-done.2
  16.4 0.0 copy-done.3
  16.4 0.0 copy-done.4
  16.4 0.6 copy-done.5
  17.0 15.3 %conv_block.2 = bf16[2048,256]{1,0:T(8,128)(2,1)} custom-call(bf16[4096,256]{1,0:T(8,128)(2,1)} %bitcast.27, bf16[4096,256]{1,0:T(8,128)(2,1)} %bitcast.28, bf16[4096,256]{1,0:T(8,128)(2,1)} %bitcast.29, bf16[64,256]{1,0:T(8,128)(2,1)} %copy-done.3, bf16[64,256]{1,0:T(8,128)(2,1)} %copy-done.2, bf16[66,256]{1,0:T(8,128)(2,1)} %copy-done.4, ...), custom_call_target="tpu_custom_call" | custom-call | flops 14336000000 | bytes 6097152 | tf_op jit(solution)/shard_map/conv_block/pallas_call | solution.py:289
  32.4 15.4 %all-to-all-start = ((bf16[64,32,256]{2,1,0:T(8,128)(2,1)}), bf16[64,32,256]{2,1,0:T(8,128)(2,1)S(1)}, u32[]{:S(2)}, u32[]{:S(2)}) async-start(bf16[64,32,256]{2,1,0:T(8,128)(2,1)} %bitcast.24), calls=%async_computation | async-start | bytes 2097152 | tf_op jit(solution)/shard_map/all_to_all | solution.py:424
  47.8 15.3 %conv_block.3 = bf16[2048,256]{1,0:T(8,128)(2,1)} custom-call(bf16[4096,256]{1,0:T(8,128)(2,1)} %bitcast.30, bf16[4096,256]{1,0:T(8,128)(2,1)} %bitcast.31, bf16[4096,256]{1,0:T(8,128)(2,1)} %bitcast.32, bf16[66,256]{1,0:T(8,128)(2,1)} %copy-done.4, bf16[66,256]{1,0:T(8,128)(2,1)} %copy-done.5, f32[1,256]{1,0:T(1,128)} %bitcast.38, f32[1,256]{1,0:T(1,128)} %bitcast.40, ...), custom_call_target="tpu_custom_call" | custom-call | flops 14336000000 | bytes 6097152 | tf_op jit(solution)/shard_map/conv_block/pallas_call | solution.py:289
  63.1 0.6 all-to-all-done.x_ref
  63.7 9.7 %all-to-all-start.2 = ((bf16[64,32,256]{2,1,0:T(8,128)(2,1)}), bf16[64,32,256]{2,1,0:T(8,128)(2,1)S(1)}, u32[]{:S(2)}, u32[]{:S(2)}) async-start(bf16[64,32,256]{2,1,0:T(8,128)(2,1)} %bitcast.23), calls=%async_computation.2 | async-start | bytes 2097152 | tf_op jit(solution)/shard_map/all_to_all | solution.py:424
  73.5 0.0 copy-done
  73.5 14.4 %grid_attend.2 = bf16[64,32,256]{2,1,0:T(8,128)(2,1)} custom-call(bf16[64,32,256]{2,1,0:T(8,128)(2,1)} %copy-done, f32[2,256]{1,0:T(2,128)} %before_gains_ref.3, bf16[256,1024]{1,0:T(8,128)(2,1)} %before_widen_ref.3, bf16[1024,256]{1,0:T(8,128)(2,1)} %before_shrink_ref.3, f32[2,256]{1,0:T(2,128)} %gains_ref.3, bf16[256,768]{1,0:T(8,128)(2,1)} %entry_ref.3, ...), custom_call_target="tpu_custom_call" | custom-call | flops 10240000000 | bytes 6097152 | tf_op jit(solution)/shard_map/grid_attend/pallas_call | solution.py:322
  87.8 0.9 all-to-all-done.2.x_ref
  88.8 9.4 %all-to-all-start.1 = ((bf16[64,32,256]{2,1,0:T(8,128)(2,1)}), bf16[64,32,256]{2,1,0:T(8,128)(2,1)S(1)}, u32[]{:S(2)}, u32[]{:S(2)}) async-start(bf16[64,32,256]{2,1,0:T(8,128)(2,1)} %grid_attend.2), calls=%async_computation.1 | async-start | bytes 2097152 | tf_op jit(solution)/shard_map/all_to_all | solution.py:424
  98.2 0.0 copy-done.1
  98.2 14.3 %grid_attend.3 = bf16[64,32,256]{2,1,0:T(8,128)(2,1)} custom-call(bf16[64,32,256]{2,1,0:T(8,128)(2,1)} %copy-done.1, f32[2,256]{1,0:T(2,128)} %before_gains_ref.3, bf16[256,1024]{1,0:T(8,128)(2,1)} %before_widen_ref.3, bf16[1024,256]{1,0:T(8,128)(2,1)} %before_shrink_ref.3, f32[2,256]{1,0:T(2,128)} %gains_ref.3, bf16[256,768]{1,0:T(8,128)(2,1)} %entry_ref.3, ...), custom_call_target="tpu_custom_call" | custom-call | flops 10240000000 | bytes 6097152 | tf_op jit(solution)/shard_map/grid_attend/pallas_call | solution.py:322
  112.6 0.4 all-to-all-done.1
  112.9 9.7 %all-to-all-start.3 = ((bf16[64,32,256]{2,1,0:T(8,128)(2,1)}), bf16[64,32,256]{2,1,0:T(8,128)(2,1)S(1)}, u32[]{:S(2)}, u32[]{:S(2)}) async-start(bf16[64,32,256]{2,1,0:T(8,128)(2,1)} %grid_attend.3), calls=%async_computation.3 | async-start | bytes 2097152 | tf_op jit(solution)/shard_map/all_to_all | solution.py:424
  122.6 0.1 fusion.1
  122.7 14.4 %all-to-all-done.3 = bf16[64,32,256]{2,1,0:T(8,128)(2,1)S(1)} async-done(((bf16[64,32,256]{2,1,0:T(8,128)(2,1)}), bf16[64,32,256]{2,1,0:T(8,128)(2,1)S(1)}, u32[]{:S(2)}, u32[]{:S(2)}) %all-to-all-start.3) | async-done | bytes 1048608 | tf_op jit(solution)/shard_map/all_to_all | solution.py:424
  137.1 1.6 %pad_maximum_fusion = bf16[64,64,256]{2,1,0:T(8,128)(2,1)} fusion(bf16[16,64,256]{2,1,0:T(8,128)(2,1)S(1)} %bitcast.22, bf16[32,64,256]{2,1,0:T(8,128)(2,1)S(1)} %bitcast.20, bf16[16,64,256]{2,1,0:T(8,128)(2,1)S(1)} %bitcast.21), kind=kLoop, calls=%fused_computation | loop fusion | flops 2097152 | bytes 4194304 | tf_op jit(solution)/shard_map/concatenate | solution.py:440
  (10 shorter events, 0.1 us)
Async XLA Ops:
  0.8 5.5 %collective-permute-start.1 = (bf16[64,256]{1,0:T(8,128)(2,1)S(1)}, bf16[64,256]{1,0:T(8,128)(2,1)S(1)}, u32[]{:S(2)}, u32[]{:S(2)}) collective-permute-start(bf16[64,256]{1,0:T(8,128)(2,1)S(1)} %get-tuple-element.7), channel_id=1, source_target_pairs={{8,0},{16,8},{24,16},{32,24},{40,32},{48,40},{56,48},{64,56},{72,6... | collective-permute-start | bytes 98312 | tf_op jit(solution)/shard_map/ppermute | solution.py:374
  2.1 4.3 %collective-permute-start = (bf16[64,256]{1,0:T(8,128)(2,1)S(1)}, bf16[64,256]{1,0:T(8,128)(2,1)S(1)}, u32[]{:S(2)}, u32[]{:S(2)}) collective-permute-start(bf16[64,256]{1,0:T(8,128)(2,1)S(1)} %get-tuple-element.8), channel_id=1, source_target_pairs={{0,8},{8,16},{16,24},{24,32},{32,40},{40,48},{48,56},{56,64},{64,7... | collective-permute-start | bytes 98312 | tf_op jit(solution)/shard_map/ppermute | solution.py:374
  6.3 10.1 %copy-start.2 = (bf16[64,256]{1,0:T(8,128)(2,1)}, bf16[64,256]{1,0:T(8,128)(2,1)S(1)}, u32[]{:S(2)}) copy-start(bf16[64,256]{1,0:T(8,128)(2,1)S(1)} %collective-permute-done.1.refs_1_) | copy-start | bytes 98308
  6.3 10.1 %copy-start.3 = (bf16[64,256]{1,0:T(8,128)(2,1)}, bf16[64,256]{1,0:T(8,128)(2,1)S(1)}, u32[]{:S(2)}) copy-start(bf16[64,256]{1,0:T(8,128)(2,1)S(1)} %collective-permute-done.refs_0_) | copy-start | bytes 98308
  6.4 5.5 %collective-permute-start.2 = (bf16[66,256]{1,0:T(8,128)(2,1)S(1)}, bf16[66,256]{1,0:T(8,128)(2,1)S(1)}, u32[]{:S(2)}, u32[]{:S(2)}) collective-permute-start(bf16[66,256]{1,0:T(8,128)(2,1)S(1)} %pad_maximum_fusion.1), channel_id=1, source_target_pairs={{0,1},{1,2},{2,3},{3,4},{4,5},{5,6},{6,7},{8,9},{9,10},{10,11},{11... | collective-permute-start | bytes 101384 | tf_op jit(solution)/shard_map/ppermute | solution.py:374
  10.3 6.1 %collective-permute-start.3 = (bf16[66,256]{1,0:T(8,128)(2,1)S(1)}, bf16[66,256]{1,0:T(8,128)(2,1)S(1)}, u32[]{:S(2)}, u32[]{:S(2)}) collective-permute-start(bf16[66,256]{1,0:T(8,128)(2,1)S(1)} %pad_maximum_fusion.2), channel_id=1, source_target_pairs={{1,0},{2,1},{3,2},{4,3},{5,4},{6,5},{7,6},{9,8},{10,9},{11,10},{12... | collective-permute-start | bytes 101384 | tf_op jit(solution)/shard_map/ppermute | solution.py:374
  11.9 4.5 %copy-start.4 = (bf16[66,256]{1,0:T(8,128)(2,1)}, bf16[66,256]{1,0:T(8,128)(2,1)S(1)}, u32[]{:S(2)}) copy-start(bf16[66,256]{1,0:T(8,128)(2,1)S(1)} %collective-permute-done.2.refs_2_.refs_0_) | copy-start | bytes 101380
  16.4 0.6 copy-start.5
  32.4 31.4 %all-to-all-start = ((bf16[64,32,256]{2,1,0:T(8,128)(2,1)}), bf16[64,32,256]{2,1,0:T(8,128)(2,1)S(1)}, u32[]{:S(2)}, u32[]{:S(2)}) async-start(bf16[64,32,256]{2,1,0:T(8,128)(2,1)} %bitcast.24), calls=%async_computation | async-start | bytes 2097152 | tf_op jit(solution)/shard_map/all_to_all | solution.py:424
  63.7 9.8 %copy-start = (bf16[64,32,256]{2,1,0:T(8,128)(2,1)}, bf16[64,32,256]{2,1,0:T(8,128)(2,1)S(1)}, u32[]{:S(2)}) copy-start(bf16[64,32,256]{2,1,0:T(8,128)(2,1)S(1)} %all-to-all-done.x_ref) | copy-start | bytes 3145732
  63.7 25.1 %all-to-all-start.2 = ((bf16[64,32,256]{2,1,0:T(8,128)(2,1)}), bf16[64,32,256]{2,1,0:T(8,128)(2,1)S(1)}, u32[]{:S(2)}, u32[]{:S(2)}) async-start(bf16[64,32,256]{2,1,0:T(8,128)(2,1)} %bitcast.23), calls=%async_computation.2 | async-start | bytes 2097152 | tf_op jit(solution)/shard_map/all_to_all | solution.py:424
  88.8 9.4 %copy-start.1 = (bf16[64,32,256]{2,1,0:T(8,128)(2,1)}, bf16[64,32,256]{2,1,0:T(8,128)(2,1)S(1)}, u32[]{:S(2)}) copy-start(bf16[64,32,256]{2,1,0:T(8,128)(2,1)S(1)} %all-to-all-done.2.x_ref) | copy-start | bytes 3145732
  88.8 24.2 %all-to-all-start.1 = ((bf16[64,32,256]{2,1,0:T(8,128)(2,1)}), bf16[64,32,256]{2,1,0:T(8,128)(2,1)S(1)}, u32[]{:S(2)}, u32[]{:S(2)}) async-start(bf16[64,32,256]{2,1,0:T(8,128)(2,1)} %grid_attend.2), calls=%async_computation.1 | async-start | bytes 2097152 | tf_op jit(solution)/shard_map/all_to_all | solution.py:424
  112.9 24.1 %all-to-all-start.3 = ((bf16[64,32,256]{2,1,0:T(8,128)(2,1)}), bf16[64,32,256]{2,1,0:T(8,128)(2,1)S(1)}, u32[]{:S(2)}, u32[]{:S(2)}) async-start(bf16[64,32,256]{2,1,0:T(8,128)(2,1)} %grid_attend.3), calls=%async_computation.3 | async-start | bytes 2097152 | tf_op jit(solution)/shard_map/all_to_all | solution.py:424

commit v5 on v4

--- a/solution.py
+++ b/solution.py
@@ -115,10 +115,8 @@
     return (attended + GELU_BACK * halves_dot(hidden, shrink_ref[...])).astype(BF16)
 
 
-def conv_block_kernel(edge, x_ref, above_ref, below_ref, *refs):
-    if edge:
-        halo_above_ref, halo_below_ref = refs[:2]
-        refs = refs[2:]
+def conv_block_kernel(second_half, x_ref, above_ref, below_ref, *refs):
+    halo_ref, *refs = refs
     (
         left_ref,
         right_ref,
@@ -149,16 +147,17 @@
         prepare_offsets(offsets_ref, offs_scr)
         for which, ref in enumerate((left_ref, right_ref)):
             side = ref[...].astype(F32)
-            first = 0 if edge else STRIP
-            second = side.shape[0] - STRIP - 2 - first
-            side_scr[which, 0:18, :] = side[first : first + 18]
-            side_scr[which, 24:42, :] = side[second : second + 18]
+            for part in range(2):
+                first = (2 * second_half + part) * STRIP
+                side_scr[which, 24 * part : 24 * part + 18, :] = side[first : first + 18]
 
     above = above_ref[...].astype(F32)
     below = below_ref[...].astype(F32)
-    if edge:
-        above = jnp.where(step == 0, halo_above_ref[...].astype(F32), above)
-        below = jnp.where(step == steps - 1, halo_below_ref[...].astype(F32), below)
+    halo = halo_ref[...].astype(F32)
+    if second_half:
+        below = jnp.where(step == steps - 1, halo, below)
+    else:
+        above = jnp.where(step == 0, halo, above)
 
     ext = STRIP + 2
     store_halves(wide_scr, slice(0, 64), above)
@@ -195,9 +194,10 @@
 
     row, rows_of = lax.axis_index(ROW), lax.axis_size(ROW)
     col, cols_of = lax.axis_index("col"), lax.axis_size("col")
-    if edge:
-        top = keep(sub < 8, jnp.logical_and(step == 0, row == 0))
-        bottom = keep(sub >= 8, jnp.logical_and(step == steps - 1, row == rows_of - 1))
+    if second_half:
+        border = keep(sub >= 8, jnp.logical_and(step == steps - 1, row == rows_of - 1))
+    else:
+        border = keep(sub < 8, jnp.logical_and(step == 0, row == 0))
     at_left = keep(sub % 8 == 0, col == 0)
     at_right = keep(sub % 8 == 7, col == cols_of - 1)
 
@@ -209,10 +209,10 @@
         for slot in range(10):
             one = scaled_gelu(dot(slots[slot], expand_ref[:, here]).astype(BF16) + bias)
             one = one.reshape(10, 16, 256)
-            if edge:
-                one = jnp.concatenate(
-                    [one[:1] * top[None], one[1:9], one[9:] * bottom[None]], axis=0
-                )
+            if second_half:
+                one = jnp.concatenate([one[:9], one[9:] * border[None]], axis=0)
+            else:
+                one = jnp.concatenate([one[:1] * border[None], one[1:]], axis=0)
             if slot == 0:
                 one = one * at_left[None]
             if slot == 9:
@@ -281,21 +281,28 @@
     return pl.BlockSpec(shape, lambda i: (0,) * len(shape))
 
 
-def conv_block(x, body, above, below, halos, left, right, weights):
-    channels = x.shape[1]
-    steps = 2
-    tokens = STRIP * 64
+def conv_block(second_half, x, halo, left, right, weights):
+    tokens, channels = STRIP * 64, x.shape[1]
+    blocks = x.shape[0] // tokens
+    steps = blocks // 2
     row = (64, channels)
+    base = steps * second_half
+
+    def above(i):
+        return jnp.maximum(STRIP * (base + i) - 1, 0)
+
+    def below(i):
+        return jnp.minimum(STRIP * (base + i + 1), STRIP * blocks - 1)
+
     return pl.pallas_call(
-        functools.partial(conv_block_kernel, bool(halos)),
+        functools.partial(conv_block_kernel, second_half),
         grid=(steps,),
         in_specs=[
-            pl.BlockSpec((tokens, channels), lambda i: (body(i), 0)),
+            pl.BlockSpec((tokens, channels), lambda i: (base + i, 0)),
             pl.BlockSpec(row, lambda i: (above(i), 0)),
             pl.BlockSpec(row, lambda i: (below(i), 0)),
         ]
-        + [whole(h.shape) for h in halos]
-        + [whole(left.shape), whole(right.shape)]
+        + [whole(halo.shape), whole(left.shape), whole(right.shape)]
         + [whole(w.shape) for w in weights],
         out_specs=pl.BlockSpec((tokens, channels), lambda i: (i, 0)),
         out_shape=jax.ShapeDtypeStruct((steps * tokens, channels), BF16),
@@ -312,7 +319,7 @@
             transcendentals=0,
         ),
         name="conv_block",
-    )(x, x, x, *halos, left, right, *weights)
+    )(x, x, x, halo, left, right, *weights)
 
 
 def grid_attend(x, weights):
@@ -374,8 +381,13 @@
         return lax.ppermute(values, axis, pairs)
 
     x = radar_tiles.reshape(rows_here * cols_here, channels)
-    above = shifted(x[-cols_here:], ROW, row_count, 1)
-    below = shifted(x[:cols_here], ROW, row_count, -1)
+    even = lax.axis_index("core") == 0
+    top, bottom = x[:cols_here], x[-cols_here:]
+    near = lax.ppermute(jnp.where(even, bottom, top), "core", [(0, 1), (1, 0)])
+    ends = [(r, r + 1) for r in range(1, row_count - 1, 2)]
+    far = lax.ppermute(jnp.where(even, top, bottom), ROW, ends + [(b, a) for a, b in ends])
+    above = jnp.where(even, far, near)
+    below = jnp.where(even, near, far)
     edges = [
         jnp.concatenate([above[e][None], radar_tiles[:, e], below[e][None]], axis=0)
         for e in (-1, 0)
@@ -407,37 +419,18 @@
         grid_shrink,
     )
     group = row_count // 2 * col_count
-    blocks = rows_here // STRIP
-    inner = conv_block(
-        x,
-        lambda i: i + 1,
-        lambda i: STRIP * (i + 1) - 1,
-        lambda i: STRIP * (i + 2),
-        (),
-        left,
-        right,
-        weights,
-    )
-
     def spread(values):
         values = values.reshape(group, -1, channels)
         return lax.all_to_all(values, GROUP, split_axis=0, concat_axis=0, tiled=True)
 
-    inner_there = spread(inner)
-    outer = conv_block(
-        x,
-        lambda i: (blocks - 1) * i,
-        lambda i: (rows_here - STRIP - 1) * i,
-        lambda i: STRIP + (rows_here - STRIP - 1) * i,
-        (above, below),
-        left,
-        right,
-        weights,
-    )
-    outer_there = spread(outer)
-    inner_back = spread(grid_attend(inner_there, grid_weights)).reshape(-1, cols_here, channels)
-    outer_back = spread(grid_attend(outer_there, grid_weights)).reshape(-1, cols_here, channels)
-    return jnp.concatenate([outer_back[:STRIP], inner_back, outer_back[STRIP:]], axis=0)
+    upper_there = spread(conv_block(False, x, above, left, right, weights))
+    lower_there = spread(conv_block(True, x, below, left, right, weights))
+    half = (rows_here // 2, cols_here, channels)
+    upper = spread(grid_attend(upper_there, grid_weights)).reshape(half)
+    lower = spread(grid_attend(lower_there, grid_weights)).reshape(half)
+    result = jnp.pad(upper, ((0, half[0]), (0, 0), (0, 0)))
+    result = lax.optimization_barrier(result)
+    return lax.dynamic_update_slice(result, lower, (half[0], 0, 0))
 
 
 def solution(mesh):

time: 139 us -> 138 us (level)
  starting transfers between devices: 53.8 us -> 45.8 us
  waiting for transfers between devices: 21.1 us -> 27.2 us
  local copies, waits for them, and re-layouts: 2.64 us -> 4.38 us
    all_to_all x4, waiting for transfers between devices: 16.3 us -> 22.6 us  [spread(): lax.all_to_all(values, GROUP, split_axis=0, concat_axis=0, tiled=True)]
    all_to_all x4, starting transfers between devices: 44.3 us -> 39.9 us  [spread(): lax.all_to_all(values, GROUP, split_axis=0, concat_axis=0, tiled=True)]
    ppermute x4 -> x2, starting transfers between devices: 9.51 us -> 5.2 us  [shifted(): return lax.ppermute(values, axis, pairs)]
    concatenate x1 -> x0, other arithmetic: 1.56 us -> none  [shards(): jnp.concatenate([outer_back[:STRIP], inner_back, outer_back[STRIP:]], axi...]
    pad x0 -> x1, local copies, waits for them, and re-layouts: none -> 1.56 us  [shards(): result = jnp.pad(upper, ((0, half[0]), (0, 0), (0, 0)))]
    ppermute x4 -> x2, waiting for transfers between devices: 4.81 us -> 4.55 us  [shifted(): return lax.ppermute(values, axis, pairs)]
  transfers between devices with their start and end apart: 8 -> 8, of which waited for: 6 -> 6; matrix products, arithmetic and copies ran while one was open for 1% -> 2% of each run, Pallas kernels for 32% -> 32%
where the time goes in v5:
time: 138 us
  Pallas kernels  59.3 us (43%)
  starting transfers between devices  45.8 us (33%)
  waiting for transfers between devices  27.2 us (20%)
  local copies, waits for them, and re-layouts  4.38 us (3%)
    all_to_all x4, starting transfers between devices, spread(): lax.all_to_all(values, GROUP, split_axis=0, concat_axis=0, tiled=True)  39.9 us
    pallas_call x2, Pallas kernels, conv_block(): pl.pallas_call(functools.partial(conv_block_kernel, second_half), grid=(s...  30.6 us
    pallas_call x2, Pallas kernels, grid_attend(): pl.pallas_call(grid_kernel, grid=(count // GRID_WINDOWS,), in_specs=[bloc...  28.7 us
    all_to_all x4, waiting for transfers between devices, spread(): lax.all_to_all(values, GROUP, split_axis=0, concat_axis=0, tiled=True)  22.6 us
    ppermute x2, starting transfers between devices, shifted(): return lax.ppermute(values, axis, pairs)  5.2 us
    ppermute x2, waiting for transfers between devices, shifted(): return lax.ppermute(values, axis, pairs)  4.55 us
  transfers between devices with their start and end apart: 8, of which 6 were waited for; matrix products, arithmetic and copies ran while one was open for 2% of the time, Pallas kernels for 32%

profile of v5, /device:TPU:0, one launch (start us, length us, event | category | flops | bytes accessed | tf_op | source)
XLA Modules:
  0.0 137.7 jit_solution(10765303914913097612)
XLA Ops:
  0.0 0.8 select_bitcast_fusion
  0.8 0.1 collective-permute-start.1
  0.9 0.7 collective-permute-start
  1.5 1.1 fusion
  2.7 0.0 collective-permute-done.1
  2.7 0.0 collective-permute-done
  2.8 0.0 copy-start.3
  2.8 0.0 copy-start.2
  2.8 3.9 %collective-permute-start.2 = (bf16[66,256]{1,0:T(8,128)(2,1)S(1)}, bf16[66,256]{1,0:T(8,128)(2,1)S(1)}, u32[]{:S(2)}, u32[]{:S(2)}) collective-permute-start(bf16[66,256]{1,0:T(8,128)(2,1)S(1)} %pad_maximum_fusion), channel_id=1, source_target_pairs={{0,1},{1,2},{2,3},{3,4},{4,5},{5,6},{6,7},{8,9},{9,10},{10,11},{11... | collective-permute-start | bytes 101384 | tf_op jit(solution)/shard_map/ppermute | solution.py:381
  6.8 1.3 collective-permute-start.3
  8.1 0.3 collective-permute-done.2.refs_1_
  8.3 4.3 %collective-permute-done.3.refs_2_ = bf16[66,256]{1,0:T(8,128)(2,1)S(1)} collective-permute-done((bf16[66,256]{1,0:T(8,128)(2,1)S(1)}, bf16[66,256]{1,0:T(8,128)(2,1)S(1)}, u32[]{:S(2)}, u32[]{:S(2)}) %collective-permute-start.3) | collective-permute-done | bytes 33824 | tf_op jit(solution)/shard_map/ppermute | solution.py:381
  12.6 0.0 copy-done.3
  12.6 0.0 copy-done.4
  12.6 0.6 copy-done.5
  13.2 15.3 %conv_block.2 = bf16[2048,256]{1,0:T(8,128)(2,1)} custom-call(bf16[4096,256]{1,0:T(8,128)(2,1)} %bitcast.27, bf16[4096,256]{1,0:T(8,128)(2,1)} %bitcast.28, bf16[4096,256]{1,0:T(8,128)(2,1)} %bitcast.29, bf16[64,256]{1,0:T(8,128)(2,1)} %copy-done.3, bf16[66,256]{1,0:T(8,128)(2,1)} %copy-done.4, bf16[66,256]{1,0:T(8,128)(2,1)} %copy-done.5, ...), custom_call_target="tpu_custom_call" | custom-call | flops 14336000000 | bytes 6097152 | tf_op jit(solution)/shard_map/conv_block/pallas_call | solution.py:297
  28.5 0.0 copy-done.2
  28.5 16.9 %all-to-all-start = ((bf16[64,32,256]{2,1,0:T(8,128)(2,1)}), bf16[64,32,256]{2,1,0:T(8,128)(2,1)S(1)}, u32[]{:S(2)}, u32[]{:S(2)}) async-start(bf16[64,32,256]{2,1,0:T(8,128)(2,1)} %bitcast.24), calls=%async_computation | async-start | bytes 2097152 | tf_op jit(solution)/shard_map/all_to_all | solution.py:424
  45.3 15.3 %conv_block.3 = bf16[2048,256]{1,0:T(8,128)(2,1)} custom-call(bf16[4096,256]{1,0:T(8,128)(2,1)} %bitcast.30, bf16[4096,256]{1,0:T(8,128)(2,1)} %bitcast.31, bf16[4096,256]{1,0:T(8,128)(2,1)} %bitcast.32, bf16[64,256]{1,0:T(8,128)(2,1)} %copy-done.2, bf16[66,256]{1,0:T(8,128)(2,1)} %copy-done.4, bf16[66,256]{1,0:T(8,128)(2,1)} %copy-done.5, ...), custom_call_target="tpu_custom_call" | custom-call | flops 14336000000 | bytes 6097152 | tf_op jit(solution)/shard_map/conv_block/pallas_call | solution.py:297
  60.7 2.6 %all-to-all-done.x_ref = bf16[64,32,256]{2,1,0:T(8,128)(2,1)S(1)} async-done(((bf16[64,32,256]{2,1,0:T(8,128)(2,1)}), bf16[64,32,256]{2,1,0:T(8,128)(2,1)S(1)}, u32[]{:S(2)}, u32[]{:S(2)}) %all-to-all-start) | async-done | bytes 1048608 | tf_op jit(solution)/shard_map/all_to_all | solution.py:424
  63.2 7.8 %all-to-all-start.2 = ((bf16[64,32,256]{2,1,0:T(8,128)(2,1)}), bf16[64,32,256]{2,1,0:T(8,128)(2,1)S(1)}, u32[]{:S(2)}, u32[]{:S(2)}) async-start(bf16[64,32,256]{2,1,0:T(8,128)(2,1)} %bitcast.23), calls=%async_computation.2 | async-start | bytes 2097152 | tf_op jit(solution)/shard_map/all_to_all | solution.py:424
  71.1 0.0 copy-done
  71.1 14.4 %grid_attend.2 = bf16[64,32,256]{2,1,0:T(8,128)(2,1)} custom-call(bf16[64,32,256]{2,1,0:T(8,128)(2,1)} %copy-done, f32[2,256]{1,0:T(2,128)} %before_gains_ref.3, bf16[256,1024]{1,0:T(8,128)(2,1)} %before_widen_ref.3, bf16[1024,256]{1,0:T(8,128)(2,1)} %before_shrink_ref.3, f32[2,256]{1,0:T(2,128)} %gains_ref.3, bf16[256,768]{1,0:T(8,128)(2,1)} %entry_ref.3, ...), custom_call_target="tpu_custom_call" | custom-call | flops 10240000000 | bytes 6097152 | tf_op jit(solution)/shard_map/grid_attend/pallas_call | solution.py:329
  85.4 3.0 %all-to-all-done.2.x_ref = bf16[64,32,256]{2,1,0:T(8,128)(2,1)S(1)} async-done(((bf16[64,32,256]{2,1,0:T(8,128)(2,1)}), bf16[64,32,256]{2,1,0:T(8,128)(2,1)S(1)}, u32[]{:S(2)}, u32[]{:S(2)}) %all-to-all-start.2) | async-done | bytes 1048608 | tf_op jit(solution)/shard_map/all_to_all | solution.py:424
  88.4 7.4 %all-to-all-start.1 = ((bf16[64,32,256]{2,1,0:T(8,128)(2,1)}), bf16[64,32,256]{2,1,0:T(8,128)(2,1)S(1)}, u32[]{:S(2)}, u32[]{:S(2)}) async-start(bf16[64,32,256]{2,1,0:T(8,128)(2,1)} %grid_attend.2), calls=%async_computation.1 | async-start | bytes 2097152 | tf_op jit(solution)/shard_map/all_to_all | solution.py:424
  95.8 0.0 copy-done.1
  95.8 14.4 %grid_attend.3 = bf16[64,32,256]{2,1,0:T(8,128)(2,1)} custom-call(bf16[64,32,256]{2,1,0:T(8,128)(2,1)} %copy-done.1, f32[2,256]{1,0:T(2,128)} %before_gains_ref.3, bf16[256,1024]{1,0:T(8,128)(2,1)} %before_widen_ref.3, bf16[1024,256]{1,0:T(8,128)(2,1)} %before_shrink_ref.3, f32[2,256]{1,0:T(2,128)} %gains_ref.3, bf16[256,768]{1,0:T(8,128)(2,1)} %entry_ref.3, ...), custom_call_target="tpu_custom_call" | custom-call | flops 10240000000 | bytes 6097152 | tf_op jit(solution)/shard_map/grid_attend/pallas_call | solution.py:329
  110.2 2.2 %all-to-all-done.1 = bf16[64,32,256]{2,1,0:T(8,128)(2,1)S(1)} async-done(((bf16[64,32,256]{2,1,0:T(8,128)(2,1)}), bf16[64,32,256]{2,1,0:T(8,128)(2,1)S(1)}, u32[]{:S(2)}, u32[]{:S(2)}) %all-to-all-start.1) | async-done | bytes 1048608 | tf_op jit(solution)/shard_map/all_to_all | solution.py:424
  112.4 7.8 %all-to-all-start.3 = ((bf16[64,32,256]{2,1,0:T(8,128)(2,1)}), bf16[64,32,256]{2,1,0:T(8,128)(2,1)S(1)}, u32[]{:S(2)}, u32[]{:S(2)}) async-start(bf16[64,32,256]{2,1,0:T(8,128)(2,1)} %grid_attend.3), calls=%async_computation.3 | async-start | bytes 2097152 | tf_op jit(solution)/shard_map/all_to_all | solution.py:424
  120.2 1.6 %pad.4 = bf16[64,64,256]{2,1,0:T(8,128)(2,1)} pad(bf16[32,64,256]{2,1,0:T(8,128)(2,1)S(1)} %bitcast.21, bf16[]{:T(256)} %constant.10.clone.1), padding=0_32x0_0x0_0 | pad | bytes 3145730 | tf_op jit(solution)/shard_map/jit(_pad)/pad | solution.py:431
  121.8 14.9 %all-to-all-done.3 = bf16[64,32,256]{2,1,0:T(8,128)(2,1)S(1)} async-done(((bf16[64,32,256]{2,1,0:T(8,128)(2,1)}), bf16[64,32,256]{2,1,0:T(8,128)(2,1)S(1)}, u32[]{:S(2)}, u32[]{:S(2)}) %all-to-all-start.3) | async-done | bytes 1048608 | tf_op jit(solution)/shard_map/all_to_all | solution.py:424
  136.7 1.0 bitcast_dynamic-update-slice_fusion
  (10 shorter events, 0.1 us)
Async XLA Ops:
  0.8 1.9 %collective-permute-start.1 = (bf16[64,256]{1,0:T(8,128)(2,1)S(1)}, bf16[64,256]{1,0:T(8,128)(2,1)S(1)}, u32[]{:S(2)}, u32[]{:S(2)}) collective-permute-start(bf16[64,256]{1,0:T(8,128)(2,1)S(1)} %get-tuple-element.7), channel_id=1, source_target_pairs={{0,8},{8,0},{1,9},{9,1},{2,10},{10,2},{3,11},{11,3},{4,12},{12,4},... | collective-permute-start | bytes 98312 | tf_op jit(solution)/shard_map/ppermute | solution.py:386
  0.9 1.9 %collective-permute-start = (bf16[64,256]{1,0:T(8,128)(2,1)S(1)}, bf16[64,256]{1,0:T(8,128)(2,1)S(1)}, u32[]{:S(2)}, u32[]{:S(2)}) collective-permute-start(bf16[64,256]{1,0:T(8,128)(2,1)S(1)} %get-tuple-element.8), channel_id=1, source_target_pairs={{8,16},{24,32},{40,48},{56,64},{72,80},{88,96},{104,112},{16,8},{3... | collective-permute-start | bytes 98312 | tf_op jit(solution)/shard_map/ppermute | solution.py:388
  2.8 9.9 %copy-start.3 = (bf16[64,256]{1,0:T(8,128)(2,1)}, bf16[64,256]{1,0:T(8,128)(2,1)S(1)}, u32[]{:S(2)}) copy-start(bf16[64,256]{1,0:T(8,128)(2,1)S(1)} %get-tuple-element.10.refs_0_) | copy-start | bytes 98308
  2.8 25.7 %copy-start.2 = (bf16[64,256]{1,0:T(8,128)(2,1)}, bf16[64,256]{1,0:T(8,128)(2,1)S(1)}, u32[]{:S(2)}) copy-start(bf16[64,256]{1,0:T(8,128)(2,1)S(1)} %get-tuple-element.9.refs_0_) | copy-start | bytes 98308
  2.8 5.5 %collective-permute-start.2 = (bf16[66,256]{1,0:T(8,128)(2,1)S(1)}, bf16[66,256]{1,0:T(8,128)(2,1)S(1)}, u32[]{:S(2)}, u32[]{:S(2)}) collective-permute-start(bf16[66,256]{1,0:T(8,128)(2,1)S(1)} %pad_maximum_fusion), channel_id=1, source_target_pairs={{0,1},{1,2},{2,3},{3,4},{4,5},{5,6},{6,7},{8,9},{9,10},{10,11},{11... | collective-permute-start | bytes 101384 | tf_op jit(solution)/shard_map/ppermute | solution.py:381
  6.8 5.9 %collective-permute-start.3 = (bf16[66,256]{1,0:T(8,128)(2,1)S(1)}, bf16[66,256]{1,0:T(8,128)(2,1)S(1)}, u32[]{:S(2)}, u32[]{:S(2)}) collective-permute-start(bf16[66,256]{1,0:T(8,128)(2,1)S(1)} %pad_maximum_fusion.1), channel_id=1, source_target_pairs={{1,0},{2,1},{3,2},{4,3},{5,4},{6,5},{7,6},{9,8},{10,9},{11,10},{12... | collective-permute-start | bytes 101384 | tf_op jit(solution)/shard_map/ppermute | solution.py:381
  8.3 4.3 %copy-start.4 = (bf16[66,256]{1,0:T(8,128)(2,1)}, bf16[66,256]{1,0:T(8,128)(2,1)S(1)}, u32[]{:S(2)}) copy-start(bf16[66,256]{1,0:T(8,128)(2,1)S(1)} %collective-permute-done.2.refs_1_) | copy-start | bytes 101380
  12.6 0.6 copy-start.5
  28.5 34.8 %all-to-all-start = ((bf16[64,32,256]{2,1,0:T(8,128)(2,1)}), bf16[64,32,256]{2,1,0:T(8,128)(2,1)S(1)}, u32[]{:S(2)}, u32[]{:S(2)}) async-start(bf16[64,32,256]{2,1,0:T(8,128)(2,1)} %bitcast.24), calls=%async_computation | async-start | bytes 2097152 | tf_op jit(solution)/shard_map/all_to_all | solution.py:424
  63.2 7.8 %copy-start = (bf16[64,32,256]{2,1,0:T(8,128)(2,1)}, bf16[64,32,256]{2,1,0:T(8,128)(2,1)S(1)}, u32[]{:S(2)}) copy-start(bf16[64,32,256]{2,1,0:T(8,128)(2,1)S(1)} %all-to-all-done.x_ref) | copy-start | bytes 3145732
  63.2 25.1 %all-to-all-start.2 = ((bf16[64,32,256]{2,1,0:T(8,128)(2,1)}), bf16[64,32,256]{2,1,0:T(8,128)(2,1)S(1)}, u32[]{:S(2)}, u32[]{:S(2)}) async-start(bf16[64,32,256]{2,1,0:T(8,128)(2,1)} %bitcast.23), calls=%async_computation.2 | async-start | bytes 2097152 | tf_op jit(solution)/shard_map/all_to_all | solution.py:424
  88.4 7.4 %copy-start.1 = (bf16[64,32,256]{2,1,0:T(8,128)(2,1)}, bf16[64,32,256]{2,1,0:T(8,128)(2,1)S(1)}, u32[]{:S(2)}) copy-start(bf16[64,32,256]{2,1,0:T(8,128)(2,1)S(1)} %all-to-all-done.2.x_ref) | copy-start | bytes 3145732
  88.4 24.0 %all-to-all-start.1 = ((bf16[64,32,256]{2,1,0:T(8,128)(2,1)}), bf16[64,32,256]{2,1,0:T(8,128)(2,1)S(1)}, u32[]{:S(2)}, u32[]{:S(2)}) async-start(bf16[64,32,256]{2,1,0:T(8,128)(2,1)} %grid_attend.2), calls=%async_computation.1 | async-start | bytes 2097152 | tf_op jit(solution)/shard_map/all_to_all | solution.py:424
  112.4 24.3 %all-to-all-start.3 = ((bf16[64,32,256]{2,1,0:T(8,128)(2,1)}), bf16[64,32,256]{2,1,0:T(8,128)(2,1)S(1)}, u32[]{:S(2)}, u32[]{:S(2)}) async-start(bf16[64,32,256]{2,1,0:T(8,128)(2,1)} %grid_attend.3), calls=%async_computation.3 | async-start | bytes 2097152 | tf_op jit(solution)/shard_map/all_to_all | solution.py:424

commit v6 on v5

--- a/solution.py
+++ b/solution.py
@@ -229,11 +229,18 @@
             part = dot(scaled_gelu(total).reshape(128, 256), project_ref[here, :])
             product[low] = part if product[low] is None else product[low] + part
     for low in range(8):
-        store_halves(prod_scr, slice(low * 128, (low + 1) * 128), product[low])
+        for strip in range(16):
+            first = (strip * 8 + low) * 8
+            store_halves(
+                prod_scr, slice(first, first + 8), product[low][strip * 8 : strip * 8 + 8]
+            )
     pieces = []
-    for w in range(16):
-        for y in range(8):
-            pieces.append(load_halves(prod_scr, pl.ds(y * 16 + w, 8, stride=128)))
+    for half in range(2):
+        for w in range(8):
+            for y in range(8):
+                pieces.append(
+                    load_halves(prod_scr, pl.ds((2 * y + half) * 64 + w, 8, stride=8))
+                )
     source = x_ref[...].astype(F32)
     source = source.reshape(2, 8, 8, 8, 256).swapaxes(1, 2).reshape(tokens, 256)
     rows = (source + GELU_BACK * jnp.concatenate(pieces, axis=0)).astype(BF16).astype(F32)

time: 138 us -> 137 us (level)
  no operation moved by 1% of the time
where the time goes in v6:
time: 137 us; the launch traced here: 136 us
  Pallas kernels  58 us (42%)
  starting transfers between devices  45.2 us (33%)
  waiting for transfers between devices  27.9 us (20%)
  local copies, waits for them, and re-layouts  4.38 us (3%)
    all_to_all x4, starting transfers between devices, spread(): lax.all_to_all(values, GROUP, split_axis=0, concat_axis=0, tiled=True)  39.2 us
    pallas_call x2, Pallas kernels, conv_block(): pl.pallas_call(functools.partial(conv_block_kernel, second_half), grid=(s...  29.2 us
    pallas_call x2, Pallas kernels, grid_attend(): pl.pallas_call(grid_kernel, grid=(count // GRID_WINDOWS,), in_specs=[bloc...  28.7 us
    all_to_all x4, waiting for transfers between devices, spread(): lax.all_to_all(values, GROUP, split_axis=0, concat_axis=0, tiled=True)  23.3 us
    ppermute x2, starting transfers between devices, shifted(): return lax.ppermute(values, axis, pairs)  5.2 us
    ppermute x2, waiting for transfers between devices, shifted(): return lax.ppermute(values, axis, pairs)  4.55 us
  transfers between devices with their start and end apart: 8, of which 6 were waited for; matrix products, arithmetic and copies ran while one was open for 2% of the time, Pallas kernels for 32%

profile of v6, /device:TPU:0, one launch (start us, length us, event | category | flops | bytes accessed | tf_op | source)
XLA Modules:
  0.0 136.4 jit_solution(15484841438806325897)
XLA Ops:
  0.0 0.8 select_bitcast_fusion
  0.8 0.1 collective-permute-start.1
  0.9 0.7 collective-permute-start
  1.5 1.1 fusion
  2.7 0.0 collective-permute-done.1
  2.7 0.0 collective-permute-done
  2.8 0.0 copy-start.3
  2.8 0.0 copy-start.2
  2.8 3.9 %collective-permute-start.2 = (bf16[66,256]{1,0:T(8,128)(2,1)S(1)}, bf16[66,256]{1,0:T(8,128)(2,1)S(1)}, u32[]{:S(2)}, u32[]{:S(2)}) collective-permute-start(bf16[66,256]{1,0:T(8,128)(2,1)S(1)} %pad_maximum_fusion), channel_id=1, source_target_pairs={{0,1},{1,2},{2,3},{3,4},{4,5},{5,6},{6,7},{8,9},{9,10},{10,11},{11... | collective-permute-start | bytes 101384 | tf_op jit(solution)/shard_map/ppermute | solution.py:388
  6.8 1.3 collective-permute-start.3
  8.1 0.3 collective-permute-done.2.refs_1_
  8.3 4.3 %collective-permute-done.3.refs_2_ = bf16[66,256]{1,0:T(8,128)(2,1)S(1)} collective-permute-done((bf16[66,256]{1,0:T(8,128)(2,1)S(1)}, bf16[66,256]{1,0:T(8,128)(2,1)S(1)}, u32[]{:S(2)}, u32[]{:S(2)}) %collective-permute-start.3) | collective-permute-done | bytes 33824 | tf_op jit(solution)/shard_map/ppermute | solution.py:388
  12.6 0.0 copy-done.3
  12.6 0.0 copy-done.4
  12.6 0.6 copy-done.5
  13.2 14.6 %conv_block.2 = bf16[2048,256]{1,0:T(8,128)(2,1)} custom-call(bf16[4096,256]{1,0:T(8,128)(2,1)} %bitcast.27, bf16[4096,256]{1,0:T(8,128)(2,1)} %bitcast.28, bf16[4096,256]{1,0:T(8,128)(2,1)} %bitcast.29, bf16[64,256]{1,0:T(8,128)(2,1)} %copy-done.3, bf16[66,256]{1,0:T(8,128)(2,1)} %copy-done.4, bf16[66,256]{1,0:T(8,128)(2,1)} %copy-done.5, ...), custom_call_target="tpu_custom_call" | custom-call | flops 14336000000 | bytes 6097152 | tf_op jit(solution)/shard_map/conv_block/pallas_call | solution.py:304
  27.8 0.0 copy-done.2
  27.8 16.9 %all-to-all-start = ((bf16[64,32,256]{2,1,0:T(8,128)(2,1)}), bf16[64,32,256]{2,1,0:T(8,128)(2,1)S(1)}, u32[]{:S(2)}, u32[]{:S(2)}) async-start(bf16[64,32,256]{2,1,0:T(8,128)(2,1)} %bitcast.24), calls=%async_computation | async-start | bytes 2097152 | tf_op jit(solution)/shard_map/all_to_all | solution.py:431
  44.7 14.7 %conv_block.3 = bf16[2048,256]{1,0:T(8,128)(2,1)} custom-call(bf16[4096,256]{1,0:T(8,128)(2,1)} %bitcast.30, bf16[4096,256]{1,0:T(8,128)(2,1)} %bitcast.31, bf16[4096,256]{1,0:T(8,128)(2,1)} %bitcast.32, bf16[64,256]{1,0:T(8,128)(2,1)} %copy-done.2, bf16[66,256]{1,0:T(8,128)(2,1)} %copy-done.4, bf16[66,256]{1,0:T(8,128)(2,1)} %copy-done.5, ...), custom_call_target="tpu_custom_call" | custom-call | flops 14336000000 | bytes 6097152 | tf_op jit(solution)/shard_map/conv_block/pallas_call | solution.py:304
  59.3 3.2 %all-to-all-done.x_ref = bf16[64,32,256]{2,1,0:T(8,128)(2,1)S(1)} async-done(((bf16[64,32,256]{2,1,0:T(8,128)(2,1)}), bf16[64,32,256]{2,1,0:T(8,128)(2,1)S(1)}, u32[]{:S(2)}, u32[]{:S(2)}) %all-to-all-start) | async-done | bytes 1048608 | tf_op jit(solution)/shard_map/all_to_all | solution.py:431
  62.6 7.1 %all-to-all-start.2 = ((bf16[64,32,256]{2,1,0:T(8,128)(2,1)}), bf16[64,32,256]{2,1,0:T(8,128)(2,1)S(1)}, u32[]{:S(2)}, u32[]{:S(2)}) async-start(bf16[64,32,256]{2,1,0:T(8,128)(2,1)} %bitcast.23), calls=%async_computation.2 | async-start | bytes 2097152 | tf_op jit(solution)/shard_map/all_to_all | solution.py:431
  69.7 0.0 copy-done
  69.7 14.4 %grid_attend.2 = bf16[64,32,256]{2,1,0:T(8,128)(2,1)} custom-call(bf16[64,32,256]{2,1,0:T(8,128)(2,1)} %copy-done, f32[2,256]{1,0:T(2,128)} %before_gains_ref.3, bf16[256,1024]{1,0:T(8,128)(2,1)} %before_widen_ref.3, bf16[1024,256]{1,0:T(8,128)(2,1)} %before_shrink_ref.3, f32[2,256]{1,0:T(2,128)} %gains_ref.3, bf16[256,768]{1,0:T(8,128)(2,1)} %entry_ref.3, ...), custom_call_target="tpu_custom_call" | custom-call | flops 10240000000 | bytes 6097152 | tf_op jit(solution)/shard_map/grid_attend/pallas_call | solution.py:336
  84.1 3.0 %all-to-all-done.2.x_ref = bf16[64,32,256]{2,1,0:T(8,128)(2,1)S(1)} async-done(((bf16[64,32,256]{2,1,0:T(8,128)(2,1)}), bf16[64,32,256]{2,1,0:T(8,128)(2,1)S(1)}, u32[]{:S(2)}, u32[]{:S(2)}) %all-to-all-start.2) | async-done | bytes 1048608 | tf_op jit(solution)/shard_map/all_to_all | solution.py:431
  87.1 7.4 %all-to-all-start.1 = ((bf16[64,32,256]{2,1,0:T(8,128)(2,1)}), bf16[64,32,256]{2,1,0:T(8,128)(2,1)S(1)}, u32[]{:S(2)}, u32[]{:S(2)}) async-start(bf16[64,32,256]{2,1,0:T(8,128)(2,1)} %grid_attend.2), calls=%async_computation.1 | async-start | bytes 2097152 | tf_op jit(solution)/shard_map/all_to_all | solution.py:431
  94.5 0.0 copy-done.1
  94.5 14.4 %grid_attend.3 = bf16[64,32,256]{2,1,0:T(8,128)(2,1)} custom-call(bf16[64,32,256]{2,1,0:T(8,128)(2,1)} %copy-done.1, f32[2,256]{1,0:T(2,128)} %before_gains_ref.3, bf16[256,1024]{1,0:T(8,128)(2,1)} %before_widen_ref.3, bf16[1024,256]{1,0:T(8,128)(2,1)} %before_shrink_ref.3, f32[2,256]{1,0:T(2,128)} %gains_ref.3, bf16[256,768]{1,0:T(8,128)(2,1)} %entry_ref.3, ...), custom_call_target="tpu_custom_call" | custom-call | flops 10240000000 | bytes 6097152 | tf_op jit(solution)/shard_map/grid_attend/pallas_call | solution.py:336
  108.8 2.2 %all-to-all-done.1 = bf16[64,32,256]{2,1,0:T(8,128)(2,1)S(1)} async-done(((bf16[64,32,256]{2,1,0:T(8,128)(2,1)}), bf16[64,32,256]{2,1,0:T(8,128)(2,1)S(1)}, u32[]{:S(2)}, u32[]{:S(2)}) %all-to-all-start.1) | async-done | bytes 1048608 | tf_op jit(solution)/shard_map/all_to_all | solution.py:431
  111.1 7.8 %all-to-all-start.3 = ((bf16[64,32,256]{2,1,0:T(8,128)(2,1)}), bf16[64,32,256]{2,1,0:T(8,128)(2,1)S(1)}, u32[]{:S(2)}, u32[]{:S(2)}) async-start(bf16[64,32,256]{2,1,0:T(8,128)(2,1)} %grid_attend.3), calls=%async_computation.3 | async-start | bytes 2097152 | tf_op jit(solution)/shard_map/all_to_all | solution.py:431
  118.9 1.6 %pad.4 = bf16[64,64,256]{2,1,0:T(8,128)(2,1)} pad(bf16[32,64,256]{2,1,0:T(8,128)(2,1)S(1)} %bitcast.21, bf16[]{:T(256)} %constant.10.clone.1), padding=0_32x0_0x0_0 | pad | bytes 3145730 | tf_op jit(solution)/shard_map/jit(_pad)/pad | solution.py:438
  120.5 14.9 %all-to-all-done.3 = bf16[64,32,256]{2,1,0:T(8,128)(2,1)S(1)} async-done(((bf16[64,32,256]{2,1,0:T(8,128)(2,1)}), bf16[64,32,256]{2,1,0:T(8,128)(2,1)S(1)}, u32[]{:S(2)}, u32[]{:S(2)}) %all-to-all-start.3) | async-done | bytes 1048608 | tf_op jit(solution)/shard_map/all_to_all | solution.py:431
  135.3 1.0 bitcast_dynamic-update-slice_fusion
  (10 shorter events, 0.1 us)
Async XLA Ops:
  0.8 1.9 %collective-permute-start.1 = (bf16[64,256]{1,0:T(8,128)(2,1)S(1)}, bf16[64,256]{1,0:T(8,128)(2,1)S(1)}, u32[]{:S(2)}, u32[]{:S(2)}) collective-permute-start(bf16[64,256]{1,0:T(8,128)(2,1)S(1)} %get-tuple-element.7), channel_id=1, source_target_pairs={{0,8},{8,0},{1,9},{9,1},{2,10},{10,2},{3,11},{11,3},{4,12},{12,4},... | collective-permute-start | bytes 98312 | tf_op jit(solution)/shard_map/ppermute | solution.py:393
  0.9 1.9 %collective-permute-start = (bf16[64,256]{1,0:T(8,128)(2,1)S(1)}, bf16[64,256]{1,0:T(8,128)(2,1)S(1)}, u32[]{:S(2)}, u32[]{:S(2)}) collective-permute-start(bf16[64,256]{1,0:T(8,128)(2,1)S(1)} %get-tuple-element.8), channel_id=1, source_target_pairs={{8,16},{24,32},{40,48},{56,64},{72,80},{88,96},{104,112},{16,8},{3... | collective-permute-start | bytes 98312 | tf_op jit(solution)/shard_map/ppermute | solution.py:395
  2.8 9.9 %copy-start.3 = (bf16[64,256]{1,0:T(8,128)(2,1)}, bf16[64,256]{1,0:T(8,128)(2,1)S(1)}, u32[]{:S(2)}) copy-start(bf16[64,256]{1,0:T(8,128)(2,1)S(1)} %get-tuple-element.10.refs_0_) | copy-start | bytes 98308
  2.8 25.0 %copy-start.2 = (bf16[64,256]{1,0:T(8,128)(2,1)}, bf16[64,256]{1,0:T(8,128)(2,1)S(1)}, u32[]{:S(2)}) copy-start(bf16[64,256]{1,0:T(8,128)(2,1)S(1)} %get-tuple-element.9.refs_0_) | copy-start | bytes 98308
  2.8 5.5 %collective-permute-start.2 = (bf16[66,256]{1,0:T(8,128)(2,1)S(1)}, bf16[66,256]{1,0:T(8,128)(2,1)S(1)}, u32[]{:S(2)}, u32[]{:S(2)}) collective-permute-start(bf16[66,256]{1,0:T(8,128)(2,1)S(1)} %pad_maximum_fusion), channel_id=1, source_target_pairs={{0,1},{1,2},{2,3},{3,4},{4,5},{5,6},{6,7},{8,9},{9,10},{10,11},{11... | collective-permute-start | bytes 101384 | tf_op jit(solution)/shard_map/ppermute | solution.py:388
  6.8 5.9 %collective-permute-start.3 = (bf16[66,256]{1,0:T(8,128)(2,1)S(1)}, bf16[66,256]{1,0:T(8,128)(2,1)S(1)}, u32[]{:S(2)}, u32[]{:S(2)}) collective-permute-start(bf16[66,256]{1,0:T(8,128)(2,1)S(1)} %pad_maximum_fusion.1), channel_id=1, source_target_pairs={{1,0},{2,1},{3,2},{4,3},{5,4},{6,5},{7,6},{9,8},{10,9},{11,10},{12... | collective-permute-start | bytes 101384 | tf_op jit(solution)/shard_map/ppermute | solution.py:388
  8.3 4.3 %copy-start.4 = (bf16[66,256]{1,0:T(8,128)(2,1)}, bf16[66,256]{1,0:T(8,128)(2,1)S(1)}, u32[]{:S(2)}) copy-start(bf16[66,256]{1,0:T(8,128)(2,1)S(1)} %collective-permute-done.2.refs_1_) | copy-start | bytes 101380
  12.6 0.6 copy-start.5
  27.8 34.8 %all-to-all-start = ((bf16[64,32,256]{2,1,0:T(8,128)(2,1)}), bf16[64,32,256]{2,1,0:T(8,128)(2,1)S(1)}, u32[]{:S(2)}, u32[]{:S(2)}) async-start(bf16[64,32,256]{2,1,0:T(8,128)(2,1)} %bitcast.24), calls=%async_computation | async-start | bytes 2097152 | tf_op jit(solution)/shard_map/all_to_all | solution.py:431
  62.6 7.2 %copy-start = (bf16[64,32,256]{2,1,0:T(8,128)(2,1)}, bf16[64,32,256]{2,1,0:T(8,128)(2,1)S(1)}, u32[]{:S(2)}) copy-start(bf16[64,32,256]{2,1,0:T(8,128)(2,1)S(1)} %all-to-all-done.x_ref) | copy-start | bytes 3145732
  62.6 24.5 %all-to-all-start.2 = ((bf16[64,32,256]{2,1,0:T(8,128)(2,1)}), bf16[64,32,256]{2,1,0:T(8,128)(2,1)S(1)}, u32[]{:S(2)}, u32[]{:S(2)}) async-start(bf16[64,32,256]{2,1,0:T(8,128)(2,1)} %bitcast.23), calls=%async_computation.2 | async-start | bytes 2097152 | tf_op jit(solution)/shard_map/all_to_all | solution.py:431
  87.1 7.4 %copy-start.1 = (bf16[64,32,256]{2,1,0:T(8,128)(2,1)}, bf16[64,32,256]{2,1,0:T(8,128)(2,1)S(1)}, u32[]{:S(2)}) copy-start(bf16[64,32,256]{2,1,0:T(8,128)(2,1)S(1)} %all-to-all-done.2.x_ref) | copy-start | bytes 3145732
  87.1 24.0 %all-to-all-start.1 = ((bf16[64,32,256]{2,1,0:T(8,128)(2,1)}), bf16[64,32,256]{2,1,0:T(8,128)(2,1)S(1)}, u32[]{:S(2)}, u32[]{:S(2)}) async-start(bf16[64,32,256]{2,1,0:T(8,128)(2,1)} %grid_attend.2), calls=%async_computation.1 | async-start | bytes 2097152 | tf_op jit(solution)/shard_map/all_to_all | solution.py:431
  111.1 24.3 %all-to-all-start.3 = ((bf16[64,32,256]{2,1,0:T(8,128)(2,1)}), bf16[64,32,256]{2,1,0:T(8,128)(2,1)S(1)}, u32[]{:S(2)}, u32[]{:S(2)}) async-start(bf16[64,32,256]{2,1,0:T(8,128)(2,1)} %grid_attend.3), calls=%async_computation.3 | async-start | bytes 2097152 | tf_op jit(solution)/shard_map/all_to_all | solution.py:431

commit v7 on v6

--- a/solution.py
+++ b/solution.py
@@ -273,15 +273,17 @@
     tokens = count * 64
     came = x_ref[...].astype(F32).reshape(tokens, 256)
     came = feed_forward(came, before_gains_ref, before_widen_ref, before_shrink_ref)
-    store_halves(in_scr, slice(0, tokens), came.astype(F32))
-    rows = jnp.concatenate(
-        [load_halves(in_scr, pl.ds(w, 64, stride=count)) for w in range(count)], axis=0
-    )
+    groups = count // 8
+    came = came.astype(F32).reshape(64, groups, 8, 256).swapaxes(0, 1).reshape(tokens, 256)
+    store_halves(in_scr, slice(0, tokens), came)
+    places = [pl.ds((w // 8) * 512 + w % 8, 64, stride=8) for w in range(count)]
+    rows = jnp.concatenate([load_halves(in_scr, place) for place in places], axis=0)
     attended = attend_rows(rows, gains_ref, entry_ref, leave_ref, offs_scr)
     done = feed_forward(attended, gains_ref, widen_ref, shrink_ref).astype(F32)
-    for w in range(count):
-        store_halves(back_scr, pl.ds(w, 64, stride=count), done[w * 64 : (w + 1) * 64])
-    out_ref[...] = load_halves(back_scr, slice(0, tokens)).reshape(64, count, 256).astype(BF16)
+    for w, place in enumerate(places):
+        store_halves(back_scr, place, done[w * 64 : (w + 1) * 64])
+    done = load_halves(back_scr, slice(0, tokens)).reshape(groups, 64, 8, 256).swapaxes(0, 1)
+    out_ref[...] = done.reshape(64, count, 256).astype(BF16)
 
 
 def whole(shape):

time: 137 us -> 136 us (level)
  transfers between devices with their start and end apart: 8 -> 8, of which waited for: 6 -> 6; matrix products, arithmetic and copies ran while one was open for 2% -> 2% of each run, Pallas kernels for 32% -> 31%
where the time goes in v7:
time: 136 us; the launch traced here: 135 us
  Pallas kernels  56.9 us (42%)
  starting transfers between devices  43.9 us (32%)
  waiting for transfers between devices  29.1 us (21%)
  local copies, waits for them, and re-layouts  4.38 us (3%)
    all_to_all x4, starting transfers between devices, spread(): lax.all_to_all(values, GROUP, split_axis=0, concat_axis=0, tiled=True)  38 us
    pallas_call x2, Pallas kernels, conv_block(): pl.pallas_call(functools.partial(conv_block_kernel, second_half), grid=(s...  29.2 us
    pallas_call x2, Pallas kernels, grid_attend(): pl.pallas_call(grid_kernel, grid=(count // GRID_WINDOWS,), in_specs=[bloc...  27.7 us
    all_to_all x4, waiting for transfers between devices, spread(): lax.all_to_all(values, GROUP, split_axis=0, concat_axis=0, tiled=True)  24.6 us
    ppermute x2, starting transfers between devices, shifted(): return lax.ppermute(values, axis, pairs)  5.2 us
    ppermute x2, waiting for transfers between devices, shifted(): return lax.ppermute(values, axis, pairs)  4.55 us
  transfers between devices with their start and end apart: 8, of which 6 were waited for; matrix products, arithmetic and copies ran while one was open for 2% of the time, Pallas kernels for 31%

profile of v7, /device:TPU:0, one launch (start us, length us, event | category | flops | bytes accessed | tf_op | source)
XLA Modules:
  0.0 135.3 jit_solution(1639270195744551244)
XLA Ops:
  0.0 0.8 select_bitcast_fusion
  0.8 0.1 collective-permute-start.1
  0.9 0.7 collective-permute-start
  1.5 1.1 fusion
  2.7 0.0 collective-permute-done.1
  2.7 0.0 collective-permute-done
  2.8 0.0 copy-start.3
  2.8 0.0 copy-start.2
  2.8 3.9 %collective-permute-start.2 = (bf16[66,256]{1,0:T(8,128)(2,1)S(1)}, bf16[66,256]{1,0:T(8,128)(2,1)S(1)}, u32[]{:S(2)}, u32[]{:S(2)}) collective-permute-start(bf16[66,256]{1,0:T(8,128)(2,1)S(1)} %pad_maximum_fusion), channel_id=1, source_target_pairs={{0,1},{1,2},{2,3},{3,4},{4,5},{5,6},{6,7},{8,9},{9,10},{10,11},{11... | collective-permute-start | bytes 101384 | tf_op jit(solution)/shard_map/ppermute | solution.py:390
  6.8 1.3 collective-permute-start.3
  8.1 0.3 collective-permute-done.2.refs_1_
  8.3 4.3 %collective-permute-done.3.refs_2_ = bf16[66,256]{1,0:T(8,128)(2,1)S(1)} collective-permute-done((bf16[66,256]{1,0:T(8,128)(2,1)S(1)}, bf16[66,256]{1,0:T(8,128)(2,1)S(1)}, u32[]{:S(2)}, u32[]{:S(2)}) %collective-permute-start.3) | collective-permute-done | bytes 33824 | tf_op jit(solution)/shard_map/ppermute | solution.py:390
  12.6 0.0 copy-done.3
  12.6 0.0 copy-done.4
  12.6 0.6 copy-done.5
  13.2 14.6 %conv_block.2 = bf16[2048,256]{1,0:T(8,128)(2,1)} custom-call(bf16[4096,256]{1,0:T(8,128)(2,1)} %bitcast.27, bf16[4096,256]{1,0:T(8,128)(2,1)} %bitcast.28, bf16[4096,256]{1,0:T(8,128)(2,1)} %bitcast.29, bf16[64,256]{1,0:T(8,128)(2,1)} %copy-done.3, bf16[66,256]{1,0:T(8,128)(2,1)} %copy-done.4, bf16[66,256]{1,0:T(8,128)(2,1)} %copy-done.5, ...), custom_call_target="tpu_custom_call" | custom-call | flops 14336000000 | bytes 6097152 | tf_op jit(solution)/shard_map/conv_block/pallas_call | solution.py:306
  27.8 0.0 copy-done.2
  27.8 16.9 %all-to-all-start = ((bf16[64,32,256]{2,1,0:T(8,128)(2,1)}), bf16[64,32,256]{2,1,0:T(8,128)(2,1)S(1)}, u32[]{:S(2)}, u32[]{:S(2)}) async-start(bf16[64,32,256]{2,1,0:T(8,128)(2,1)} %bitcast.24), calls=%async_computation | async-start | bytes 2097152 | tf_op jit(solution)/shard_map/all_to_all | solution.py:433
  44.7 14.7 %conv_block.3 = bf16[2048,256]{1,0:T(8,128)(2,1)} custom-call(bf16[4096,256]{1,0:T(8,128)(2,1)} %bitcast.30, bf16[4096,256]{1,0:T(8,128)(2,1)} %bitcast.31, bf16[4096,256]{1,0:T(8,128)(2,1)} %bitcast.32, bf16[64,256]{1,0:T(8,128)(2,1)} %copy-done.2, bf16[66,256]{1,0:T(8,128)(2,1)} %copy-done.4, bf16[66,256]{1,0:T(8,128)(2,1)} %copy-done.5, ...), custom_call_target="tpu_custom_call" | custom-call | flops 14336000000 | bytes 6097152 | tf_op jit(solution)/shard_map/conv_block/pallas_call | solution.py:306
  59.3 3.2 %all-to-all-done.x_ref = bf16[64,32,256]{2,1,0:T(8,128)(2,1)S(1)} async-done(((bf16[64,32,256]{2,1,0:T(8,128)(2,1)}), bf16[64,32,256]{2,1,0:T(8,128)(2,1)S(1)}, u32[]{:S(2)}, u32[]{:S(2)}) %all-to-all-start) | async-done | bytes 1048608 | tf_op jit(solution)/shard_map/all_to_all | solution.py:433
  62.6 7.1 %all-to-all-start.2 = ((bf16[64,32,256]{2,1,0:T(8,128)(2,1)}), bf16[64,32,256]{2,1,0:T(8,128)(2,1)S(1)}, u32[]{:S(2)}, u32[]{:S(2)}) async-start(bf16[64,32,256]{2,1,0:T(8,128)(2,1)} %bitcast.23), calls=%async_computation.2 | async-start | bytes 2097152 | tf_op jit(solution)/shard_map/all_to_all | solution.py:433
  69.7 0.0 copy-done
  69.7 13.9 %grid_attend.2 = bf16[64,32,256]{2,1,0:T(8,128)(2,1)} custom-call(bf16[64,32,256]{2,1,0:T(8,128)(2,1)} %copy-done, f32[2,256]{1,0:T(2,128)} %before_gains_ref.3, bf16[256,1024]{1,0:T(8,128)(2,1)} %before_widen_ref.3, bf16[1024,256]{1,0:T(8,128)(2,1)} %before_shrink_ref.3, f32[2,256]{1,0:T(2,128)} %gains_ref.3, bf16[256,768]{1,0:T(8,128)(2,1)} %entry_ref.3, ...), custom_call_target="tpu_custom_call" | custom-call | flops 10240000000 | bytes 6097152 | tf_op jit(solution)/shard_map/grid_attend/pallas_call | solution.py:338
  83.6 3.5 %all-to-all-done.2.x_ref = bf16[64,32,256]{2,1,0:T(8,128)(2,1)S(1)} async-done(((bf16[64,32,256]{2,1,0:T(8,128)(2,1)}), bf16[64,32,256]{2,1,0:T(8,128)(2,1)S(1)}, u32[]{:S(2)}, u32[]{:S(2)}) %all-to-all-start.2) | async-done | bytes 1048608 | tf_op jit(solution)/shard_map/all_to_all | solution.py:433
  87.1 6.6 %all-to-all-start.1 = ((bf16[64,32,256]{2,1,0:T(8,128)(2,1)}), bf16[64,32,256]{2,1,0:T(8,128)(2,1)S(1)}, u32[]{:S(2)}, u32[]{:S(2)}) async-start(bf16[64,32,256]{2,1,0:T(8,128)(2,1)} %grid_attend.2), calls=%async_computation.1 | async-start | bytes 2097152 | tf_op jit(solution)/shard_map/all_to_all | solution.py:433
  93.7 0.0 copy-done.1
  93.7 13.8 %grid_attend.3 = bf16[64,32,256]{2,1,0:T(8,128)(2,1)} custom-call(bf16[64,32,256]{2,1,0:T(8,128)(2,1)} %copy-done.1, f32[2,256]{1,0:T(2,128)} %before_gains_ref.3, bf16[256,1024]{1,0:T(8,128)(2,1)} %before_widen_ref.3, bf16[1024,256]{1,0:T(8,128)(2,1)} %before_shrink_ref.3, f32[2,256]{1,0:T(2,128)} %gains_ref.3, bf16[256,768]{1,0:T(8,128)(2,1)} %entry_ref.3, ...), custom_call_target="tpu_custom_call" | custom-call | flops 10240000000 | bytes 6097152 | tf_op jit(solution)/shard_map/grid_attend/pallas_call | solution.py:338
  107.6 3.0 %all-to-all-done.1 = bf16[64,32,256]{2,1,0:T(8,128)(2,1)S(1)} async-done(((bf16[64,32,256]{2,1,0:T(8,128)(2,1)}), bf16[64,32,256]{2,1,0:T(8,128)(2,1)S(1)}, u32[]{:S(2)}, u32[]{:S(2)}) %all-to-all-start.1) | async-done | bytes 1048608 | tf_op jit(solution)/shard_map/all_to_all | solution.py:433
  110.6 7.3 %all-to-all-start.3 = ((bf16[64,32,256]{2,1,0:T(8,128)(2,1)}), bf16[64,32,256]{2,1,0:T(8,128)(2,1)S(1)}, u32[]{:S(2)}, u32[]{:S(2)}) async-start(bf16[64,32,256]{2,1,0:T(8,128)(2,1)} %grid_attend.3), calls=%async_computation.3 | async-start | bytes 2097152 | tf_op jit(solution)/shard_map/all_to_all | solution.py:433
  117.9 1.6 %pad.4 = bf16[64,64,256]{2,1,0:T(8,128)(2,1)} pad(bf16[32,64,256]{2,1,0:T(8,128)(2,1)S(1)} %bitcast.21, bf16[]{:T(256)} %constant.10.clone.1), padding=0_32x0_0x0_0 | pad | bytes 3145730 | tf_op jit(solution)/shard_map/jit(_pad)/pad | solution.py:440
  119.4 14.9 %all-to-all-done.3 = bf16[64,32,256]{2,1,0:T(8,128)(2,1)S(1)} async-done(((bf16[64,32,256]{2,1,0:T(8,128)(2,1)}), bf16[64,32,256]{2,1,0:T(8,128)(2,1)S(1)}, u32[]{:S(2)}, u32[]{:S(2)}) %all-to-all-start.3) | async-done | bytes 1048608 | tf_op jit(solution)/shard_map/all_to_all | solution.py:433
  134.3 1.0 bitcast_dynamic-update-slice_fusion
  (10 shorter events, 0.1 us)
Async XLA Ops:
  0.8 1.9 %collective-permute-start.1 = (bf16[64,256]{1,0:T(8,128)(2,1)S(1)}, bf16[64,256]{1,0:T(8,128)(2,1)S(1)}, u32[]{:S(2)}, u32[]{:S(2)}) collective-permute-start(bf16[64,256]{1,0:T(8,128)(2,1)S(1)} %get-tuple-element.7), channel_id=1, source_target_pairs={{0,8},{8,0},{1,9},{9,1},{2,10},{10,2},{3,11},{11,3},{4,12},{12,4},... | collective-permute-start | bytes 98312 | tf_op jit(solution)/shard_map/ppermute | solution.py:395
  0.9 1.9 %collective-permute-start = (bf16[64,256]{1,0:T(8,128)(2,1)S(1)}, bf16[64,256]{1,0:T(8,128)(2,1)S(1)}, u32[]{:S(2)}, u32[]{:S(2)}) collective-permute-start(bf16[64,256]{1,0:T(8,128)(2,1)S(1)} %get-tuple-element.8), channel_id=1, source_target_pairs={{8,16},{24,32},{40,48},{56,64},{72,80},{88,96},{104,112},{16,8},{3... | collective-permute-start | bytes 98312 | tf_op jit(solution)/shard_map/ppermute | solution.py:397
  2.8 9.9 %copy-start.3 = (bf16[64,256]{1,0:T(8,128)(2,1)}, bf16[64,256]{1,0:T(8,128)(2,1)S(1)}, u32[]{:S(2)}) copy-start(bf16[64,256]{1,0:T(8,128)(2,1)S(1)} %get-tuple-element.10.refs_0_) | copy-start | bytes 98308
  2.8 25.0 %copy-start.2 = (bf16[64,256]{1,0:T(8,128)(2,1)}, bf16[64,256]{1,0:T(8,128)(2,1)S(1)}, u32[]{:S(2)}) copy-start(bf16[64,256]{1,0:T(8,128)(2,1)S(1)} %get-tuple-element.9.refs_0_) | copy-start | bytes 98308
  2.8 5.5 %collective-permute-start.2 = (bf16[66,256]{1,0:T(8,128)(2,1)S(1)}, bf16[66,256]{1,0:T(8,128)(2,1)S(1)}, u32[]{:S(2)}, u32[]{:S(2)}) collective-permute-start(bf16[66,256]{1,0:T(8,128)(2,1)S(1)} %pad_maximum_fusion), channel_id=1, source_target_pairs={{0,1},{1,2},{2,3},{3,4},{4,5},{5,6},{6,7},{8,9},{9,10},{10,11},{11... | collective-permute-start | bytes 101384 | tf_op jit(solution)/shard_map/ppermute | solution.py:390
  6.8 5.9 %collective-permute-start.3 = (bf16[66,256]{1,0:T(8,128)(2,1)S(1)}, bf16[66,256]{1,0:T(8,128)(2,1)S(1)}, u32[]{:S(2)}, u32[]{:S(2)}) collective-permute-start(bf16[66,256]{1,0:T(8,128)(2,1)S(1)} %pad_maximum_fusion.1), channel_id=1, source_target_pairs={{1,0},{2,1},{3,2},{4,3},{5,4},{6,5},{7,6},{9,8},{10,9},{11,10},{12... | collective-permute-start | bytes 101384 | tf_op jit(solution)/shard_map/ppermute | solution.py:390
  8.3 4.3 %copy-start.4 = (bf16[66,256]{1,0:T(8,128)(2,1)}, bf16[66,256]{1,0:T(8,128)(2,1)S(1)}, u32[]{:S(2)}) copy-start(bf16[66,256]{1,0:T(8,128)(2,1)S(1)} %collective-permute-done.2.refs_1_) | copy-start | bytes 101380
  12.6 0.6 copy-start.5
  27.8 34.8 %all-to-all-start = ((bf16[64,32,256]{2,1,0:T(8,128)(2,1)}), bf16[64,32,256]{2,1,0:T(8,128)(2,1)S(1)}, u32[]{:S(2)}, u32[]{:S(2)}) async-start(bf16[64,32,256]{2,1,0:T(8,128)(2,1)} %bitcast.24), calls=%async_computation | async-start | bytes 2097152 | tf_op jit(solution)/shard_map/all_to_all | solution.py:433
  62.6 7.2 %copy-start = (bf16[64,32,256]{2,1,0:T(8,128)(2,1)}, bf16[64,32,256]{2,1,0:T(8,128)(2,1)S(1)}, u32[]{:S(2)}) copy-start(bf16[64,32,256]{2,1,0:T(8,128)(2,1)S(1)} %all-to-all-done.x_ref) | copy-start | bytes 3145732
  62.6 24.5 %all-to-all-start.2 = ((bf16[64,32,256]{2,1,0:T(8,128)(2,1)}), bf16[64,32,256]{2,1,0:T(8,128)(2,1)S(1)}, u32[]{:S(2)}, u32[]{:S(2)}) async-start(bf16[64,32,256]{2,1,0:T(8,128)(2,1)} %bitcast.23), calls=%async_computation.2 | async-start | bytes 2097152 | tf_op jit(solution)/shard_map/all_to_all | solution.py:433
  87.1 6.7 %copy-start.1 = (bf16[64,32,256]{2,1,0:T(8,128)(2,1)}, bf16[64,32,256]{2,1,0:T(8,128)(2,1)S(1)}, u32[]{:S(2)}) copy-start(bf16[64,32,256]{2,1,0:T(8,128)(2,1)S(1)} %all-to-all-done.2.x_ref) | copy-start | bytes 3145732
  87.1 23.5 %all-to-all-start.1 = ((bf16[64,32,256]{2,1,0:T(8,128)(2,1)}), bf16[64,32,256]{2,1,0:T(8,128)(2,1)S(1)}, u32[]{:S(2)}, u32[]{:S(2)}) async-start(bf16[64,32,256]{2,1,0:T(8,128)(2,1)} %grid_attend.2), calls=%async_computation.1 | async-start | bytes 2097152 | tf_op jit(solution)/shard_map/all_to_all | solution.py:433
  110.6 23.7 %all-to-all-start.3 = ((bf16[64,32,256]{2,1,0:T(8,128)(2,1)}), bf16[64,32,256]{2,1,0:T(8,128)(2,1)S(1)}, u32[]{:S(2)}, u32[]{:S(2)}) async-start(bf16[64,32,256]{2,1,0:T(8,128)(2,1)} %grid_attend.3), calls=%async_computation.3 | async-start | bytes 2097152 | tf_op jit(solution)/shard_map/all_to_all | solution.py:433

commit v8 on v7

--- a/solution.py
+++ b/solution.py
@@ -90,8 +90,8 @@
             )
             probs.append(jnp.exp2(score + offs_scr[:, wide_part]))
         prob = jnp.concatenate(probs, axis=0)
-        total = halves_dot(prob.astype(BF16), adder)
-        weight = (prob / total).astype(BF16)
+        prob = prob.astype(BF16)
+        weight = prob / halves_dot(prob, adder).astype(BF16)
         mixed = []
         for w in range(windows):
             here = slice(w * 64, (w + 1) * 64)

time: 136 us -> 136 us (level)
  no operation moved by 1% of the time
where the time goes in v8:
time: 136 us; the launch traced here: 135 us
  Pallas kernels  57 us (42%)
  starting transfers between devices  44 us (32%)
  waiting for transfers between devices  29 us (21%)
  local copies, waits for them, and re-layouts  4.38 us (3%)
    all_to_all x4, starting transfers between devices, spread(): lax.all_to_all(values, GROUP, split_axis=0, concat_axis=0, tiled=True)  38 us
    pallas_call x2, Pallas kernels, conv_block(): pl.pallas_call(functools.partial(conv_block_kernel, second_half), grid=(s...  29.2 us
    pallas_call x2, Pallas kernels, grid_attend(): pl.pallas_call(grid_kernel, grid=(count // GRID_WINDOWS,), in_specs=[bloc...  27.8 us
    all_to_all x4, waiting for transfers between devices, spread(): lax.all_to_all(values, GROUP, split_axis=0, concat_axis=0, tiled=True)  24.5 us
    ppermute x2, starting transfers between devices, shifted(): return lax.ppermute(values, axis, pairs)  5.2 us
    ppermute x2, waiting for transfers between devices, shifted(): return lax.ppermute(values, axis, pairs)  4.55 us
  transfers between devices with their start and end apart: 8, of which 6 were waited for; matrix products, arithmetic and copies ran while one was open for 2% of the time, Pallas kernels for 31%

profile of v8, /device:TPU:0, one launch (start us, length us, event | category | flops | bytes accessed | tf_op | source)
XLA Modules:
  0.0 135.4 jit_solution(2039538782691347974)
XLA Ops:
  0.0 0.8 select_bitcast_fusion
  0.8 0.1 collective-permute-start.1
  0.9 0.7 collective-permute-start
  1.5 1.1 fusion
  2.7 0.0 collective-permute-done.1
  2.7 0.0 collective-permute-done
  2.8 0.0 copy-start.3
  2.8 0.0 copy-start.2
  2.8 3.9 %collective-permute-start.2 = (bf16[66,256]{1,0:T(8,128)(2,1)S(1)}, bf16[66,256]{1,0:T(8,128)(2,1)S(1)}, u32[]{:S(2)}, u32[]{:S(2)}) collective-permute-start(bf16[66,256]{1,0:T(8,128)(2,1)S(1)} %pad_maximum_fusion), channel_id=1, source_target_pairs={{0,1},{1,2},{2,3},{3,4},{4,5},{5,6},{6,7},{8,9},{9,10},{10,11},{11... | collective-permute-start | bytes 101384 | tf_op jit(solution)/shard_map/ppermute | solution.py:390
  6.8 1.3 collective-permute-start.3
  8.1 0.3 collective-permute-done.2.refs_1_
  8.3 4.3 %collective-permute-done.3.refs_2_ = bf16[66,256]{1,0:T(8,128)(2,1)S(1)} collective-permute-done((bf16[66,256]{1,0:T(8,128)(2,1)S(1)}, bf16[66,256]{1,0:T(8,128)(2,1)S(1)}, u32[]{:S(2)}, u32[]{:S(2)}) %collective-permute-start.3) | collective-permute-done | bytes 33824 | tf_op jit(solution)/shard_map/ppermute | solution.py:390
  12.6 0.0 copy-done.3
  12.6 0.0 copy-done.4
  12.6 0.6 copy-done.5
  13.2 14.6 %conv_block.2 = bf16[2048,256]{1,0:T(8,128)(2,1)} custom-call(bf16[4096,256]{1,0:T(8,128)(2,1)} %bitcast.27, bf16[4096,256]{1,0:T(8,128)(2,1)} %bitcast.28, bf16[4096,256]{1,0:T(8,128)(2,1)} %bitcast.29, bf16[64,256]{1,0:T(8,128)(2,1)} %copy-done.3, bf16[66,256]{1,0:T(8,128)(2,1)} %copy-done.4, bf16[66,256]{1,0:T(8,128)(2,1)} %copy-done.5, ...), custom_call_target="tpu_custom_call" | custom-call | flops 14336000000 | bytes 6097152 | tf_op jit(solution)/shard_map/conv_block/pallas_call | solution.py:306
  27.8 0.0 copy-done.2
  27.8 16.9 %all-to-all-start = ((bf16[64,32,256]{2,1,0:T(8,128)(2,1)}), bf16[64,32,256]{2,1,0:T(8,128)(2,1)S(1)}, u32[]{:S(2)}, u32[]{:S(2)}) async-start(bf16[64,32,256]{2,1,0:T(8,128)(2,1)} %bitcast.24), calls=%async_computation | async-start | bytes 2097152 | tf_op jit(solution)/shard_map/all_to_all | solution.py:433
  44.7 14.7 %conv_block.3 = bf16[2048,256]{1,0:T(8,128)(2,1)} custom-call(bf16[4096,256]{1,0:T(8,128)(2,1)} %bitcast.30, bf16[4096,256]{1,0:T(8,128)(2,1)} %bitcast.31, bf16[4096,256]{1,0:T(8,128)(2,1)} %bitcast.32, bf16[64,256]{1,0:T(8,128)(2,1)} %copy-done.2, bf16[66,256]{1,0:T(8,128)(2,1)} %copy-done.4, bf16[66,256]{1,0:T(8,128)(2,1)} %copy-done.5, ...), custom_call_target="tpu_custom_call" | custom-call | flops 14336000000 | bytes 6097152 | tf_op jit(solution)/shard_map/conv_block/pallas_call | solution.py:306
  59.3 3.2 %all-to-all-done.x_ref = bf16[64,32,256]{2,1,0:T(8,128)(2,1)S(1)} async-done(((bf16[64,32,256]{2,1,0:T(8,128)(2,1)}), bf16[64,32,256]{2,1,0:T(8,128)(2,1)S(1)}, u32[]{:S(2)}, u32[]{:S(2)}) %all-to-all-start) | async-done | bytes 1048608 | tf_op jit(solution)/shard_map/all_to_all | solution.py:433
  62.6 7.1 %all-to-all-start.2 = ((bf16[64,32,256]{2,1,0:T(8,128)(2,1)}), bf16[64,32,256]{2,1,0:T(8,128)(2,1)S(1)}, u32[]{:S(2)}, u32[]{:S(2)}) async-start(bf16[64,32,256]{2,1,0:T(8,128)(2,1)} %bitcast.23), calls=%async_computation.2 | async-start | bytes 2097152 | tf_op jit(solution)/shard_map/all_to_all | solution.py:433
  69.7 0.0 copy-done
  69.7 13.9 %grid_attend.2 = bf16[64,32,256]{2,1,0:T(8,128)(2,1)} custom-call(bf16[64,32,256]{2,1,0:T(8,128)(2,1)} %copy-done, f32[2,256]{1,0:T(2,128)} %before_gains_ref.3, bf16[256,1024]{1,0:T(8,128)(2,1)} %before_widen_ref.3, bf16[1024,256]{1,0:T(8,128)(2,1)} %before_shrink_ref.3, f32[2,256]{1,0:T(2,128)} %gains_ref.3, bf16[256,768]{1,0:T(8,128)(2,1)} %entry_ref.3, ...), custom_call_target="tpu_custom_call" | custom-call | flops 10240000000 | bytes 6097152 | tf_op jit(solution)/shard_map/grid_attend/pallas_call | solution.py:338
  83.6 3.4 %all-to-all-done.2.x_ref = bf16[64,32,256]{2,1,0:T(8,128)(2,1)S(1)} async-done(((bf16[64,32,256]{2,1,0:T(8,128)(2,1)}), bf16[64,32,256]{2,1,0:T(8,128)(2,1)S(1)}, u32[]{:S(2)}, u32[]{:S(2)}) %all-to-all-start.2) | async-done | bytes 1048608 | tf_op jit(solution)/shard_map/all_to_all | solution.py:433
  87.0 6.7 %all-to-all-start.1 = ((bf16[64,32,256]{2,1,0:T(8,128)(2,1)}), bf16[64,32,256]{2,1,0:T(8,128)(2,1)S(1)}, u32[]{:S(2)}, u32[]{:S(2)}) async-start(bf16[64,32,256]{2,1,0:T(8,128)(2,1)} %grid_attend.2), calls=%async_computation.1 | async-start | bytes 2097152 | tf_op jit(solution)/shard_map/all_to_all | solution.py:433
  93.7 0.0 copy-done.1
  93.7 13.9 %grid_attend.3 = bf16[64,32,256]{2,1,0:T(8,128)(2,1)} custom-call(bf16[64,32,256]{2,1,0:T(8,128)(2,1)} %copy-done.1, f32[2,256]{1,0:T(2,128)} %before_gains_ref.3, bf16[256,1024]{1,0:T(8,128)(2,1)} %before_widen_ref.3, bf16[1024,256]{1,0:T(8,128)(2,1)} %before_shrink_ref.3, f32[2,256]{1,0:T(2,128)} %gains_ref.3, bf16[256,768]{1,0:T(8,128)(2,1)} %entry_ref.3, ...), custom_call_target="tpu_custom_call" | custom-call | flops 10240000000 | bytes 6097152 | tf_op jit(solution)/shard_map/grid_attend/pallas_call | solution.py:338
  107.6 3.0 %all-to-all-done.1 = bf16[64,32,256]{2,1,0:T(8,128)(2,1)S(1)} async-done(((bf16[64,32,256]{2,1,0:T(8,128)(2,1)}), bf16[64,32,256]{2,1,0:T(8,128)(2,1)S(1)}, u32[]{:S(2)}, u32[]{:S(2)}) %all-to-all-start.1) | async-done | bytes 1048608 | tf_op jit(solution)/shard_map/all_to_all | solution.py:433
  110.6 7.4 %all-to-all-start.3 = ((bf16[64,32,256]{2,1,0:T(8,128)(2,1)}), bf16[64,32,256]{2,1,0:T(8,128)(2,1)S(1)}, u32[]{:S(2)}, u32[]{:S(2)}) async-start(bf16[64,32,256]{2,1,0:T(8,128)(2,1)} %grid_attend.3), calls=%async_computation.3 | async-start | bytes 2097152 | tf_op jit(solution)/shard_map/all_to_all | solution.py:433
  118.0 1.6 %pad.4 = bf16[64,64,256]{2,1,0:T(8,128)(2,1)} pad(bf16[32,64,256]{2,1,0:T(8,128)(2,1)S(1)} %bitcast.21, bf16[]{:T(256)} %constant.10.clone.1), padding=0_32x0_0x0_0 | pad | bytes 3145730 | tf_op jit(solution)/shard_map/jit(_pad)/pad | solution.py:440
  119.5 14.9 %all-to-all-done.3 = bf16[64,32,256]{2,1,0:T(8,128)(2,1)S(1)} async-done(((bf16[64,32,256]{2,1,0:T(8,128)(2,1)}), bf16[64,32,256]{2,1,0:T(8,128)(2,1)S(1)}, u32[]{:S(2)}, u32[]{:S(2)}) %all-to-all-start.3) | async-done | bytes 1048608 | tf_op jit(solution)/shard_map/all_to_all | solution.py:433
  134.4 1.0 bitcast_dynamic-update-slice_fusion
  (10 shorter events, 0.1 us)
Async XLA Ops:
  0.8 1.9 %collective-permute-start.1 = (bf16[64,256]{1,0:T(8,128)(2,1)S(1)}, bf16[64,256]{1,0:T(8,128)(2,1)S(1)}, u32[]{:S(2)}, u32[]{:S(2)}) collective-permute-start(bf16[64,256]{1,0:T(8,128)(2,1)S(1)} %get-tuple-element.7), channel_id=1, source_target_pairs={{0,8},{8,0},{1,9},{9,1},{2,10},{10,2},{3,11},{11,3},{4,12},{12,4},... | collective-permute-start | bytes 98312 | tf_op jit(solution)/shard_map/ppermute | solution.py:395
  0.9 1.9 %collective-permute-start = (bf16[64,256]{1,0:T(8,128)(2,1)S(1)}, bf16[64,256]{1,0:T(8,128)(2,1)S(1)}, u32[]{:S(2)}, u32[]{:S(2)}) collective-permute-start(bf16[64,256]{1,0:T(8,128)(2,1)S(1)} %get-tuple-element.8), channel_id=1, source_target_pairs={{8,16},{24,32},{40,48},{56,64},{72,80},{88,96},{104,112},{16,8},{3... | collective-permute-start | bytes 98312 | tf_op jit(solution)/shard_map/ppermute | solution.py:397
  2.8 9.9 %copy-start.3 = (bf16[64,256]{1,0:T(8,128)(2,1)}, bf16[64,256]{1,0:T(8,128)(2,1)S(1)}, u32[]{:S(2)}) copy-start(bf16[64,256]{1,0:T(8,128)(2,1)S(1)} %get-tuple-element.10.refs_0_) | copy-start | bytes 98308
  2.8 25.0 %copy-start.2 = (bf16[64,256]{1,0:T(8,128)(2,1)}, bf16[64,256]{1,0:T(8,128)(2,1)S(1)}, u32[]{:S(2)}) copy-start(bf16[64,256]{1,0:T(8,128)(2,1)S(1)} %get-tuple-element.9.refs_0_) | copy-start | bytes 98308
  2.8 5.5 %collective-permute-start.2 = (bf16[66,256]{1,0:T(8,128)(2,1)S(1)}, bf16[66,256]{1,0:T(8,128)(2,1)S(1)}, u32[]{:S(2)}, u32[]{:S(2)}) collective-permute-start(bf16[66,256]{1,0:T(8,128)(2,1)S(1)} %pad_maximum_fusion), channel_id=1, source_target_pairs={{0,1},{1,2},{2,3},{3,4},{4,5},{5,6},{6,7},{8,9},{9,10},{10,11},{11... | collective-permute-start | bytes 101384 | tf_op jit(solution)/shard_map/ppermute | solution.py:390
  6.8 5.9 %collective-permute-start.3 = (bf16[66,256]{1,0:T(8,128)(2,1)S(1)}, bf16[66,256]{1,0:T(8,128)(2,1)S(1)}, u32[]{:S(2)}, u32[]{:S(2)}) collective-permute-start(bf16[66,256]{1,0:T(8,128)(2,1)S(1)} %pad_maximum_fusion.1), channel_id=1, source_target_pairs={{1,0},{2,1},{3,2},{4,3},{5,4},{6,5},{7,6},{9,8},{10,9},{11,10},{12... | collective-permute-start | bytes 101384 | tf_op jit(solution)/shard_map/ppermute | solution.py:390
  8.3 4.3 %copy-start.4 = (bf16[66,256]{1,0:T(8,128)(2,1)}, bf16[66,256]{1,0:T(8,128)(2,1)S(1)}, u32[]{:S(2)}) copy-start(bf16[66,256]{1,0:T(8,128)(2,1)S(1)} %collective-permute-done.2.refs_1_) | copy-start | bytes 101380
  12.6 0.6 copy-start.5
  27.8 34.8 %all-to-all-start = ((bf16[64,32,256]{2,1,0:T(8,128)(2,1)}), bf16[64,32,256]{2,1,0:T(8,128)(2,1)S(1)}, u32[]{:S(2)}, u32[]{:S(2)}) async-start(bf16[64,32,256]{2,1,0:T(8,128)(2,1)} %bitcast.24), calls=%async_computation | async-start | bytes 2097152 | tf_op jit(solution)/shard_map/all_to_all | solution.py:433
  62.6 7.1 %copy-start = (bf16[64,32,256]{2,1,0:T(8,128)(2,1)}, bf16[64,32,256]{2,1,0:T(8,128)(2,1)S(1)}, u32[]{:S(2)}) copy-start(bf16[64,32,256]{2,1,0:T(8,128)(2,1)S(1)} %all-to-all-done.x_ref) | copy-start | bytes 3145732
  62.6 24.5 %all-to-all-start.2 = ((bf16[64,32,256]{2,1,0:T(8,128)(2,1)}), bf16[64,32,256]{2,1,0:T(8,128)(2,1)S(1)}, u32[]{:S(2)}, u32[]{:S(2)}) async-start(bf16[64,32,256]{2,1,0:T(8,128)(2,1)} %bitcast.23), calls=%async_computation.2 | async-start | bytes 2097152 | tf_op jit(solution)/shard_map/all_to_all | solution.py:433
  87.0 6.7 %copy-start.1 = (bf16[64,32,256]{2,1,0:T(8,128)(2,1)}, bf16[64,32,256]{2,1,0:T(8,128)(2,1)S(1)}, u32[]{:S(2)}) copy-start(bf16[64,32,256]{2,1,0:T(8,128)(2,1)S(1)} %all-to-all-done.2.x_ref) | copy-start | bytes 3145732
  87.0 23.6 %all-to-all-start.1 = ((bf16[64,32,256]{2,1,0:T(8,128)(2,1)}), bf16[64,32,256]{2,1,0:T(8,128)(2,1)S(1)}, u32[]{:S(2)}, u32[]{:S(2)}) async-start(bf16[64,32,256]{2,1,0:T(8,128)(2,1)} %grid_attend.2), calls=%async_computation.1 | async-start | bytes 2097152 | tf_op jit(solution)/shard_map/all_to_all | solution.py:433
  110.6 23.8 %all-to-all-start.3 = ((bf16[64,32,256]{2,1,0:T(8,128)(2,1)}), bf16[64,32,256]{2,1,0:T(8,128)(2,1)S(1)}, u32[]{:S(2)}, u32[]{:S(2)}) async-start(bf16[64,32,256]{2,1,0:T(8,128)(2,1)} %grid_attend.3), calls=%async_computation.3 | async-start | bytes 2097152 | tf_op jit(solution)/shard_map/all_to_all | solution.py:433
